TPU v7x, 32 devices: a whole 2x2x4 slice. The times are simulated.
32 devices in a mesh: groups: 2 (over x), seq: 8 (over z, y), expert: 2 (over core).
Axes of the slice: x: 2, y: 2, z: 4, core: 2. Of those that a mesh axis runs over, the one named last changes fastest.
Arguments:
- queries: bfloat16 [4, 1024, 2048], P(('groups', 'expert'), 'seq'), parts along dimension 0, may hold values from -6 to 6
- key_rows: bfloat16 [4, 1024, 2048], P(('groups', 'expert'), 'seq'), parts along dimension 0, may hold values from -6 to 6
- value_rows: bfloat16 [4, 1024, 2048], P(('groups', 'expert'), 'seq'), parts along dimension 0, may hold values from -6 to 6
- head_gain: float32 [2048], replicated, may hold values from 0.25 to 1.75
- ffn_gain: float32 [2048], replicated, may hold values from 0.25 to 1.75
- expert_ids: int32 [4, 1024, 8], P(('groups', 'expert'), 'seq'), parts along dimension 0, may hold values from 0 to 15, all different within a row; in each aligned block of 128 rows (0 to 127, 128 to 255, ..., all dimensions but the last counted through in order) at most 96 rows name the same one
- router_weight: float32 [4, 1024, 8], P(('groups', 'expert'), 'seq'), parts along dimension 0, may hold values from 0.05 to 1
- w_gate: bfloat16 [16, 2048, 512], P(('seq', 'expert')), may hold values from -0.125 to 0.125
- w_up: bfloat16 [16, 2048, 512], P(('seq', 'expert')), may hold values from -0.125 to 0.125
- w_down: bfloat16 [16, 512, 2048], P(('seq', 'expert')), may hold values from -0.25 to 0.25
Outputs:
- attention: bfloat16 [4, 1024, 2048], P(('groups', 'expert'), 'seq'), parts along dimension 0
- layer_out: bfloat16 [4, 1024, 2048], P(('groups', 'expert'), 'seq'), parts along dimension 0
There are 2 independent parts, one for each index of `groups`. A program takes and returns all parts, laid end to end along the dimension named above; an argument that names none is the same for every part. Nothing has to cross between parts.
Inputs may be any that keep to these rules, and one draw needn't show every extreme that they name: `expert_ids`: each token names 8 different experts. Among the 128 positions k * 128 to (k + 1) * 128 - 1 of one sequence no expert is named more than 96 times, and in every draw some expert is named exactly 96 times there.
All inputs are finite; a program needn't handle non-finite values.
Results may differ from a plain program's by a relative error of at most 0.0075.
Values may be sent and summed in bfloat16 or wider, within the bound.
No kernel may reach another device: no remote copies, remote signals or barrier semaphores. Data moves between devices by JAX's collectives and lax.ppermute only.
A program may use at most 128 MiB of HBM per device.

v0:
```python
import functools

import jax
import jax.numpy as jnp
from jax import lax
from jax.experimental import pallas as pl
from jax.experimental.pallas import tpu as pltpu
from jax.sharding import PartitionSpec as P


HEAD_DIM = 128
PAD = 16
CHUNKS = 4
PIECES = 2

epsilon = 1e-06
f32 = jnp.float32
bf16 = jnp.bfloat16


VMEM = pl.BlockSpec(memory_space=pltpu.VMEM)
ANY = pl.BlockSpec(memory_space=pl.ANY)
HBM = pl.BlockSpec(memory_space=pltpu.HBM)
SMEM = pl.BlockSpec(memory_space=pltpu.SMEM)
SMALL = pltpu.CompilerParams(vmem_limit_bytes=16 << 20)


def dot(a, b, dims=((1,), (0,))):
    return lax.dot_general(a, b, (dims, ((), ())), preferred_element_type=f32)


def state_kernel(half, at_ref, ids_hbm, rw_hbm, k_hbm, v_hbm, *refs):
    sends, (state_ref, ids_ref, rw_ref, k_ref, v_ref, sems) = refs[:half], refs[half:]
    width = k_ref.shape[1]
    part = width // half
    chunk = width // CHUNKS
    copies = []
    for c in range(CHUNKS):
        cols = slice(c * chunk, (c + 1) * chunk)
        for i, (src, dst) in enumerate(((k_hbm, k_ref), (v_hbm, v_ref))):
            copies.append(pltpu.make_async_copy(src.at[:, cols], dst.at[:, cols], sems.at[2 * c + i]))
    copies.append(pltpu.make_async_copy(ids_hbm, ids_ref, sems.at[2 * CHUNKS]))
    copies.append(pltpu.make_async_copy(rw_hbm, rw_ref, sems.at[2 * CHUNKS + 1]))
    for copy in copies:
        copy.start()
    for c in range(CHUNKS):
        copies[2 * c].wait()
        copies[2 * c + 1].wait()
        for h in range(c * chunk // HEAD_DIM, (c + 1) * chunk // HEAD_DIM):
            cols = slice(h * HEAD_DIM, (h + 1) * HEAD_DIM)
            state_ref[cols, :] = dot(k_ref[:, cols], v_ref[:, cols], ((0,), (0,))).astype(bf16)
    copies[-2].wait()
    copies[-1].wait()
    group, place, core = lax.div(at_ref[0], half), lax.rem(at_ref[0], half), at_ref[1]
    ids = ids_ref[...]
    shares = rw_ref[...] / jnp.sum(rw_ref[...], axis=0, keepdims=True)
    zero = jnp.zeros((PAD - 8, ids.shape[1]), f32)

    def share_of(expert):
        return jnp.sum(jnp.where(ids == expert, shares, 0.0), axis=0, keepdims=True)

    for r, send_ref in enumerate(sends):
        to = lax.rem(place + r, half)
        send_ref[:part, :] = state_ref[pl.ds(pl.multiple_of(to * part, part), part), :]
        rows = []
        for side in (group, 1 - group):
            first = 2 * (side * half + to)
            both = jnp.concatenate([share_of(first + core), share_of(first + 1 - core)], axis=0)
            high = both.astype(bf16).astype(f32)
            rows += [high, both - high]
        send_ref[part:, :] = jnp.concatenate(rows + [zero], axis=0).astype(bf16)


def total_kernel(half, *refs):
    gots, send_ref = refs[:half], refs[half]
    part = gots[0].shape[0] - PAD
    total = gots[0][:part, :].astype(f32)
    for r in range(1, half):
        total = total + gots[r][:part, :].astype(f32)
    send_ref[:part, :] = total.astype(bf16)
    for r in range(half):
        send_ref[part + r * PAD : part + (r + 1) * PAD, :] = gots[r][part:, :]


def prefix_kernel(half, at_ref, after_ref, far_ref, *refs):
    del after_ref
    gots, backs, shares_ref = refs[:half], refs[half:-1], refs[-1]
    part = backs[0].shape[0]
    group, place = lax.div(at_ref[0], half), lax.rem(at_ref[0], half)
    before = jnp.where(group == 1, far_ref[:part, :].astype(f32), 0.0)
    total = before
    for r in range(half):
        total = total + jnp.where(r <= place, gots[r][:part, :].astype(f32), 0.0)
    for r in reversed(range(half)):
        total = jnp.where(r == place, before, total)
        backs[r][...] = total.astype(bf16)
        total = total + gots[r][:part, :].astype(f32)
        source = lax.rem(place + half - r, half)
        terms = gots[r][part:, :].astype(f32)
        shares_ref[group * half + source] = terms[0:8] + terms[2:10]
        terms = far_ref[part + r * PAD : part + (r + 1) * PAD, :].astype(f32)
        shares_ref[(1 - group) * half + source] = terms[4:12] + terms[6:14]


def local_kernel(q_ref, k_ref, v_ref, within_ref):
    rows, width = q_ref.shape
    causal = lax.broadcasted_iota(jnp.int32, (rows, rows), 0) >= lax.broadcasted_iota(
        jnp.int32, (rows, rows), 1
    )
    for h in range(width // HEAD_DIM):
        cols = slice(h * HEAD_DIM, (h + 1) * HEAD_DIM)
        v = v_ref[:, cols]
        scores = jnp.where(causal, dot(q_ref[:, cols], k_ref[:, cols], ((1,), (1,))), 0.0)
        high = scores.astype(bf16)
        low = (scores - high.astype(f32)).astype(bf16)
        within_ref[:, cols] = dot(high, v) + dot(low, v)


def attention_kernel(half, first, at_ref, after_ref, q_ref, within_ref, hg_ref, fg_ref, *refs):
    del after_ref
    carried, (att_ref, normed_ref, p_ref) = refs[:half], refs[half:]
    rows, width = att_ref.shape
    take = slice(first, first + rows)
    part = width // half
    for r in range(half):
        s = lax.rem(lax.rem(at_ref[0], half) + r, half)
        p_ref[pl.ds(pl.multiple_of(s * part, part), part), :] = carried[r][...]
    feature_sq = jnp.zeros((rows, HEAD_DIM), f32)
    for h in range(width // HEAD_DIM):
        cols = slice(h * HEAD_DIM, (h + 1) * HEAD_DIM)
        raw = within_ref[take, cols] + dot(q_ref[take, cols], p_ref[cols, :])
        mean_square = jnp.mean(raw * raw, axis=-1, keepdims=True)
        att = (raw * lax.rsqrt(mean_square + epsilon) * hg_ref[:, cols]).astype(bf16)
        att_ref[:, cols] = att
        att = att.astype(f32)
        feature_sq = feature_sq + att * att
    scale = lax.rsqrt(jnp.sum(feature_sq, axis=-1, keepdims=True) / width + epsilon)
    for h in range(width // HEAD_DIM):
        cols = slice(h * HEAD_DIM, (h + 1) * HEAD_DIM)
        normed_ref[:, cols] = (att_ref[:, cols].astype(f32) * scale * fg_ref[:, cols]).astype(bf16)


def expert_kernel(hop, at_ref, w_ref, g0, u0, d0, g1, u1, d1, *refs):
    n_seq = w_ref.shape[0]
    seq, core = at_ref[0], at_ref[1]
    last = n_seq - 1
    place = jnp.where(seq % 2 == 0, seq // 2, last - seq // 2)
    place = lax.rem(place + jnp.where(core == 0, n_seq - hop, hop), n_seq)
    source = jnp.where(2 * place < n_seq, 2 * place, 2 * (last - place) + 1)
    shares = jnp.transpose(w_ref[source])
    parts = len(refs) // 2
    x = jnp.concatenate([ref[...] for ref in refs[:parts]], axis=0)
    total = None
    for e, (g, u, d) in enumerate(((g0, u0, d0), (g1, u1, d1))):
        gate = dot(x, g[...])
        up = dot(x, u[...])
        hidden = (gate / (1.0 + jnp.exp(-gate)) * up * shares[:, e : e + 1]).astype(bf16)
        part = dot(hidden, d[...])
        total = part if total is None else total + part
    rows = total.shape[0] // parts
    for i, out_ref in enumerate(refs[parts:]):
        out_ref[...] = total[i * rows : (i + 1) * rows].astype(bf16)


def run_experts(hop, at, pieces, shares, weights):
    rows, width = pieces[0].shape
    hidden = weights[0].shape[1]
    count = len(pieces)
    return pl.pallas_call(
        functools.partial(expert_kernel, hop),
        in_specs=[SMEM] + [VMEM] * (7 + count),
        out_specs=[VMEM] * count,
        out_shape=[jax.ShapeDtypeStruct((rows, width), bf16)] * count,
        compiler_params=pltpu.CompilerParams(vmem_limit_bytes=24 << 20),
        cost_estimate=pl.CostEstimate(
            flops=12 * count * rows * width * hidden,
            bytes_accessed=4 * count * rows * width,
            transcendentals=2 * count * rows * hidden,
        ),
        name="experts",
    )(at, shares, *weights, *pieces)


def in_hbm(*arrays):
    return [pltpu.with_memory_space_constraint(a, pltpu.HBM) for a in arrays]


def load_kernel(count, after_ref, *refs):
    del after_ref
    sems = refs[-1]
    copies = [pltpu.make_async_copy(refs[i], refs[count + i], sems.at[i]) for i in range(count)]
    for copy in copies:
        copy.start()
    for copy in copies:
        copy.wait()


def load(after, *arrays):
    arrays = in_hbm(*arrays)
    count = len(arrays)
    size = sum(a.size * a.dtype.itemsize for a in arrays)
    return pl.pallas_call(
        functools.partial(load_kernel, count),
        in_specs=[HBM] * (count + 1),
        out_specs=[VMEM] * count,
        out_shape=[jax.ShapeDtypeStruct(a.shape, a.dtype) for a in arrays],
        scratch_shapes=[pltpu.SemaphoreType.DMA((count,))],
        compiler_params=pltpu.CompilerParams(vmem_limit_bytes=1 << 20),
        cost_estimate=pl.CostEstimate(flops=0, bytes_accessed=size, transcendentals=0),
        name="load",
    )(after, *arrays)


def ring_of(n_seq):
    return list(range(0, n_seq, 2)) + list(range(n_seq - 1, 0, -2)) if n_seq > 1 else [0]


def per_device(
    n_seq,
    queries,
    key_rows,
    value_rows,
    head_gain,
    ffn_gain,
    expert_ids,
    router_weight,
    w_gate,
    w_up,
    w_down,
):
    _, rows, width = queries.shape
    q, k, v = queries[0], key_rows[0], value_rows[0]
    own = (w_gate[0], w_up[0], w_down[0])
    other = tuple(lax.ppermute(w, "expert", [(0, 1), (1, 0)]) for w in own)
    half = n_seq // 2
    at = jnp.stack([lax.axis_index("seq"), lax.axis_index("expert")])

    ring = ring_of(n_seq)
    hops = []
    for i, s in enumerate(ring):
        hops.append((2 * s, 2 * ring[(i + 1) % n_seq]))
        hops.append((2 * s + 1, 2 * ring[i - 1] + 1))

    def hop(value):
        return lax.ppermute(value, ("seq", "expert"), hops)

    def along(blocks, sign):
        def to(s, r):
            return s // half * half + (s + sign * r) % half

        return [blocks[0]] + [
            lax.ppermute(blocks[r], "seq", [(s, to(s, r)) for s in range(n_seq)])
            for r in range(1, half)
        ]

    part = width // half
    sends = pl.pallas_call(
        functools.partial(state_kernel, half),
        in_specs=[SMEM] + [HBM] * 4,
        out_specs=[VMEM] * half,
        scratch_shapes=[
            pltpu.VMEM((width, HEAD_DIM), bf16),
            pltpu.VMEM(expert_ids.shape[:0:-1], jnp.int32),
            pltpu.VMEM(expert_ids.shape[:0:-1], f32),
            pltpu.VMEM((rows, width), bf16),
            pltpu.VMEM((rows, width), bf16),
            pltpu.SemaphoreType.DMA((2 * CHUNKS + 2,)),
        ],
        compiler_params=SMALL,
        out_shape=[jax.ShapeDtypeStruct((part + PAD, HEAD_DIM), bf16)] * half,
        name="states",
    )(at, *in_hbm(expert_ids[0].T, router_weight[0].T, k, v))
    q, k, v, head_gain, ffn_gain = load(
        sends[0], q, k, v, head_gain.reshape(1, width), ffn_gain.reshape(1, width)
    )
    within = pl.pallas_call(
        local_kernel,
        in_specs=[VMEM] * 3,
        out_specs=VMEM,
        out_shape=jax.ShapeDtypeStruct((rows, width), f32),
        compiler_params=SMALL,
        cost_estimate=pl.CostEstimate(
            flops=6 * rows * rows * width, bytes_accessed=10 * rows * width, transcendentals=0
        ),
        name="local",
    )(q, k, v)
    gots = along(sends, 1)
    near = pl.pallas_call(
        functools.partial(total_kernel, half),
        in_specs=[VMEM] * half,
        out_specs=VMEM,
        compiler_params=SMALL,
        out_shape=jax.ShapeDtypeStruct((part + PAD * half, HEAD_DIM), bf16),
        name="total",
    )(*gots)
    far = lax.ppermute(near, "seq", [(s, (s + half) % n_seq) for s in range(n_seq)])
    *backs, shares = pl.pallas_call(
        functools.partial(prefix_kernel, half),
        in_specs=[SMEM, ANY] + [VMEM] * (half + 1),
        out_specs=[VMEM] * (half + 1),
        compiler_params=SMALL,
        out_shape=[jax.ShapeDtypeStruct((part, HEAD_DIM), bf16)] * half
        + [jax.ShapeDtypeStruct((n_seq, 8, rows), f32)],
        name="prefix",
    )(at, within, far, *gots)
    carried = along(backs, -1)
    piece = rows // PIECES
    attention, normed = [], []
    for i in range(PIECES):
        att_piece, normed_piece = pl.pallas_call(
            functools.partial(attention_kernel, half, i * piece),
            in_specs=[SMEM, ANY] + [VMEM] * (half + 4),
            out_specs=[VMEM] * 2,
            scratch_shapes=[pltpu.VMEM((width, HEAD_DIM), bf16)],
            compiler_params=SMALL,
            cost_estimate=pl.CostEstimate(
                flops=2 * piece * width * HEAD_DIM,
                bytes_accessed=2 * width * HEAD_DIM + 10 * piece * width,
                transcendentals=0,
            ),
            out_shape=[jax.ShapeDtypeStruct((piece, width), bf16)] * 2,
            name="attend",
        )(at, normed[-1] if normed else within, q, within, head_gain, ffn_gain, *carried)
        attention.append(att_piece)
        normed.append(normed_piece)
    weights = load(normed[-1], *own, *other)

    held, partial, first = normed, None, None
    for step in range(n_seq):
        following = [hop(x) for x in held] if step < n_seq - 1 else held
        if step == 0:
            following[0], *weights = lax.optimization_barrier((following[0], *weights))
        result = run_experts(step, at, held, shares, weights)
        if step == 0:
            first = result
        elif step == 1:
            partial = result
        else:
            partial = [hop(x) for x in partial]
            partial = [(p.astype(f32) + r.astype(f32)).astype(bf16) for p, r in zip(partial, result)]
        held = following
    partial = [hop(x) for x in partial]
    layer_out = [
        (a.astype(f32) + (p.astype(f32) + r.astype(f32))).astype(bf16)
        for a, p, r in zip(attention, partial, first)
    ]
    return jnp.concatenate(attention)[None], jnp.concatenate(layer_out)[None]


def solution(mesh):
    n_seq = mesh.shape["seq"]

    def body(*args):
        return per_device(n_seq, *args)

    tokens = P(("groups", "expert"), "seq", None)
    experts = P(("seq", "expert"), None, None)
    return jax.shard_map(
        body,
        mesh=mesh,
        in_specs=(tokens, tokens, tokens, P(), P(), tokens, tokens, experts, experts, experts),
        out_specs=(tokens, tokens),
        check_vma=False,
    )
```

profile of v0, /device:TPU:0, one launch (start us, length us, event | category | flops | bytes accessed | tf_op | source)
XLA Modules:
  0.0 168.1 jit_solution(7349772224015759823)
XLA Ops:
  0.7 2.5 %states.1 = (bf16[528,128]{1,0:T(8,128)(2,1)S(1)}, bf16[528,128]{1,0:T(8,128)(2,1)S(1)}, bf16[528,128]{1,0:T(8,128)(2,1)S(1)}, bf16[528,128]{1,0:T(8,128)(2,1)S(1)}) custom-call(s32[2]{0:T(128)S(1)} %pad_add_fusion.at_ref, s32[8,128]{1,0:T(8,128)} %bitcast.33, f32[8,128]{1,0:T(8,128)} %bitcast.34, bf16[128,2048]{1,0:T(8,128)(2,1)} %bitcast.26, ...), custom_call_target="tpu_custom_call" | custom-call | tf_op jit(solution)/shard_map/states/pallas_call | solution.py:257
  3.2 3.0 %collective-permute-start = (bf16[528,128]{1,0:T(8,128)(2,1)S(1)}, bf16[528,128]{1,0:T(8,128)(2,1)S(1)}, u32[]{:S(2)}, u32[]{:S(2)}) collective-permute-start(bf16[528,128]{1,0:T(8,128)(2,1)S(1)} %get-tuple-element.55), channel_id=1, source_target_pairs={{0,2},{2,4},{4,6},{6,0},{8,10},{10,12},{12,14},{14,8},{1,3},{3,5},... | collective-permute-start | bytes 405512 | tf_op jit(solution)/shard_map/ppermute | solution.py:252
  9.8 2.0 %collective-permute-done.refs_1_ = bf16[528,128]{1,0:T(8,128)(2,1)S(1)} collective-permute-done((bf16[528,128]{1,0:T(8,128)(2,1)S(1)}, bf16[528,128]{1,0:T(8,128)(2,1)S(1)}, u32[]{:S(2)}, u32[]{:S(2)}) %collective-permute-start) | collective-permute-done | bytes 135200 | tf_op jit(solution)/shard_map/ppermute | solution.py:252
  13.9 2.8 %collective-permute-start.3 = (bf16[576,128]{1,0:T(8,128)(2,1)S(1)}, bf16[576,128]{1,0:T(8,128)(2,1)S(1)}, u32[]{:S(2)}, u32[]{:S(2)}) collective-permute-start(bf16[576,128]{1,0:T(8,128)(2,1)S(1)} %total.1), channel_id=1, source_target_pairs={{0,8},{2,10},{4,12},{6,14},{8,0},{10,2},{12,4},{14,6},{1,9},{3,11}... | collective-permute-start | bytes 442376 | tf_op jit(solution)/shard_map/ppermute | solution.py:296
  18.9 4.2 %collective-permute-done.3.far_ref = bf16[576,128]{1,0:T(8,128)(2,1)S(1)} collective-permute-done((bf16[576,128]{1,0:T(8,128)(2,1)S(1)}, bf16[576,128]{1,0:T(8,128)(2,1)S(1)}, u32[]{:S(2)}, u32[]{:S(2)}) %collective-permute-start.3) | collective-permute-done | bytes 147488 | tf_op jit(solution)/shard_map/ppermute | solution.py:296
  26.7 2.3 %collective-permute-done.4.refs_1_ = bf16[512,128]{1,0:T(8,128)(2,1)S(1)} collective-permute-done((bf16[512,128]{1,0:T(8,128)(2,1)S(1)}, bf16[512,128]{1,0:T(8,128)(2,1)S(1)}, u32[]{:S(2)}, u32[]{:S(2)}) %collective-permute-start.4) | collective-permute-done | bytes 131104 | tf_op jit(solution)/shard_map/ppermute | solution.py:252
  29.0 3.0 %collective-permute-start.6 = (bf16[512,128]{1,0:T(8,128)(2,1)S(1)}, bf16[512,128]{1,0:T(8,128)(2,1)S(1)}, u32[]{:S(2)}, u32[]{:S(2)}) collective-permute-start(bf16[512,128]{1,0:T(8,128)(2,1)S(1)} %get-tuple-element.61), channel_id=1, source_target_pairs={{0,2},{2,4},{4,6},{6,0},{8,10},{10,12},{12,14},{14,8},{1,3},{3,5},... | collective-permute-start | bytes 393224 | tf_op jit(solution)/shard_map/ppermute | solution.py:252
  31.9 3.4 %collective-permute-done.6.refs_3_ = bf16[512,128]{1,0:T(8,128)(2,1)S(1)} collective-permute-done((bf16[512,128]{1,0:T(8,128)(2,1)S(1)}, bf16[512,128]{1,0:T(8,128)(2,1)S(1)}, u32[]{:S(2)}, u32[]{:S(2)}) %collective-permute-start.6) | collective-permute-done | bytes 131104 | tf_op jit(solution)/shard_map/ppermute | solution.py:252
  38.7 5.4 %collective-permute-done.11.refs_1_ = bf16[64,2048]{1,0:T(8,128)(2,1)S(1)} collective-permute-done((bf16[64,2048]{1,0:T(8,128)(2,1)S(1)}, bf16[64,2048]{1,0:T(8,128)(2,1)S(1)}, u32[]{:S(2)}, u32[]{:S(2)}) %collective-permute-start.11) | collective-permute-done | bytes 262176 | tf_op jit(solution)/shard_map/ppermute | solution.py:245
  45.5 4.9 %collective-permute-done.14.refs_1_ = bf16[64,2048]{1,0:T(8,128)(2,1)S(1)} collective-permute-done((bf16[64,2048]{1,0:T(8,128)(2,1)S(1)}, bf16[64,2048]{1,0:T(8,128)(2,1)S(1)}, u32[]{:S(2)}, u32[]{:S(2)}) %collective-permute-start.14) | collective-permute-done | bytes 262176 | tf_op jit(solution)/shard_map/ppermute | solution.py:245
  51.9 4.9 %collective-permute-done.17.refs_1_ = bf16[64,2048]{1,0:T(8,128)(2,1)S(1)} collective-permute-done((bf16[64,2048]{1,0:T(8,128)(2,1)S(1)}, bf16[64,2048]{1,0:T(8,128)(2,1)S(1)}, u32[]{:S(2)}, u32[]{:S(2)}) %collective-permute-start.17) | collective-permute-done | bytes 262176 | tf_op jit(solution)/shard_map/ppermute | solution.py:245
  58.3 4.9 %collective-permute-done.20.refs_1_ = bf16[64,2048]{1,0:T(8,128)(2,1)S(1)} collective-permute-done((bf16[64,2048]{1,0:T(8,128)(2,1)S(1)}, bf16[64,2048]{1,0:T(8,128)(2,1)S(1)}, u32[]{:S(2)}, u32[]{:S(2)}) %collective-permute-start.20) | collective-permute-done | bytes 262176 | tf_op jit(solution)/shard_map/ppermute | solution.py:245
  64.6 4.9 %collective-permute-done.23.refs_1_ = bf16[64,2048]{1,0:T(8,128)(2,1)S(1)} collective-permute-done((bf16[64,2048]{1,0:T(8,128)(2,1)S(1)}, bf16[64,2048]{1,0:T(8,128)(2,1)S(1)}, u32[]{:S(2)}, u32[]{:S(2)}) %collective-permute-start.23) | collective-permute-done | bytes 262176 | tf_op jit(solution)/shard_map/ppermute | solution.py:245
  71.0 2.5 %collective-permute-start.7 = (bf16[64,2048]{1,0:T(8,128)(2,1)S(1)}, bf16[64,2048]{1,0:T(8,128)(2,1)S(1)}, u32[]{:S(2)}, u32[]{:S(2)}) collective-permute-start(bf16[64,2048]{1,0:T(8,128)(2,1)S(1)} %get-tuple-element.63.after_ref.refs_0_), channel_id=1, source_target_pairs={{0,4},{1,3},{4,8},{5,1},{8,12},{9,5},{12,14},{13,9},{14,10},{15,13... | collective-permute-start | bytes 786440 | tf_op jit(solution)/shard_map/ppermute | solution.py:245
  80.7 4.7 %load.3 = (bf16[2048,512]{1,0:T(8,128)(2,1)S(1)}, bf16[2048,512]{1,0:T(8,128)(2,1)S(1)}, bf16[512,2048]{1,0:T(8,128)(2,1)S(1)}, bf16[2048,512]{1,0:T(8,128)(2,1)...) custom-call(bf16[64,2048]{1,0:T(8,128)(2,1)S(1)} %get-tuple-element.66.after_ref.refs_1_, ...), custom_call_target="tpu_custom_call" | custom-call | bytes 12582912 | tf_op jit(solution)/shard_map/load/pallas_call | solution.py:202
  85.5 2.5 %collective-permute-start.13 = (bf16[64,2048]{1,0:T(8,128)(2,1)S(1)}, bf16[64,2048]{1,0:T(8,128)(2,1)S(1)}, u32[]{:S(2)}, u32[]{:S(2)}) collective-permute-start(bf16[64,2048]{1,0:T(8,128)(2,1)S(1)} %collective-permute-done.7.refs_0_), channel_id=1, source_target_pairs={{0,4},{1,3},{4,8},{5,1},{8,12},{9,5},{12,14},{13,9},{14,10},{15,13... | collective-permute-start | bytes 786440 | tf_op jit(solution)/shard_map/ppermute | solution.py:245
  88.0 2.6 %experts.8 = (bf16[64,2048]{1,0:T(8,128)(2,1)S(1)}, bf16[64,2048]{1,0:T(8,128)(2,1)S(1)}) custom-call(s32[2]{0:T(128)S(1)} %pad_add_fusion.at_ref, f32[8,8,128]{2,1,0:T(8,128)S(1)} %get-tuple-element.65.w_ref, bf16[2048,512]{1,0:T(8,128)(2,1)S(1)} %get-tuple-element.73.g0, bf16[2048,512]{1,0:T(8,128)(2,1)S(1)} %get-tuple-element.74.u0, ...), custom_call_target="tpu_custom_call" | custom-call | flops 1610612736 | bytes 1048576 | tf_op jit(solution)/shard_map/experts/pallas_call | solution.py:169
  91.2 2.0 %collective-permute-start.31 = (bf16[64,2048]{1,0:T(8,128)(2,1)S(1)}, bf16[64,2048]{1,0:T(8,128)(2,1)S(1)}, u32[]{:S(2)}, u32[]{:S(2)}) collective-permute-start(bf16[64,2048]{1,0:T(8,128)(2,1)S(1)} %get-tuple-element.88), channel_id=1, source_target_pairs={{0,4},{1,3},{4,8},{5,1},{8,12},{9,5},{12,14},{13,9},{14,10},{15,13... | collective-permute-start | bytes 786440 | tf_op jit(solution)/shard_map/ppermute | solution.py:245
  93.2 2.6 %experts.15 = (bf16[64,2048]{1,0:T(8,128)(2,1)S(1)}, bf16[64,2048]{1,0:T(8,128)(2,1)S(1)}) custom-call(s32[2]{0:T(128)S(1)} %pad_add_fusion.at_ref, f32[8,8,128]{2,1,0:T(8,128)S(1)} %get-tuple-element.65.w_ref, bf16[2048,512]{1,0:T(8,128)(2,1)S(1)} %get-tuple-element.73.g0, bf16[2048,512]{1,0:T(8,128)(2,1)S(1)} %get-tuple-element.74.u0, ...), custom_call_target="tpu_custom_call" | custom-call | flops 1610612736 | bytes 1048576 | tf_op jit(solution)/shard_map/experts/pallas_call | solution.py:169
  95.8 2.6 %experts.9 = (bf16[64,2048]{1,0:T(8,128)(2,1)S(1)}, bf16[64,2048]{1,0:T(8,128)(2,1)S(1)}) custom-call(s32[2]{0:T(128)S(1)} %pad_add_fusion.at_ref, f32[8,8,128]{2,1,0:T(8,128)S(1)} %get-tuple-element.65.w_ref, bf16[2048,512]{1,0:T(8,128)(2,1)S(1)} %get-tuple-element.73.g0, bf16[2048,512]{1,0:T(8,128)(2,1)S(1)} %get-tuple-element.74.u0, ...), custom_call_target="tpu_custom_call" | custom-call | flops 1610612736 | bytes 1048576 | tf_op jit(solution)/shard_map/experts/pallas_call | solution.py:169
  100.7 7.0 %collective-permute-done.16.refs_0_ = bf16[64,2048]{1,0:T(8,128)(2,1)S(1)} collective-permute-done((bf16[64,2048]{1,0:T(8,128)(2,1)S(1)}, bf16[64,2048]{1,0:T(8,128)(2,1)S(1)}, u32[]{:S(2)}, u32[]{:S(2)}) %collective-permute-start.16) | collective-permute-done | bytes 262176 | tf_op jit(solution)/shard_map/ppermute | solution.py:245
  107.7 2.6 %experts.10 = (bf16[64,2048]{1,0:T(8,128)(2,1)S(1)}, bf16[64,2048]{1,0:T(8,128)(2,1)S(1)}) custom-call(s32[2]{0:T(128)S(1)} %pad_add_fusion.at_ref, f32[8,8,128]{2,1,0:T(8,128)S(1)} %get-tuple-element.65.w_ref, bf16[2048,512]{1,0:T(8,128)(2,1)S(1)} %get-tuple-element.73.g0, bf16[2048,512]{1,0:T(8,128)(2,1)S(1)} %get-tuple-element.74.u0, ...), custom_call_target="tpu_custom_call" | custom-call | flops 1610612736 | bytes 1048576 | tf_op jit(solution)/shard_map/experts/pallas_call | solution.py:169
  111.9 7.7 %collective-permute-done.19.refs_0_ = bf16[64,2048]{1,0:T(8,128)(2,1)S(1)} collective-permute-done((bf16[64,2048]{1,0:T(8,128)(2,1)S(1)}, bf16[64,2048]{1,0:T(8,128)(2,1)S(1)}, u32[]{:S(2)}, u32[]{:S(2)}) %collective-permute-start.19) | collective-permute-done | bytes 262176 | tf_op jit(solution)/shard_map/ppermute | solution.py:245
  119.6 2.6 %experts.11 = (bf16[64,2048]{1,0:T(8,128)(2,1)S(1)}, bf16[64,2048]{1,0:T(8,128)(2,1)S(1)}) custom-call(s32[2]{0:T(128)S(1)} %pad_add_fusion.at_ref, f32[8,8,128]{2,1,0:T(8,128)S(1)} %get-tuple-element.65.w_ref, bf16[2048,512]{1,0:T(8,128)(2,1)S(1)} %get-tuple-element.73.g0, bf16[2048,512]{1,0:T(8,128)(2,1)S(1)} %get-tuple-element.74.u0, ...), custom_call_target="tpu_custom_call" | custom-call | flops 1610612736 | bytes 1048576 | tf_op jit(solution)/shard_map/experts/pallas_call | solution.py:169
  123.8 7.7 %collective-permute-done.22.refs_0_ = bf16[64,2048]{1,0:T(8,128)(2,1)S(1)} collective-permute-done((bf16[64,2048]{1,0:T(8,128)(2,1)S(1)}, bf16[64,2048]{1,0:T(8,128)(2,1)S(1)}, u32[]{:S(2)}, u32[]{:S(2)}) %collective-permute-start.22) | collective-permute-done | bytes 262176 | tf_op jit(solution)/shard_map/ppermute | solution.py:245
  131.5 2.6 %experts.12 = (bf16[64,2048]{1,0:T(8,128)(2,1)S(1)}, bf16[64,2048]{1,0:T(8,128)(2,1)S(1)}) custom-call(s32[2]{0:T(128)S(1)} %pad_add_fusion.at_ref, f32[8,8,128]{2,1,0:T(8,128)S(1)} %get-tuple-element.65.w_ref, bf16[2048,512]{1,0:T(8,128)(2,1)S(1)} %get-tuple-element.73.g0, bf16[2048,512]{1,0:T(8,128)(2,1)S(1)} %get-tuple-element.74.u0, ...), custom_call_target="tpu_custom_call" | custom-call | flops 1610612736 | bytes 1048576 | tf_op jit(solution)/shard_map/experts/pallas_call | solution.py:169
  135.7 7.7 %collective-permute-done.25.refs_0_ = bf16[64,2048]{1,0:T(8,128)(2,1)S(1)} collective-permute-done((bf16[64,2048]{1,0:T(8,128)(2,1)S(1)}, bf16[64,2048]{1,0:T(8,128)(2,1)S(1)}, u32[]{:S(2)}, u32[]{:S(2)}) %collective-permute-start.25) | collective-permute-done | bytes 262176 | tf_op jit(solution)/shard_map/ppermute | solution.py:245
  143.3 2.6 %experts.13 = (bf16[64,2048]{1,0:T(8,128)(2,1)S(1)}, bf16[64,2048]{1,0:T(8,128)(2,1)S(1)}) custom-call(s32[2]{0:T(128)S(1)} %pad_add_fusion.at_ref, f32[8,8,128]{2,1,0:T(8,128)S(1)} %get-tuple-element.65.w_ref, bf16[2048,512]{1,0:T(8,128)(2,1)S(1)} %get-tuple-element.73.g0, bf16[2048,512]{1,0:T(8,128)(2,1)S(1)} %get-tuple-element.74.u0, ...), custom_call_target="tpu_custom_call" | custom-call | flops 1610612736 | bytes 1048576 | tf_op jit(solution)/shard_map/experts/pallas_call | solution.py:169
  147.6 7.7 %collective-permute-done.28.refs_0_ = bf16[64,2048]{1,0:T(8,128)(2,1)S(1)} collective-permute-done((bf16[64,2048]{1,0:T(8,128)(2,1)S(1)}, bf16[64,2048]{1,0:T(8,128)(2,1)S(1)}, u32[]{:S(2)}, u32[]{:S(2)}) %collective-permute-start.28) | collective-permute-done | bytes 262176 | tf_op jit(solution)/shard_map/ppermute | solution.py:245
  155.2 2.6 %experts.14 = (bf16[64,2048]{1,0:T(8,128)(2,1)S(1)}, bf16[64,2048]{1,0:T(8,128)(2,1)S(1)}) custom-call(s32[2]{0:T(128)S(1)} %pad_add_fusion.at_ref, f32[8,8,128]{2,1,0:T(8,128)S(1)} %get-tuple-element.65.w_ref, bf16[2048,512]{1,0:T(8,128)(2,1)S(1)} %get-tuple-element.73.g0, bf16[2048,512]{1,0:T(8,128)(2,1)S(1)} %get-tuple-element.74.u0, ...), custom_call_target="tpu_custom_call" | custom-call | flops 1610612736 | bytes 1048576 | tf_op jit(solution)/shard_map/experts/pallas_call | solution.py:169
  159.3 5.0 %collective-permute-done.30 = bf16[64,2048]{1,0:T(8,128)(2,1)S(1)} collective-permute-done((bf16[64,2048]{1,0:T(8,128)(2,1)S(1)}, bf16[64,2048]{1,0:T(8,128)(2,1)S(1)}, u32[]{:S(2)}, u32[]{:S(2)}) %collective-permute-start.30) | collective-permute-done | bytes 262176 | tf_op jit(solution)/shard_map/ppermute | solution.py:245
  164.4 2.7 %collective-permute-done.37 = bf16[64,2048]{1,0:T(8,128)(2,1)S(1)} collective-permute-done((bf16[64,2048]{1,0:T(8,128)(2,1)S(1)}, bf16[64,2048]{1,0:T(8,128)(2,1)S(1)}, u32[]{:S(2)}, u32[]{:S(2)}) %collective-permute-start.37) | collective-permute-done | bytes 262176 | tf_op jit(solution)/shard_map/ppermute | solution.py:245
  (83 shorter events, 41.2 us)
Async XLA Ops:
  3.2 8.5 %collective-permute-start = (bf16[528,128]{1,0:T(8,128)(2,1)S(1)}, bf16[528,128]{1,0:T(8,128)(2,1)S(1)}, u32[]{:S(2)}, u32[]{:S(2)}) collective-permute-start(bf16[528,128]{1,0:T(8,128)(2,1)S(1)} %get-tuple-element.55), channel_id=1, source_target_pairs={{0,2},{2,4},{4,6},{6,0},{8,10},{10,12},{12,14},{14,8},{1,3},{3,5},... | collective-permute-start | bytes 405512 | tf_op jit(solution)/shard_map/ppermute | solution.py:252
  6.3 6.5 %collective-permute-start.1 = (bf16[528,128]{1,0:T(8,128)(2,1)S(1)}, bf16[528,128]{1,0:T(8,128)(2,1)S(1)}, u32[]{:S(2)}, u32[]{:S(2)}) collective-permute-start(bf16[528,128]{1,0:T(8,128)(2,1)S(1)} %get-tuple-element.56), channel_id=1, source_target_pairs={{0,4},{2,6},{4,0},{6,2},{8,12},{10,14},{12,8},{14,10},{1,5},{3,7},... | collective-permute-start | bytes 405512 | tf_op jit(solution)/shard_map/ppermute | solution.py:252
  9.3 68.1 %collective-permute-start.10 = (bf16[512,2048]{1,0:T(8,128)(2,1)}, bf16[512,2048]{1,0:T(8,128)(2,1)S(1)}, u32[]{:S(2)}, u32[]{:S(2)}) collective-permute-start(bf16[512,2048]{1,0:T(8,128)(2,1)} %bitcast.24), channel_id=1, source_target_pairs={{0,1},{1,0},{2,3},{3,2},{4,5},{5,4},{6,7},{7,6},{8,9},{9,8},{10,11... | collective-permute-start | bytes 6291464 | tf_op jit(solution)/shard_map/ppermute | solution.py:234
  9.3 68.1 %collective-permute-start.8 = (bf16[2048,512]{1,0:T(8,128)(2,1)}, bf16[2048,512]{1,0:T(8,128)(2,1)S(1)}, u32[]{:S(2)}, u32[]{:S(2)}) collective-permute-start(bf16[2048,512]{1,0:T(8,128)(2,1)} %bitcast.20), channel_id=1, source_target_pairs={{0,1},{1,0},{2,3},{3,2},{4,5},{5,4},{6,7},{7,6},{8,9},{9,8},{10,11... | collective-permute-start | bytes 6291464 | tf_op jit(solution)/shard_map/ppermute | solution.py:234
  11.7 65.7 %collective-permute-start.9 = (bf16[2048,512]{1,0:T(8,128)(2,1)}, bf16[2048,512]{1,0:T(8,128)(2,1)S(1)}, u32[]{:S(2)}, u32[]{:S(2)}) collective-permute-start(bf16[2048,512]{1,0:T(8,128)(2,1)} %bitcast.22), channel_id=1, source_target_pairs={{0,1},{1,0},{2,3},{3,2},{4,5},{5,4},{6,7},{7,6},{8,9},{9,8},{10,11... | collective-permute-start | bytes 6291464 | tf_op jit(solution)/shard_map/ppermute | solution.py:234
  13.9 9.3 %collective-permute-start.3 = (bf16[576,128]{1,0:T(8,128)(2,1)S(1)}, bf16[576,128]{1,0:T(8,128)(2,1)S(1)}, u32[]{:S(2)}, u32[]{:S(2)}) collective-permute-start(bf16[576,128]{1,0:T(8,128)(2,1)S(1)} %total.1), channel_id=1, source_target_pairs={{0,8},{2,10},{4,12},{6,14},{8,0},{10,2},{12,4},{14,6},{1,9},{3,11}... | collective-permute-start | bytes 442376 | tf_op jit(solution)/shard_map/ppermute | solution.py:296
  25.3 6.6 %collective-permute-start.5 = (bf16[512,128]{1,0:T(8,128)(2,1)S(1)}, bf16[512,128]{1,0:T(8,128)(2,1)S(1)}, u32[]{:S(2)}, u32[]{:S(2)}) collective-permute-start(bf16[512,128]{1,0:T(8,128)(2,1)S(1)} %get-tuple-element.60), channel_id=1, source_target_pairs={{0,4},{2,6},{4,0},{6,2},{8,12},{10,14},{12,8},{14,10},{1,5},{3,7},... | collective-permute-start | bytes 393224 | tf_op jit(solution)/shard_map/ppermute | solution.py:252
  29.0 6.4 %collective-permute-start.6 = (bf16[512,128]{1,0:T(8,128)(2,1)S(1)}, bf16[512,128]{1,0:T(8,128)(2,1)S(1)}, u32[]{:S(2)}, u32[]{:S(2)}) collective-permute-start(bf16[512,128]{1,0:T(8,128)(2,1)S(1)} %get-tuple-element.61), channel_id=1, source_target_pairs={{0,2},{2,4},{4,6},{6,0},{8,10},{10,12},{12,14},{14,8},{1,3},{3,5},... | collective-permute-start | bytes 393224 | tf_op jit(solution)/shard_map/ppermute | solution.py:252
  37.6 6.4 %collective-permute-start.11 = (bf16[64,2048]{1,0:T(8,128)(2,1)S(1)}, bf16[64,2048]{1,0:T(8,128)(2,1)S(1)}, u32[]{:S(2)}, u32[]{:S(2)}) collective-permute-start(bf16[64,2048]{1,0:T(8,128)(2,1)S(1)} %get-tuple-element.66.after_ref.refs_1_), channel_id=1, source_target_pairs={{0,4},{1,3},{4,8},{5,1},{8,12},{9,5},{12,14},{13,9},{14,10},{15,13... | collective-permute-start | bytes 786440 | tf_op jit(solution)/shard_map/ppermute | solution.py:245
  63.2 6.4 %collective-permute-start.23 = (bf16[64,2048]{1,0:T(8,128)(2,1)S(1)}, bf16[64,2048]{1,0:T(8,128)(2,1)S(1)}, u32[]{:S(2)}, u32[]{:S(2)}) collective-permute-start(bf16[64,2048]{1,0:T(8,128)(2,1)S(1)} %collective-permute-done.20.refs_1_), channel_id=1, source_target_pairs={{0,4},{1,3},{4,8},{5,1},{8,12},{9,5},{12,14},{13,9},{14,10},{15,13... | collective-permute-start | bytes 786440 | tf_op jit(solution)/shard_map/ppermute | solution.py:245
  71.0 14.4 %collective-permute-start.7 = (bf16[64,2048]{1,0:T(8,128)(2,1)S(1)}, bf16[64,2048]{1,0:T(8,128)(2,1)S(1)}, u32[]{:S(2)}, u32[]{:S(2)}) collective-permute-start(bf16[64,2048]{1,0:T(8,128)(2,1)S(1)} %get-tuple-element.63.after_ref.refs_0_), channel_id=1, source_target_pairs={{0,4},{1,3},{4,8},{5,1},{8,12},{9,5},{12,14},{13,9},{14,10},{15,13... | collective-permute-start | bytes 786440 | tf_op jit(solution)/shard_map/ppermute | solution.py:245
  75.9 71.7 %collective-permute-start.29 = (bf16[64,2048]{1,0:T(8,128)(2,1)S(1)}, bf16[64,2048]{1,0:T(8,128)(2,1)S(1)}, u32[]{:S(2)}, u32[]{:S(2)}) collective-permute-start(bf16[64,2048]{1,0:T(8,128)(2,1)S(1)} %collective-permute-done.26.refs_1_), channel_id=1, source_target_pairs={{0,4},{1,3},{4,8},{5,1},{8,12},{9,5},{12,14},{13,9},{14,10},{15,13... | collective-permute-start | bytes 786440 | tf_op jit(solution)/shard_map/ppermute | solution.py:245
  85.5 10.3 %collective-permute-start.13 = (bf16[64,2048]{1,0:T(8,128)(2,1)S(1)}, bf16[64,2048]{1,0:T(8,128)(2,1)S(1)}, u32[]{:S(2)}, u32[]{:S(2)}) collective-permute-start(bf16[64,2048]{1,0:T(8,128)(2,1)S(1)} %collective-permute-done.7.refs_0_), channel_id=1, source_target_pairs={{0,4},{1,3},{4,8},{5,1},{8,12},{9,5},{12,14},{13,9},{14,10},{15,13... | collective-permute-start | bytes 786440 | tf_op jit(solution)/shard_map/ppermute | solution.py:245
  90.6 7.8 %collective-permute-start.12 = (bf16[64,2048]{1,0:T(8,128)(2,1)S(1)}, bf16[64,2048]{1,0:T(8,128)(2,1)S(1)}, u32[]{:S(2)}, u32[]{:S(2)}) collective-permute-start(bf16[64,2048]{1,0:T(8,128)(2,1)S(1)} %get-tuple-element.80), channel_id=1, source_target_pairs={{0,4},{1,3},{4,8},{5,1},{8,12},{9,5},{12,14},{13,9},{14,10},{15,13... | collective-permute-start | bytes 786440 | tf_op jit(solution)/shard_map/ppermute | solution.py:245
  91.2 8.6 %collective-permute-start.31 = (bf16[64,2048]{1,0:T(8,128)(2,1)S(1)}, bf16[64,2048]{1,0:T(8,128)(2,1)S(1)}, u32[]{:S(2)}, u32[]{:S(2)}) collective-permute-start(bf16[64,2048]{1,0:T(8,128)(2,1)S(1)} %get-tuple-element.88), channel_id=1, source_target_pairs={{0,4},{1,3},{4,8},{5,1},{8,12},{9,5},{12,14},{13,9},{14,10},{15,13... | collective-permute-start | bytes 786440 | tf_op jit(solution)/shard_map/ppermute | solution.py:245
  98.5 11.8 %collective-permute-start.15 = (bf16[64,2048]{1,0:T(8,128)(2,1)S(1)}, bf16[64,2048]{1,0:T(8,128)(2,1)S(1)}, u32[]{:S(2)}, u32[]{:S(2)}) collective-permute-start(bf16[64,2048]{1,0:T(8,128)(2,1)S(1)} %add_convert_fusion.13), channel_id=1, source_target_pairs={{0,4},{1,3},{4,8},{5,1},{8,12},{9,5},{12,14},{13,9},{14,10},{15,13... | collective-permute-start | bytes 786440 | tf_op jit(solution)/shard_map/ppermute | solution.py:245
  98.6 9.1 %collective-permute-start.16 = (bf16[64,2048]{1,0:T(8,128)(2,1)S(1)}, bf16[64,2048]{1,0:T(8,128)(2,1)S(1)}, u32[]{:S(2)}, u32[]{:S(2)}) collective-permute-start(bf16[64,2048]{1,0:T(8,128)(2,1)S(1)} %collective-permute-done.13.refs_0_), channel_id=1, source_target_pairs={{0,4},{1,3},{4,8},{5,1},{8,12},{9,5},{12,14},{13,9},{14,10},{15,13... | collective-permute-start | bytes 786440 | tf_op jit(solution)/shard_map/ppermute | solution.py:245
  99.9 11.7 %collective-permute-start.32 = (bf16[64,2048]{1,0:T(8,128)(2,1)S(1)}, bf16[64,2048]{1,0:T(8,128)(2,1)S(1)}, u32[]{:S(2)}, u32[]{:S(2)}) collective-permute-start(bf16[64,2048]{1,0:T(8,128)(2,1)S(1)} %add_convert_fusion.6), channel_id=1, source_target_pairs={{0,4},{1,3},{4,8},{5,1},{8,12},{9,5},{12,14},{13,9},{14,10},{15,13... | collective-permute-start | bytes 786440 | tf_op jit(solution)/shard_map/ppermute | solution.py:245
  110.3 11.8 %collective-permute-start.18 = (bf16[64,2048]{1,0:T(8,128)(2,1)S(1)}, bf16[64,2048]{1,0:T(8,128)(2,1)S(1)}, u32[]{:S(2)}, u32[]{:S(2)}) collective-permute-start(bf16[64,2048]{1,0:T(8,128)(2,1)S(1)} %add_convert_fusion.12), channel_id=1, source_target_pairs={{0,4},{1,3},{4,8},{5,1},{8,12},{9,5},{12,14},{13,9},{14,10},{15,13... | collective-permute-start | bytes 786440 | tf_op jit(solution)/shard_map/ppermute | solution.py:245
  110.5 9.1 %collective-permute-start.19 = (bf16[64,2048]{1,0:T(8,128)(2,1)S(1)}, bf16[64,2048]{1,0:T(8,128)(2,1)S(1)}, u32[]{:S(2)}, u32[]{:S(2)}) collective-permute-start(bf16[64,2048]{1,0:T(8,128)(2,1)S(1)} %collective-permute-done.16.refs_0_), channel_id=1, source_target_pairs={{0,4},{1,3},{4,8},{5,1},{8,12},{9,5},{12,14},{13,9},{14,10},{15,13... | collective-permute-start | bytes 786440 | tf_op jit(solution)/shard_map/ppermute | solution.py:245
  111.7 11.8 %collective-permute-start.33 = (bf16[64,2048]{1,0:T(8,128)(2,1)S(1)}, bf16[64,2048]{1,0:T(8,128)(2,1)S(1)}, u32[]{:S(2)}, u32[]{:S(2)}) collective-permute-start(bf16[64,2048]{1,0:T(8,128)(2,1)S(1)} %add_convert_fusion.5), channel_id=1, source_target_pairs={{0,4},{1,3},{4,8},{5,1},{8,12},{9,5},{12,14},{13,9},{14,10},{15,13... | collective-permute-start | bytes 786440 | tf_op jit(solution)/shard_map/ppermute | solution.py:245
  122.2 11.8 %collective-permute-start.21 = (bf16[64,2048]{1,0:T(8,128)(2,1)S(1)}, bf16[64,2048]{1,0:T(8,128)(2,1)S(1)}, u32[]{:S(2)}, u32[]{:S(2)}) collective-permute-start(bf16[64,2048]{1,0:T(8,128)(2,1)S(1)} %add_convert_fusion.11), channel_id=1, source_target_pairs={{0,4},{1,3},{4,8},{5,1},{8,12},{9,5},{12,14},{13,9},{14,10},{15,13... | collective-permute-start | bytes 786440 | tf_op jit(solution)/shard_map/ppermute | solution.py:245
  122.3 9.1 %collective-permute-start.22 = (bf16[64,2048]{1,0:T(8,128)(2,1)S(1)}, bf16[64,2048]{1,0:T(8,128)(2,1)S(1)}, u32[]{:S(2)}, u32[]{:S(2)}) collective-permute-start(bf16[64,2048]{1,0:T(8,128)(2,1)S(1)} %collective-permute-done.19.refs_0_), channel_id=1, source_target_pairs={{0,4},{1,3},{4,8},{5,1},{8,12},{9,5},{12,14},{13,9},{14,10},{15,13... | collective-permute-start | bytes 786440 | tf_op jit(solution)/shard_map/ppermute | solution.py:245
  123.5 11.8 %collective-permute-start.34 = (bf16[64,2048]{1,0:T(8,128)(2,1)S(1)}, bf16[64,2048]{1,0:T(8,128)(2,1)S(1)}, u32[]{:S(2)}, u32[]{:S(2)}) collective-permute-start(bf16[64,2048]{1,0:T(8,128)(2,1)S(1)} %add_convert_fusion.4), channel_id=1, source_target_pairs={{0,4},{1,3},{4,8},{5,1},{8,12},{9,5},{12,14},{13,9},{14,10},{15,13... | collective-permute-start | bytes 786440 | tf_op jit(solution)/shard_map/ppermute | solution.py:245
  134.1 11.8 %collective-permute-start.24 = (bf16[64,2048]{1,0:T(8,128)(2,1)S(1)}, bf16[64,2048]{1,0:T(8,128)(2,1)S(1)}, u32[]{:S(2)}, u32[]{:S(2)}) collective-permute-start(bf16[64,2048]{1,0:T(8,128)(2,1)S(1)} %add_convert_fusion.10), channel_id=1, source_target_pairs={{0,4},{1,3},{4,8},{5,1},{8,12},{9,5},{12,14},{13,9},{14,10},{15,13... | collective-permute-start | bytes 786440 | tf_op jit(solution)/shard_map/ppermute | solution.py:245
  134.2 9.1 %collective-permute-start.25 = (bf16[64,2048]{1,0:T(8,128)(2,1)S(1)}, bf16[64,2048]{1,0:T(8,128)(2,1)S(1)}, u32[]{:S(2)}, u32[]{:S(2)}) collective-permute-start(bf16[64,2048]{1,0:T(8,128)(2,1)S(1)} %collective-permute-done.22.refs_0_), channel_id=1, source_target_pairs={{0,4},{1,3},{4,8},{5,1},{8,12},{9,5},{12,14},{13,9},{14,10},{15,13... | collective-permute-start | bytes 786440 | tf_op jit(solution)/shard_map/ppermute | solution.py:245
  135.4 11.8 %collective-permute-start.35 = (bf16[64,2048]{1,0:T(8,128)(2,1)S(1)}, bf16[64,2048]{1,0:T(8,128)(2,1)S(1)}, u32[]{:S(2)}, u32[]{:S(2)}) collective-permute-start(bf16[64,2048]{1,0:T(8,128)(2,1)S(1)} %add_convert_fusion.3), channel_id=1, source_target_pairs={{0,4},{1,3},{4,8},{5,1},{8,12},{9,5},{12,14},{13,9},{14,10},{15,13... | collective-permute-start | bytes 786440 | tf_op jit(solution)/shard_map/ppermute | solution.py:245
  146.0 11.8 %collective-permute-start.27 = (bf16[64,2048]{1,0:T(8,128)(2,1)S(1)}, bf16[64,2048]{1,0:T(8,128)(2,1)S(1)}, u32[]{:S(2)}, u32[]{:S(2)}) collective-permute-start(bf16[64,2048]{1,0:T(8,128)(2,1)S(1)} %add_convert_fusion.9), channel_id=1, source_target_pairs={{0,4},{1,3},{4,8},{5,1},{8,12},{9,5},{12,14},{13,9},{14,10},{15,13... | collective-permute-start | bytes 786440 | tf_op jit(solution)/shard_map/ppermute | solution.py:245
  146.1 9.1 %collective-permute-start.28 = (bf16[64,2048]{1,0:T(8,128)(2,1)S(1)}, bf16[64,2048]{1,0:T(8,128)(2,1)S(1)}, u32[]{:S(2)}, u32[]{:S(2)}) collective-permute-start(bf16[64,2048]{1,0:T(8,128)(2,1)S(1)} %collective-permute-done.25.refs_0_), channel_id=1, source_target_pairs={{0,4},{1,3},{4,8},{5,1},{8,12},{9,5},{12,14},{13,9},{14,10},{15,13... | collective-permute-start | bytes 786440 | tf_op jit(solution)/shard_map/ppermute | solution.py:245
  147.3 10.7 %collective-permute-start.36 = (bf16[64,2048]{1,0:T(8,128)(2,1)S(1)}, bf16[64,2048]{1,0:T(8,128)(2,1)S(1)}, u32[]{:S(2)}, u32[]{:S(2)}) collective-permute-start(bf16[64,2048]{1,0:T(8,128)(2,1)S(1)} %add_convert_fusion.2), channel_id=1, source_target_pairs={{0,4},{1,3},{4,8},{5,1},{8,12},{9,5},{12,14},{13,9},{14,10},{15,13... | collective-permute-start | bytes 786440 | tf_op jit(solution)/shard_map/ppermute | solution.py:245
  157.9 6.4 %collective-permute-start.30 = (bf16[64,2048]{1,0:T(8,128)(2,1)S(1)}, bf16[64,2048]{1,0:T(8,128)(2,1)S(1)}, u32[]{:S(2)}, u32[]{:S(2)}) collective-permute-start(bf16[64,2048]{1,0:T(8,128)(2,1)S(1)} %add_convert_fusion.8), channel_id=1, source_target_pairs={{0,4},{1,3},{4,8},{5,1},{8,12},{9,5},{12,14},{13,9},{14,10},{15,13... | collective-permute-start | bytes 786440 | tf_op jit(solution)/shard_map/ppermute | solution.py:245
  158.1 9.0 %collective-permute-start.37 = (bf16[64,2048]{1,0:T(8,128)(2,1)S(1)}, bf16[64,2048]{1,0:T(8,128)(2,1)S(1)}, u32[]{:S(2)}, u32[]{:S(2)}) collective-permute-start(bf16[64,2048]{1,0:T(8,128)(2,1)S(1)} %add_convert_fusion.1), channel_id=1, source_target_pairs={{0,4},{1,3},{4,8},{5,1},{8,12},{9,5},{12,14},{13,9},{14,10},{15,13... | collective-permute-start | bytes 786440 | tf_op jit(solution)/shard_map/ppermute | solution.py:245
  (9 other events, 41.1 us)
where the time goes:
time: 168 us
  waiting for transfers between devices  86.2 us (51%)
  starting transfers between devices  41.7 us (25%)
  Pallas kernels  33.2 us (20%)
  local copies, waits for them, and re-layouts  3.31 us (2%)
  other arithmetic  2.72 us (2%)
    ppermute x28, waiting for transfers between devices, hop(): return lax.ppermute(value, ('seq', 'expert'), hops)  72.2 us
    ppermute x28, starting transfers between devices, hop(): return lax.ppermute(value, ('seq', 'expert'), hops)  26.8 us
    pallas_call x8, Pallas kernels, run_experts(): pl.pallas_call(functools.partial(expert_kernel, hop), in_specs=[SMEM] + [...  20.5 us
    ppermute x6, starting transfers between devices, along(): lax.ppermute(blocks[r], 'seq', [(s, to(s, r)) for s in range(n_seq)])  11.7 us
    ppermute x6, waiting for transfers between devices, along(): lax.ppermute(blocks[r], 'seq', [(s, to(s, r)) for s in range(n_seq)])  9.75 us
    pallas_call x2, Pallas kernels, load(): pl.pallas_call(functools.partial(load_kernel, count), in_specs=[HBM] * (c...  6.11 us
    ppermute x1, waiting for transfers between devices, per_device(): lax.ppermute(near, 'seq', [(s, (s + half) % n_seq) for s in range(n_seq)])  4.22 us
  transfers between devices with their start and end apart: 38, of which 20 were waited for; matrix products, arithmetic and copies ran while one was open for 1% of the time, Pallas kernels for 18%

commit v1 on v0

--- a/solution.py
+++ b/solution.py
@@ -71,7 +71,8 @@
         send_ref[part:, :] = jnp.concatenate(rows + [zero], axis=0).astype(bf16)
 
 
-def total_kernel(half, *refs):
+def total_kernel(half, after_ref, *refs):
+    del after_ref
     gots, send_ref = refs[:half], refs[half]
     part = gots[0].shape[0] - PAD
     total = gots[0][:part, :].astype(f32)
@@ -231,7 +232,6 @@
     _, rows, width = queries.shape
     q, k, v = queries[0], key_rows[0], value_rows[0]
     own = (w_gate[0], w_up[0], w_down[0])
-    other = tuple(lax.ppermute(w, "expert", [(0, 1), (1, 0)]) for w in own)
     half = n_seq // 2
     at = jnp.stack([lax.axis_index("seq"), lax.axis_index("expert")])
 
@@ -245,13 +245,11 @@
         return lax.ppermute(value, ("seq", "expert"), hops)
 
     def along(blocks, sign):
-        def to(s, r):
-            return s // half * half + (s + sign * r) % half
-
-        return [blocks[0]] + [
-            lax.ppermute(blocks[r], "seq", [(s, to(s, r)) for s in range(n_seq)])
-            for r in range(1, half)
-        ]
+        moved = [blocks[0]]
+        for r in range(1, half):
+            pairs = [(s, s // half * half + (s + sign * r) % half) for s in range(n_seq)]
+            moved.append(lax.ppermute(blocks[r], "seq", pairs))
+        return moved
 
     part = width // half
     sends = pl.pallas_call(
@@ -284,15 +282,17 @@
         ),
         name="local",
     )(q, k, v)
+    own = load(sends[0], *own)
+    other = [lax.ppermute(w, "expert", [(0, 1), (1, 0)]) for w in own]
     gots = along(sends, 1)
     near = pl.pallas_call(
         functools.partial(total_kernel, half),
-        in_specs=[VMEM] * half,
+        in_specs=[ANY] + [VMEM] * half,
         out_specs=VMEM,
         compiler_params=SMALL,
         out_shape=jax.ShapeDtypeStruct((part + PAD * half, HEAD_DIM), bf16),
         name="total",
-    )(*gots)
+    )(own[0], *gots)
     far = lax.ppermute(near, "seq", [(s, (s + half) % n_seq) for s in range(n_seq)])
     *backs, shares = pl.pallas_call(
         functools.partial(prefix_kernel, half),
@@ -323,13 +323,11 @@
         )(at, normed[-1] if normed else within, q, within, head_gain, ffn_gain, *carried)
         attention.append(att_piece)
         normed.append(normed_piece)
-    weights = load(normed[-1], *own, *other)
+    weights = [*own, *other]
 
     held, partial, first = normed, None, None
     for step in range(n_seq):
         following = [hop(x) for x in held] if step < n_seq - 1 else held
-        if step == 0:
-            following[0], *weights = lax.optimization_barrier((following[0], *weights))
         result = run_experts(step, at, held, shares, weights)
         if step == 0:
             first = result
@@ -344,7 +342,8 @@
         (a.astype(f32) + (p.astype(f32) + r.astype(f32))).astype(bf16)
         for a, p, r in zip(attention, partial, first)
     ]
-    return jnp.concatenate(attention)[None], jnp.concatenate(layer_out)[None]
+    attention = jnp.concatenate(attention)[None]
+    return attention, jnp.concatenate(layer_out)[None]
 
 
 def solution(mesh):

time: 168 us -> 147 us (0.88)
  waiting for transfers between devices: 86.2 us -> 49.8 us
  starting transfers between devices: 41.7 us -> 62 us
  local copies, waits for them, and re-layouts: 3.31 us -> 0 us
    ppermute x28, waiting for transfers between devices: 72.2 us -> 38.7 us  [hop(): return lax.ppermute(value, ('seq', 'expert'), hops)]
    ppermute x28, starting transfers between devices: 26.8 us -> 47 us  [hop(): return lax.ppermute(value, ('seq', 'expert'), hops)]
    unnamed x6 -> x0, local copies, waits for them, and re-layouts: 3.31 us -> none
    ppermute x9, waiting for transfers between devices: 9.76 us -> 6.78 us  [the longest x6 6.77 us: along(): moved.append(lax.ppermute(blocks[r], 'seq', pairs))]
    pallas_call x2, Pallas kernels: 6.11 us -> 4.29 us  [load(): pl.pallas_call(functools.partial(load_kernel, count), in_specs=[HBM] * (c...]
  transfers between devices with their start and end apart: 38 -> 38, of which waited for: 20 -> 28; matrix products, arithmetic and copies ran while one was open for 1% -> 1% of each run, Pallas kernels for 18% -> 20%
where the time goes in v1:
time: 147 us
  starting transfers between devices  62 us (42%)
  waiting for transfers between devices  49.8 us (34%)
  Pallas kernels  31.6 us (21%)
  other arithmetic  2.72 us (2%)
    ppermute x28, starting transfers between devices, hop(): return lax.ppermute(value, ('seq', 'expert'), hops)  47 us
    ppermute x28, waiting for transfers between devices, hop(): return lax.ppermute(value, ('seq', 'expert'), hops)  38.7 us
    pallas_call x8, Pallas kernels, run_experts(): pl.pallas_call(functools.partial(expert_kernel, hop), in_specs=[SMEM] + [...  20.8 us
    ppermute x6, starting transfers between devices, along(): moved.append(lax.ppermute(blocks[r], 'seq', pairs))  11.6 us
    ppermute x6, waiting for transfers between devices, along(): moved.append(lax.ppermute(blocks[r], 'seq', pairs))  6.77 us
    pallas_call x2, Pallas kernels, load(): pl.pallas_call(functools.partial(load_kernel, count), in_specs=[HBM] * (c...  4.29 us
    ppermute x1, waiting for transfers between devices, per_device(): lax.ppermute(near, 'seq', [(s, (s + half) % n_seq) for s in range(n_seq)])  4.28 us
  transfers between devices with their start and end apart: 38, of which 28 were waited for; matrix products, arithmetic and copies ran while one was open for 1% of the time, Pallas kernels for 20%

profile of v1, /device:TPU:0, one launch (start us, length us, event | category | flops | bytes accessed | tf_op | source)
XLA Modules:
  0.0 147.0 jit_solution(5537514949116999171)
XLA Ops:
  0.7 2.5 %states.1 = (bf16[528,128]{1,0:T(8,128)(2,1)S(1)}, bf16[528,128]{1,0:T(8,128)(2,1)S(1)}, bf16[528,128]{1,0:T(8,128)(2,1)S(1)}, bf16[528,128]{1,0:T(8,128)(2,1)S(1)}) custom-call(s32[2]{0:T(128)S(1)} %pad_add_fusion.at_ref, s32[8,128]{1,0:T(8,128)} %bitcast.30, f32[8,128]{1,0:T(8,128)} %bitcast.31, bf16[128,2048]{1,0:T(8,128)(2,1)} %bitcast.20, ...), custom_call_target="tpu_custom_call" | custom-call | tf_op jit(solution)/shard_map/states/pallas_call | solution.py:255
  3.2 3.0 %collective-permute-start = (bf16[528,128]{1,0:T(8,128)(2,1)S(1)}, bf16[528,128]{1,0:T(8,128)(2,1)S(1)}, u32[]{:S(2)}, u32[]{:S(2)}) collective-permute-start(bf16[528,128]{1,0:T(8,128)(2,1)S(1)} %get-tuple-element.46), channel_id=1, source_target_pairs={{0,2},{2,4},{4,6},{6,0},{8,10},{10,12},{12,14},{14,8},{1,3},{3,5},... | collective-permute-start | bytes 405512 | tf_op jit(solution)/shard_map/ppermute | solution.py:251
  9.3 2.9 %load.3 = (bf16[2048,512]{1,0:T(8,128)(2,1)S(1)}, bf16[2048,512]{1,0:T(8,128)(2,1)S(1)}, bf16[512,2048]{1,0:T(8,128)(2,1)S(1)}) custom-call(bf16[528,128]{1,0:T(8,128)(2,1)S(1)} %get-tuple-element.39.after_ref.refs_0_, bf16[2048,512]{1,0:T(8,128)(2,1)} %bitcast.24, bf16[2048,512]{1,0:T(8,128)(2,1)} %bitcast.25, bf16[512,2048]{1,0:T(8,128)(2,1)} %bitcast.26), custom_call_target="tpu_custom_call" | custom-call | bytes 6291456 | tf_op jit(solution)/shard_map/load/pallas_call | solution.py:203
  13.9 2.8 %collective-permute-start.3 = (bf16[576,128]{1,0:T(8,128)(2,1)S(1)}, bf16[576,128]{1,0:T(8,128)(2,1)S(1)}, u32[]{:S(2)}, u32[]{:S(2)}) collective-permute-start(bf16[576,128]{1,0:T(8,128)(2,1)S(1)} %total.1), channel_id=1, source_target_pairs={{0,8},{2,10},{4,12},{6,14},{8,0},{10,2},{12,4},{14,6},{1,9},{3,11}... | collective-permute-start | bytes 442376 | tf_op jit(solution)/shard_map/ppermute | solution.py:296
  18.9 4.3 %collective-permute-done.3.far_ref = bf16[576,128]{1,0:T(8,128)(2,1)S(1)} collective-permute-done((bf16[576,128]{1,0:T(8,128)(2,1)S(1)}, bf16[576,128]{1,0:T(8,128)(2,1)S(1)}, u32[]{:S(2)}, u32[]{:S(2)}) %collective-permute-start.3) | collective-permute-done | bytes 147488 | tf_op jit(solution)/shard_map/ppermute | solution.py:296
  26.7 2.4 %collective-permute-done.4.refs_1_ = bf16[512,128]{1,0:T(8,128)(2,1)S(1)} collective-permute-done((bf16[512,128]{1,0:T(8,128)(2,1)S(1)}, bf16[512,128]{1,0:T(8,128)(2,1)S(1)}, u32[]{:S(2)}, u32[]{:S(2)}) %collective-permute-start.4) | collective-permute-done | bytes 131104 | tf_op jit(solution)/shard_map/ppermute | solution.py:251
  29.0 2.9 %collective-permute-start.6 = (bf16[512,128]{1,0:T(8,128)(2,1)S(1)}, bf16[512,128]{1,0:T(8,128)(2,1)S(1)}, u32[]{:S(2)}, u32[]{:S(2)}) collective-permute-start(bf16[512,128]{1,0:T(8,128)(2,1)S(1)} %get-tuple-element.52), channel_id=1, source_target_pairs={{0,2},{2,4},{4,6},{6,0},{8,10},{10,12},{12,14},{14,8},{1,3},{3,5},... | collective-permute-start | bytes 393224 | tf_op jit(solution)/shard_map/ppermute | solution.py:251
  31.9 3.4 %collective-permute-done.6.refs_3_ = bf16[512,128]{1,0:T(8,128)(2,1)S(1)} collective-permute-done((bf16[512,128]{1,0:T(8,128)(2,1)S(1)}, bf16[512,128]{1,0:T(8,128)(2,1)S(1)}, u32[]{:S(2)}, u32[]{:S(2)}) %collective-permute-start.6) | collective-permute-done | bytes 131104 | tf_op jit(solution)/shard_map/ppermute | solution.py:251
  38.7 3.0 %collective-permute-start.10 = (bf16[64,2048]{1,0:T(8,128)(2,1)S(1)}, bf16[64,2048]{1,0:T(8,128)(2,1)S(1)}, u32[]{:S(2)}, u32[]{:S(2)}) collective-permute-start(bf16[64,2048]{1,0:T(8,128)(2,1)S(1)} %get-tuple-element.54.after_ref.refs_0_), channel_id=1, source_target_pairs={{0,4},{1,3},{4,8},{5,1},{8,12},{9,5},{12,14},{13,9},{14,10},{15,13... | collective-permute-start | bytes 786440 | tf_op jit(solution)/shard_map/ppermute | solution.py:245
  41.6 2.4 %collective-permute-done.11.refs_1_ = bf16[64,2048]{1,0:T(8,128)(2,1)S(1)} collective-permute-done((bf16[64,2048]{1,0:T(8,128)(2,1)S(1)}, bf16[64,2048]{1,0:T(8,128)(2,1)S(1)}, u32[]{:S(2)}, u32[]{:S(2)}) %collective-permute-start.11) | collective-permute-done | bytes 262176 | tf_op jit(solution)/shard_map/ppermute | solution.py:245
  48.3 2.1 %collective-permute-done.14.refs_1_ = bf16[64,2048]{1,0:T(8,128)(2,1)S(1)} collective-permute-done((bf16[64,2048]{1,0:T(8,128)(2,1)S(1)}, bf16[64,2048]{1,0:T(8,128)(2,1)S(1)}, u32[]{:S(2)}, u32[]{:S(2)}) %collective-permute-start.14) | collective-permute-done | bytes 262176 | tf_op jit(solution)/shard_map/ppermute | solution.py:245
  54.7 2.1 %collective-permute-done.17.refs_1_ = bf16[64,2048]{1,0:T(8,128)(2,1)S(1)} collective-permute-done((bf16[64,2048]{1,0:T(8,128)(2,1)S(1)}, bf16[64,2048]{1,0:T(8,128)(2,1)S(1)}, u32[]{:S(2)}, u32[]{:S(2)}) %collective-permute-start.17) | collective-permute-done | bytes 262176 | tf_op jit(solution)/shard_map/ppermute | solution.py:245
  61.1 2.1 %collective-permute-done.20.refs_1_ = bf16[64,2048]{1,0:T(8,128)(2,1)S(1)} collective-permute-done((bf16[64,2048]{1,0:T(8,128)(2,1)S(1)}, bf16[64,2048]{1,0:T(8,128)(2,1)S(1)}, u32[]{:S(2)}, u32[]{:S(2)}) %collective-permute-start.20) | collective-permute-done | bytes 262176 | tf_op jit(solution)/shard_map/ppermute | solution.py:245
  67.5 2.1 %collective-permute-done.23.refs_1_ = bf16[64,2048]{1,0:T(8,128)(2,1)S(1)} collective-permute-done((bf16[64,2048]{1,0:T(8,128)(2,1)S(1)}, bf16[64,2048]{1,0:T(8,128)(2,1)S(1)}, u32[]{:S(2)}, u32[]{:S(2)}) %collective-permute-start.23) | collective-permute-done | bytes 262176 | tf_op jit(solution)/shard_map/ppermute | solution.py:245
  80.2 2.6 %experts.8 = (bf16[64,2048]{1,0:T(8,128)(2,1)S(1)}, bf16[64,2048]{1,0:T(8,128)(2,1)S(1)}) custom-call(s32[2]{0:T(128)S(1)} %pad_add_fusion.at_ref, f32[8,8,128]{2,1,0:T(8,128)S(1)} %get-tuple-element.56.w_ref, bf16[2048,512]{1,0:T(8,128)(2,1)S(1)} %get-tuple-element.45.after_ref.g0, bf16[2048,512]{1,0:T(8,128)(2,1)S(1)} %get-tuple-element.57.u0, ...), custom_call_target="tpu_custom_call" | custom-call | flops 1610612736 | bytes 1048576 | tf_op jit(solution)/shard_map/experts/pallas_call | solution.py:170
  82.8 2.5 %collective-permute-start.12 = (bf16[64,2048]{1,0:T(8,128)(2,1)S(1)}, bf16[64,2048]{1,0:T(8,128)(2,1)S(1)}, u32[]{:S(2)}, u32[]{:S(2)}) collective-permute-start(bf16[64,2048]{1,0:T(8,128)(2,1)S(1)} %get-tuple-element.60), channel_id=1, source_target_pairs={{0,4},{1,3},{4,8},{5,1},{8,12},{9,5},{12,14},{13,9},{14,10},{15,13... | collective-permute-start | bytes 786440 | tf_op jit(solution)/shard_map/ppermute | solution.py:245
  86.0 2.6 %experts.9 = (bf16[64,2048]{1,0:T(8,128)(2,1)S(1)}, bf16[64,2048]{1,0:T(8,128)(2,1)S(1)}) custom-call(s32[2]{0:T(128)S(1)} %pad_add_fusion.at_ref, f32[8,8,128]{2,1,0:T(8,128)S(1)} %get-tuple-element.56.w_ref, bf16[2048,512]{1,0:T(8,128)(2,1)S(1)} %get-tuple-element.45.after_ref.g0, bf16[2048,512]{1,0:T(8,128)(2,1)S(1)} %get-tuple-element.57.u0, ...), custom_call_target="tpu_custom_call" | custom-call | flops 1610612736 | bytes 1048576 | tf_op jit(solution)/shard_map/experts/pallas_call | solution.py:170
  88.5 2.6 %experts.10 = (bf16[64,2048]{1,0:T(8,128)(2,1)S(1)}, bf16[64,2048]{1,0:T(8,128)(2,1)S(1)}) custom-call(s32[2]{0:T(128)S(1)} %pad_add_fusion.at_ref, f32[8,8,128]{2,1,0:T(8,128)S(1)} %get-tuple-element.56.w_ref, bf16[2048,512]{1,0:T(8,128)(2,1)S(1)} %get-tuple-element.45.after_ref.g0, bf16[2048,512]{1,0:T(8,128)(2,1)S(1)} %get-tuple-element.57.u0, ...), custom_call_target="tpu_custom_call" | custom-call | flops 1610612736 | bytes 1048576 | tf_op jit(solution)/shard_map/experts/pallas_call | solution.py:170
  91.1 2.6 %experts.11 = (bf16[64,2048]{1,0:T(8,128)(2,1)S(1)}, bf16[64,2048]{1,0:T(8,128)(2,1)S(1)}) custom-call(s32[2]{0:T(128)S(1)} %pad_add_fusion.at_ref, f32[8,8,128]{2,1,0:T(8,128)S(1)} %get-tuple-element.56.w_ref, bf16[2048,512]{1,0:T(8,128)(2,1)S(1)} %get-tuple-element.45.after_ref.g0, bf16[2048,512]{1,0:T(8,128)(2,1)S(1)} %get-tuple-element.57.u0, ...), custom_call_target="tpu_custom_call" | custom-call | flops 1610612736 | bytes 1048576 | tf_op jit(solution)/shard_map/experts/pallas_call | solution.py:170
  93.7 2.6 %experts.12 = (bf16[64,2048]{1,0:T(8,128)(2,1)S(1)}, bf16[64,2048]{1,0:T(8,128)(2,1)S(1)}) custom-call(s32[2]{0:T(128)S(1)} %pad_add_fusion.at_ref, f32[8,8,128]{2,1,0:T(8,128)S(1)} %get-tuple-element.56.w_ref, bf16[2048,512]{1,0:T(8,128)(2,1)S(1)} %get-tuple-element.45.after_ref.g0, bf16[2048,512]{1,0:T(8,128)(2,1)S(1)} %get-tuple-element.57.u0, ...), custom_call_target="tpu_custom_call" | custom-call | flops 1610612736 | bytes 1048576 | tf_op jit(solution)/shard_map/experts/pallas_call | solution.py:170
  96.3 2.6 %experts.13 = (bf16[64,2048]{1,0:T(8,128)(2,1)S(1)}, bf16[64,2048]{1,0:T(8,128)(2,1)S(1)}) custom-call(s32[2]{0:T(128)S(1)} %pad_add_fusion.at_ref, f32[8,8,128]{2,1,0:T(8,128)S(1)} %get-tuple-element.56.w_ref, bf16[2048,512]{1,0:T(8,128)(2,1)S(1)} %get-tuple-element.45.after_ref.g0, bf16[2048,512]{1,0:T(8,128)(2,1)S(1)} %get-tuple-element.57.u0, ...), custom_call_target="tpu_custom_call" | custom-call | flops 1610612736 | bytes 1048576 | tf_op jit(solution)/shard_map/experts/pallas_call | solution.py:170
  98.8 2.6 %experts.15 = (bf16[64,2048]{1,0:T(8,128)(2,1)S(1)}, bf16[64,2048]{1,0:T(8,128)(2,1)S(1)}) custom-call(s32[2]{0:T(128)S(1)} %pad_add_fusion.at_ref, f32[8,8,128]{2,1,0:T(8,128)S(1)} %get-tuple-element.56.w_ref, bf16[2048,512]{1,0:T(8,128)(2,1)S(1)} %get-tuple-element.45.after_ref.g0, bf16[2048,512]{1,0:T(8,128)(2,1)S(1)} %get-tuple-element.57.u0, ...), custom_call_target="tpu_custom_call" | custom-call | flops 1610612736 | bytes 1048576 | tf_op jit(solution)/shard_map/experts/pallas_call | solution.py:170
  101.5 2.8 %experts.14 = (bf16[64,2048]{1,0:T(8,128)(2,1)S(1)}, bf16[64,2048]{1,0:T(8,128)(2,1)S(1)}) custom-call(s32[2]{0:T(128)S(1)} %pad_add_fusion.at_ref, f32[8,8,128]{2,1,0:T(8,128)S(1)} %get-tuple-element.56.w_ref, bf16[2048,512]{1,0:T(8,128)(2,1)S(1)} %get-tuple-element.45.after_ref.g0, bf16[2048,512]{1,0:T(8,128)(2,1)S(1)} %get-tuple-element.57.u0, ...), custom_call_target="tpu_custom_call" | custom-call | flops 1610612736 | bytes 1048576 | tf_op jit(solution)/shard_map/experts/pallas_call | solution.py:170
  104.4 2.0 %collective-permute-start.15 = (bf16[64,2048]{1,0:T(8,128)(2,1)S(1)}, bf16[64,2048]{1,0:T(8,128)(2,1)S(1)}, u32[]{:S(2)}, u32[]{:S(2)}) collective-permute-start(bf16[64,2048]{1,0:T(8,128)(2,1)S(1)} %add_convert_fusion.13), channel_id=1, source_target_pairs={{0,4},{1,3},{4,8},{5,1},{8,12},{9,5},{12,14},{13,9},{14,10},{15,13... | collective-permute-start | bytes 786440 | tf_op jit(solution)/shard_map/ppermute | solution.py:245
  106.8 4.0 %collective-permute-done.15 = bf16[64,2048]{1,0:T(8,128)(2,1)S(1)} collective-permute-done((bf16[64,2048]{1,0:T(8,128)(2,1)S(1)}, bf16[64,2048]{1,0:T(8,128)(2,1)S(1)}, u32[]{:S(2)}, u32[]{:S(2)}) %collective-permute-start.15) | collective-permute-done | bytes 262176 | tf_op jit(solution)/shard_map/ppermute | solution.py:245
  110.9 2.0 %collective-permute-start.18 = (bf16[64,2048]{1,0:T(8,128)(2,1)S(1)}, bf16[64,2048]{1,0:T(8,128)(2,1)S(1)}, u32[]{:S(2)}, u32[]{:S(2)}) collective-permute-start(bf16[64,2048]{1,0:T(8,128)(2,1)S(1)} %add_convert_fusion.12), channel_id=1, source_target_pairs={{0,4},{1,3},{4,8},{5,1},{8,12},{9,5},{12,14},{13,9},{14,10},{15,13... | collective-permute-start | bytes 786440 | tf_op jit(solution)/shard_map/ppermute | solution.py:245
  113.7 2.0 %collective-permute-start.33 = (bf16[64,2048]{1,0:T(8,128)(2,1)S(1)}, bf16[64,2048]{1,0:T(8,128)(2,1)S(1)}, u32[]{:S(2)}, u32[]{:S(2)}) collective-permute-start(bf16[64,2048]{1,0:T(8,128)(2,1)S(1)} %add_convert_fusion.5), channel_id=1, source_target_pairs={{0,4},{1,3},{4,8},{5,1},{8,12},{9,5},{12,14},{13,9},{14,10},{15,13... | collective-permute-start | bytes 786440 | tf_op jit(solution)/shard_map/ppermute | solution.py:245
  117.4 2.0 %collective-permute-start.21 = (bf16[64,2048]{1,0:T(8,128)(2,1)S(1)}, bf16[64,2048]{1,0:T(8,128)(2,1)S(1)}, u32[]{:S(2)}, u32[]{:S(2)}) collective-permute-start(bf16[64,2048]{1,0:T(8,128)(2,1)S(1)} %add_convert_fusion.11), channel_id=1, source_target_pairs={{0,4},{1,3},{4,8},{5,1},{8,12},{9,5},{12,14},{13,9},{14,10},{15,13... | collective-permute-start | bytes 786440 | tf_op jit(solution)/shard_map/ppermute | solution.py:245
  120.2 2.0 %collective-permute-start.34 = (bf16[64,2048]{1,0:T(8,128)(2,1)S(1)}, bf16[64,2048]{1,0:T(8,128)(2,1)S(1)}, u32[]{:S(2)}, u32[]{:S(2)}) collective-permute-start(bf16[64,2048]{1,0:T(8,128)(2,1)S(1)} %add_convert_fusion.4), channel_id=1, source_target_pairs={{0,4},{1,3},{4,8},{5,1},{8,12},{9,5},{12,14},{13,9},{14,10},{15,13... | collective-permute-start | bytes 786440 | tf_op jit(solution)/shard_map/ppermute | solution.py:245
  123.8 2.0 %collective-permute-start.24 = (bf16[64,2048]{1,0:T(8,128)(2,1)S(1)}, bf16[64,2048]{1,0:T(8,128)(2,1)S(1)}, u32[]{:S(2)}, u32[]{:S(2)}) collective-permute-start(bf16[64,2048]{1,0:T(8,128)(2,1)S(1)} %add_convert_fusion.10), channel_id=1, source_target_pairs={{0,4},{1,3},{4,8},{5,1},{8,12},{9,5},{12,14},{13,9},{14,10},{15,13... | collective-permute-start | bytes 786440 | tf_op jit(solution)/shard_map/ppermute | solution.py:245
  126.7 2.0 %collective-permute-start.35 = (bf16[64,2048]{1,0:T(8,128)(2,1)S(1)}, bf16[64,2048]{1,0:T(8,128)(2,1)S(1)}, u32[]{:S(2)}, u32[]{:S(2)}) collective-permute-start(bf16[64,2048]{1,0:T(8,128)(2,1)S(1)} %add_convert_fusion.3), channel_id=1, source_target_pairs={{0,4},{1,3},{4,8},{5,1},{8,12},{9,5},{12,14},{13,9},{14,10},{15,13... | collective-permute-start | bytes 786440 | tf_op jit(solution)/shard_map/ppermute | solution.py:245
  143.4 2.7 %collective-permute-done.37 = bf16[64,2048]{1,0:T(8,128)(2,1)S(1)} collective-permute-done((bf16[64,2048]{1,0:T(8,128)(2,1)S(1)}, bf16[64,2048]{1,0:T(8,128)(2,1)S(1)}, u32[]{:S(2)}, u32[]{:S(2)}) %collective-permute-start.37) | collective-permute-done | bytes 262176 | tf_op jit(solution)/shard_map/ppermute | solution.py:245
  (77 shorter events, 64.0 us)
Async XLA Ops:
  3.2 9.5 %collective-permute-start = (bf16[528,128]{1,0:T(8,128)(2,1)S(1)}, bf16[528,128]{1,0:T(8,128)(2,1)S(1)}, u32[]{:S(2)}, u32[]{:S(2)}) collective-permute-start(bf16[528,128]{1,0:T(8,128)(2,1)S(1)} %get-tuple-element.46), channel_id=1, source_target_pairs={{0,2},{2,4},{4,6},{6,0},{8,10},{10,12},{12,14},{14,8},{1,3},{3,5},... | collective-permute-start | bytes 405512 | tf_op jit(solution)/shard_map/ppermute | solution.py:251
  6.3 6.5 %collective-permute-start.1 = (bf16[528,128]{1,0:T(8,128)(2,1)S(1)}, bf16[528,128]{1,0:T(8,128)(2,1)S(1)}, u32[]{:S(2)}, u32[]{:S(2)}) collective-permute-start(bf16[528,128]{1,0:T(8,128)(2,1)S(1)} %get-tuple-element.47), channel_id=1, source_target_pairs={{0,4},{2,6},{4,0},{6,2},{8,12},{10,14},{12,8},{14,10},{1,5},{3,7},... | collective-permute-start | bytes 405512 | tf_op jit(solution)/shard_map/ppermute | solution.py:251
  12.2 68.0 %collective-permute-start.7 = (bf16[2048,512]{1,0:T(8,128)(2,1)S(1)}, bf16[2048,512]{1,0:T(8,128)(2,1)S(1)}, u32[]{:S(2)}, u32[]{:S(2)}) collective-permute-start(bf16[2048,512]{1,0:T(8,128)(2,1)S(1)} %get-tuple-element.45.after_ref.g0), channel_id=1, source_target_pairs={{0,1},{1,0},{2,3},{3,2},{4,5},{5,4},{6,7},{7,6},{8,9},{9,8},{10,11... | collective-permute-start | bytes 6291464 | tf_op jit(solution)/shard_map/ppermute | solution.py:286
  12.2 68.0 %collective-permute-start.8 = (bf16[2048,512]{1,0:T(8,128)(2,1)S(1)}, bf16[2048,512]{1,0:T(8,128)(2,1)S(1)}, u32[]{:S(2)}, u32[]{:S(2)}) collective-permute-start(bf16[2048,512]{1,0:T(8,128)(2,1)S(1)} %get-tuple-element.57.u0), channel_id=1, source_target_pairs={{0,1},{1,0},{2,3},{3,2},{4,5},{5,4},{6,7},{7,6},{8,9},{9,8},{10,11... | collective-permute-start | bytes 6291464 | tf_op jit(solution)/shard_map/ppermute | solution.py:286
  12.7 67.5 %collective-permute-start.9 = (bf16[512,2048]{1,0:T(8,128)(2,1)S(1)}, bf16[512,2048]{1,0:T(8,128)(2,1)S(1)}, u32[]{:S(2)}, u32[]{:S(2)}) collective-permute-start(bf16[512,2048]{1,0:T(8,128)(2,1)S(1)} %get-tuple-element.58.d0), channel_id=1, source_target_pairs={{0,1},{1,0},{2,3},{3,2},{4,5},{5,4},{6,7},{7,6},{8,9},{9,8},{10,11... | collective-permute-start | bytes 6291464 | tf_op jit(solution)/shard_map/ppermute | solution.py:286
  13.9 9.4 %collective-permute-start.3 = (bf16[576,128]{1,0:T(8,128)(2,1)S(1)}, bf16[576,128]{1,0:T(8,128)(2,1)S(1)}, u32[]{:S(2)}, u32[]{:S(2)}) collective-permute-start(bf16[576,128]{1,0:T(8,128)(2,1)S(1)} %total.1), channel_id=1, source_target_pairs={{0,8},{2,10},{4,12},{6,14},{8,0},{10,2},{12,4},{14,6},{1,9},{3,11}... | collective-permute-start | bytes 442376 | tf_op jit(solution)/shard_map/ppermute | solution.py:296
  25.3 6.6 %collective-permute-start.5 = (bf16[512,128]{1,0:T(8,128)(2,1)S(1)}, bf16[512,128]{1,0:T(8,128)(2,1)S(1)}, u32[]{:S(2)}, u32[]{:S(2)}) collective-permute-start(bf16[512,128]{1,0:T(8,128)(2,1)S(1)} %get-tuple-element.51), channel_id=1, source_target_pairs={{0,4},{2,6},{4,0},{6,2},{8,12},{10,14},{12,8},{14,10},{1,5},{3,7},... | collective-permute-start | bytes 393224 | tf_op jit(solution)/shard_map/ppermute | solution.py:251
  37.6 6.4 %collective-permute-start.11 = (bf16[64,2048]{1,0:T(8,128)(2,1)S(1)}, bf16[64,2048]{1,0:T(8,128)(2,1)S(1)}, u32[]{:S(2)}, u32[]{:S(2)}) collective-permute-start(bf16[64,2048]{1,0:T(8,128)(2,1)S(1)} %get-tuple-element.59.refs_1_), channel_id=1, source_target_pairs={{0,4},{1,3},{4,8},{5,1},{8,12},{9,5},{12,14},{13,9},{14,10},{15,13... | collective-permute-start | bytes 786440 | tf_op jit(solution)/shard_map/ppermute | solution.py:245
  38.7 8.2 %collective-permute-start.10 = (bf16[64,2048]{1,0:T(8,128)(2,1)S(1)}, bf16[64,2048]{1,0:T(8,128)(2,1)S(1)}, u32[]{:S(2)}, u32[]{:S(2)}) collective-permute-start(bf16[64,2048]{1,0:T(8,128)(2,1)S(1)} %get-tuple-element.54.after_ref.refs_0_), channel_id=1, source_target_pairs={{0,4},{1,3},{4,8},{5,1},{8,12},{9,5},{12,14},{13,9},{14,10},{15,13... | collective-permute-start | bytes 786440 | tf_op jit(solution)/shard_map/ppermute | solution.py:245
  44.1 6.4 %collective-permute-start.14 = (bf16[64,2048]{1,0:T(8,128)(2,1)S(1)}, bf16[64,2048]{1,0:T(8,128)(2,1)S(1)}, u32[]{:S(2)}, u32[]{:S(2)}) collective-permute-start(bf16[64,2048]{1,0:T(8,128)(2,1)S(1)} %collective-permute-done.11.refs_1_), channel_id=1, source_target_pairs={{0,4},{1,3},{4,8},{5,1},{8,12},{9,5},{12,14},{13,9},{14,10},{15,13... | collective-permute-start | bytes 786440 | tf_op jit(solution)/shard_map/ppermute | solution.py:245
  46.9 6.4 %collective-permute-start.13 = (bf16[64,2048]{1,0:T(8,128)(2,1)S(1)}, bf16[64,2048]{1,0:T(8,128)(2,1)S(1)}, u32[]{:S(2)}, u32[]{:S(2)}) collective-permute-start(bf16[64,2048]{1,0:T(8,128)(2,1)S(1)} %collective-permute-done.10.refs_0_), channel_id=1, source_target_pairs={{0,4},{1,3},{4,8},{5,1},{8,12},{9,5},{12,14},{13,9},{14,10},{15,13... | collective-permute-start | bytes 786440 | tf_op jit(solution)/shard_map/ppermute | solution.py:245
  50.4 6.4 %collective-permute-start.17 = (bf16[64,2048]{1,0:T(8,128)(2,1)S(1)}, bf16[64,2048]{1,0:T(8,128)(2,1)S(1)}, u32[]{:S(2)}, u32[]{:S(2)}) collective-permute-start(bf16[64,2048]{1,0:T(8,128)(2,1)S(1)} %collective-permute-done.14.refs_1_), channel_id=1, source_target_pairs={{0,4},{1,3},{4,8},{5,1},{8,12},{9,5},{12,14},{13,9},{14,10},{15,13... | collective-permute-start | bytes 786440 | tf_op jit(solution)/shard_map/ppermute | solution.py:245
  53.2 6.4 %collective-permute-start.16 = (bf16[64,2048]{1,0:T(8,128)(2,1)S(1)}, bf16[64,2048]{1,0:T(8,128)(2,1)S(1)}, u32[]{:S(2)}, u32[]{:S(2)}) collective-permute-start(bf16[64,2048]{1,0:T(8,128)(2,1)S(1)} %collective-permute-done.13.refs_0_), channel_id=1, source_target_pairs={{0,4},{1,3},{4,8},{5,1},{8,12},{9,5},{12,14},{13,9},{14,10},{15,13... | collective-permute-start | bytes 786440 | tf_op jit(solution)/shard_map/ppermute | solution.py:245
  56.8 6.4 %collective-permute-start.20 = (bf16[64,2048]{1,0:T(8,128)(2,1)S(1)}, bf16[64,2048]{1,0:T(8,128)(2,1)S(1)}, u32[]{:S(2)}, u32[]{:S(2)}) collective-permute-start(bf16[64,2048]{1,0:T(8,128)(2,1)S(1)} %collective-permute-done.17.refs_1_), channel_id=1, source_target_pairs={{0,4},{1,3},{4,8},{5,1},{8,12},{9,5},{12,14},{13,9},{14,10},{15,13... | collective-permute-start | bytes 786440 | tf_op jit(solution)/shard_map/ppermute | solution.py:245
  59.6 6.4 %collective-permute-start.19 = (bf16[64,2048]{1,0:T(8,128)(2,1)S(1)}, bf16[64,2048]{1,0:T(8,128)(2,1)S(1)}, u32[]{:S(2)}, u32[]{:S(2)}) collective-permute-start(bf16[64,2048]{1,0:T(8,128)(2,1)S(1)} %collective-permute-done.16.refs_0_), channel_id=1, source_target_pairs={{0,4},{1,3},{4,8},{5,1},{8,12},{9,5},{12,14},{13,9},{14,10},{15,13... | collective-permute-start | bytes 786440 | tf_op jit(solution)/shard_map/ppermute | solution.py:245
  66.0 6.4 %collective-permute-start.22 = (bf16[64,2048]{1,0:T(8,128)(2,1)S(1)}, bf16[64,2048]{1,0:T(8,128)(2,1)S(1)}, u32[]{:S(2)}, u32[]{:S(2)}) collective-permute-start(bf16[64,2048]{1,0:T(8,128)(2,1)S(1)} %collective-permute-done.19.refs_0_), channel_id=1, source_target_pairs={{0,4},{1,3},{4,8},{5,1},{8,12},{9,5},{12,14},{13,9},{14,10},{15,13... | collective-permute-start | bytes 786440 | tf_op jit(solution)/shard_map/ppermute | solution.py:245
  75.9 25.5 %collective-permute-start.29 = (bf16[64,2048]{1,0:T(8,128)(2,1)S(1)}, bf16[64,2048]{1,0:T(8,128)(2,1)S(1)}, u32[]{:S(2)}, u32[]{:S(2)}) collective-permute-start(bf16[64,2048]{1,0:T(8,128)(2,1)S(1)} %collective-permute-done.26.refs_1_), channel_id=1, source_target_pairs={{0,4},{1,3},{4,8},{5,1},{8,12},{9,5},{12,14},{13,9},{14,10},{15,13... | collective-permute-start | bytes 786440 | tf_op jit(solution)/shard_map/ppermute | solution.py:245
  78.7 22.7 %collective-permute-start.28 = (bf16[64,2048]{1,0:T(8,128)(2,1)S(1)}, bf16[64,2048]{1,0:T(8,128)(2,1)S(1)}, u32[]{:S(2)}, u32[]{:S(2)}) collective-permute-start(bf16[64,2048]{1,0:T(8,128)(2,1)S(1)} %collective-permute-done.25.refs_0_), channel_id=1, source_target_pairs={{0,4},{1,3},{4,8},{5,1},{8,12},{9,5},{12,14},{13,9},{14,10},{15,13... | collective-permute-start | bytes 786440 | tf_op jit(solution)/shard_map/ppermute | solution.py:245
  82.8 21.5 %collective-permute-start.12 = (bf16[64,2048]{1,0:T(8,128)(2,1)S(1)}, bf16[64,2048]{1,0:T(8,128)(2,1)S(1)}, u32[]{:S(2)}, u32[]{:S(2)}) collective-permute-start(bf16[64,2048]{1,0:T(8,128)(2,1)S(1)} %get-tuple-element.60), channel_id=1, source_target_pairs={{0,4},{1,3},{4,8},{5,1},{8,12},{9,5},{12,14},{13,9},{14,10},{15,13... | collective-permute-start | bytes 786440 | tf_op jit(solution)/shard_map/ppermute | solution.py:245
  85.3 21.1 %collective-permute-start.31 = (bf16[64,2048]{1,0:T(8,128)(2,1)S(1)}, bf16[64,2048]{1,0:T(8,128)(2,1)S(1)}, u32[]{:S(2)}, u32[]{:S(2)}) collective-permute-start(bf16[64,2048]{1,0:T(8,128)(2,1)S(1)} %get-tuple-element.68), channel_id=1, source_target_pairs={{0,4},{1,3},{4,8},{5,1},{8,12},{9,5},{12,14},{13,9},{14,10},{15,13... | collective-permute-start | bytes 786440 | tf_op jit(solution)/shard_map/ppermute | solution.py:245
  104.4 6.4 %collective-permute-start.15 = (bf16[64,2048]{1,0:T(8,128)(2,1)S(1)}, bf16[64,2048]{1,0:T(8,128)(2,1)S(1)}, u32[]{:S(2)}, u32[]{:S(2)}) collective-permute-start(bf16[64,2048]{1,0:T(8,128)(2,1)S(1)} %add_convert_fusion.13), channel_id=1, source_target_pairs={{0,4},{1,3},{4,8},{5,1},{8,12},{9,5},{12,14},{13,9},{14,10},{15,13... | collective-permute-start | bytes 786440 | tf_op jit(solution)/shard_map/ppermute | solution.py:245
  106.4 7.2 %collective-permute-start.32 = (bf16[64,2048]{1,0:T(8,128)(2,1)S(1)}, bf16[64,2048]{1,0:T(8,128)(2,1)S(1)}, u32[]{:S(2)}, u32[]{:S(2)}) collective-permute-start(bf16[64,2048]{1,0:T(8,128)(2,1)S(1)} %add_convert_fusion.6), channel_id=1, source_target_pairs={{0,4},{1,3},{4,8},{5,1},{8,12},{9,5},{12,14},{13,9},{14,10},{15,13... | collective-permute-start | bytes 786440 | tf_op jit(solution)/shard_map/ppermute | solution.py:245
  110.9 6.4 %collective-permute-start.18 = (bf16[64,2048]{1,0:T(8,128)(2,1)S(1)}, bf16[64,2048]{1,0:T(8,128)(2,1)S(1)}, u32[]{:S(2)}, u32[]{:S(2)}) collective-permute-start(bf16[64,2048]{1,0:T(8,128)(2,1)S(1)} %add_convert_fusion.12), channel_id=1, source_target_pairs={{0,4},{1,3},{4,8},{5,1},{8,12},{9,5},{12,14},{13,9},{14,10},{15,13... | collective-permute-start | bytes 786440 | tf_op jit(solution)/shard_map/ppermute | solution.py:245
  113.7 6.4 %collective-permute-start.33 = (bf16[64,2048]{1,0:T(8,128)(2,1)S(1)}, bf16[64,2048]{1,0:T(8,128)(2,1)S(1)}, u32[]{:S(2)}, u32[]{:S(2)}) collective-permute-start(bf16[64,2048]{1,0:T(8,128)(2,1)S(1)} %add_convert_fusion.5), channel_id=1, source_target_pairs={{0,4},{1,3},{4,8},{5,1},{8,12},{9,5},{12,14},{13,9},{14,10},{15,13... | collective-permute-start | bytes 786440 | tf_op jit(solution)/shard_map/ppermute | solution.py:245
  117.4 6.4 %collective-permute-start.21 = (bf16[64,2048]{1,0:T(8,128)(2,1)S(1)}, bf16[64,2048]{1,0:T(8,128)(2,1)S(1)}, u32[]{:S(2)}, u32[]{:S(2)}) collective-permute-start(bf16[64,2048]{1,0:T(8,128)(2,1)S(1)} %add_convert_fusion.11), channel_id=1, source_target_pairs={{0,4},{1,3},{4,8},{5,1},{8,12},{9,5},{12,14},{13,9},{14,10},{15,13... | collective-permute-start | bytes 786440 | tf_op jit(solution)/shard_map/ppermute | solution.py:245
  120.2 6.4 %collective-permute-start.34 = (bf16[64,2048]{1,0:T(8,128)(2,1)S(1)}, bf16[64,2048]{1,0:T(8,128)(2,1)S(1)}, u32[]{:S(2)}, u32[]{:S(2)}) collective-permute-start(bf16[64,2048]{1,0:T(8,128)(2,1)S(1)} %add_convert_fusion.4), channel_id=1, source_target_pairs={{0,4},{1,3},{4,8},{5,1},{8,12},{9,5},{12,14},{13,9},{14,10},{15,13... | collective-permute-start | bytes 786440 | tf_op jit(solution)/shard_map/ppermute | solution.py:245
  123.8 6.4 %collective-permute-start.24 = (bf16[64,2048]{1,0:T(8,128)(2,1)S(1)}, bf16[64,2048]{1,0:T(8,128)(2,1)S(1)}, u32[]{:S(2)}, u32[]{:S(2)}) collective-permute-start(bf16[64,2048]{1,0:T(8,128)(2,1)S(1)} %add_convert_fusion.10), channel_id=1, source_target_pairs={{0,4},{1,3},{4,8},{5,1},{8,12},{9,5},{12,14},{13,9},{14,10},{15,13... | collective-permute-start | bytes 786440 | tf_op jit(solution)/shard_map/ppermute | solution.py:245
  126.7 6.4 %collective-permute-start.35 = (bf16[64,2048]{1,0:T(8,128)(2,1)S(1)}, bf16[64,2048]{1,0:T(8,128)(2,1)S(1)}, u32[]{:S(2)}, u32[]{:S(2)}) collective-permute-start(bf16[64,2048]{1,0:T(8,128)(2,1)S(1)} %add_convert_fusion.3), channel_id=1, source_target_pairs={{0,4},{1,3},{4,8},{5,1},{8,12},{9,5},{12,14},{13,9},{14,10},{15,13... | collective-permute-start | bytes 786440 | tf_op jit(solution)/shard_map/ppermute | solution.py:245
  130.3 6.4 %collective-permute-start.27 = (bf16[64,2048]{1,0:T(8,128)(2,1)S(1)}, bf16[64,2048]{1,0:T(8,128)(2,1)S(1)}, u32[]{:S(2)}, u32[]{:S(2)}) collective-permute-start(bf16[64,2048]{1,0:T(8,128)(2,1)S(1)} %add_convert_fusion.9), channel_id=1, source_target_pairs={{0,4},{1,3},{4,8},{5,1},{8,12},{9,5},{12,14},{13,9},{14,10},{15,13... | collective-permute-start | bytes 786440 | tf_op jit(solution)/shard_map/ppermute | solution.py:245
  133.2 6.4 %collective-permute-start.36 = (bf16[64,2048]{1,0:T(8,128)(2,1)S(1)}, bf16[64,2048]{1,0:T(8,128)(2,1)S(1)}, u32[]{:S(2)}, u32[]{:S(2)}) collective-permute-start(bf16[64,2048]{1,0:T(8,128)(2,1)S(1)} %add_convert_fusion.2), channel_id=1, source_target_pairs={{0,4},{1,3},{4,8},{5,1},{8,12},{9,5},{12,14},{13,9},{14,10},{15,13... | collective-permute-start | bytes 786440 | tf_op jit(solution)/shard_map/ppermute | solution.py:245
  136.8 6.4 %collective-permute-start.30 = (bf16[64,2048]{1,0:T(8,128)(2,1)S(1)}, bf16[64,2048]{1,0:T(8,128)(2,1)S(1)}, u32[]{:S(2)}, u32[]{:S(2)}) collective-permute-start(bf16[64,2048]{1,0:T(8,128)(2,1)S(1)} %add_convert_fusion.8), channel_id=1, source_target_pairs={{0,4},{1,3},{4,8},{5,1},{8,12},{9,5},{12,14},{13,9},{14,10},{15,13... | collective-permute-start | bytes 786440 | tf_op jit(solution)/shard_map/ppermute | solution.py:245
  139.6 6.4 %collective-permute-start.37 = (bf16[64,2048]{1,0:T(8,128)(2,1)S(1)}, bf16[64,2048]{1,0:T(8,128)(2,1)S(1)}, u32[]{:S(2)}, u32[]{:S(2)}) collective-permute-start(bf16[64,2048]{1,0:T(8,128)(2,1)S(1)} %add_convert_fusion.1), channel_id=1, source_target_pairs={{0,4},{1,3},{4,8},{5,1},{8,12},{9,5},{12,14},{13,9},{14,10},{15,13... | collective-permute-start | bytes 786440 | tf_op jit(solution)/shard_map/ppermute | solution.py:245
  (6 other events, 36.4 us)

commit v2 on v1

--- a/solution.py
+++ b/solution.py
@@ -12,6 +12,7 @@
 PAD = 16
 CHUNKS = 4
 PIECES = 2
+STRIP = 32
 
 epsilon = 1e-06
 f32 = jnp.float32
@@ -21,7 +22,6 @@
 VMEM = pl.BlockSpec(memory_space=pltpu.VMEM)
 ANY = pl.BlockSpec(memory_space=pl.ANY)
 HBM = pl.BlockSpec(memory_space=pltpu.HBM)
-SMEM = pl.BlockSpec(memory_space=pltpu.SMEM)
 SMALL = pltpu.CompilerParams(vmem_limit_bytes=16 << 20)
 
 
@@ -29,7 +29,7 @@
     return lax.dot_general(a, b, (dims, ((), ())), preferred_element_type=f32)
 
 
-def state_kernel(half, at_ref, ids_hbm, rw_hbm, k_hbm, v_hbm, *refs):
+def state_kernel(half, ids_hbm, rw_hbm, k_hbm, v_hbm, *refs):
     sends, (state_ref, ids_ref, rw_ref, k_ref, v_ref, sems) = refs[:half], refs[half:]
     width = k_ref.shape[1]
     part = width // half
@@ -41,17 +41,11 @@
             copies.append(pltpu.make_async_copy(src.at[:, cols], dst.at[:, cols], sems.at[2 * c + i]))
     copies.append(pltpu.make_async_copy(ids_hbm, ids_ref, sems.at[2 * CHUNKS]))
     copies.append(pltpu.make_async_copy(rw_hbm, rw_ref, sems.at[2 * CHUNKS + 1]))
-    for copy in copies:
+    for copy in copies[-2:] + copies[:-2]:
         copy.start()
-    for c in range(CHUNKS):
-        copies[2 * c].wait()
-        copies[2 * c + 1].wait()
-        for h in range(c * chunk // HEAD_DIM, (c + 1) * chunk // HEAD_DIM):
-            cols = slice(h * HEAD_DIM, (h + 1) * HEAD_DIM)
-            state_ref[cols, :] = dot(k_ref[:, cols], v_ref[:, cols], ((0,), (0,))).astype(bf16)
     copies[-2].wait()
     copies[-1].wait()
-    group, place, core = lax.div(at_ref[0], half), lax.rem(at_ref[0], half), at_ref[1]
+    group, place, core = lax.div(lax.axis_index("seq"), half), lax.rem(lax.axis_index("seq"), half), lax.axis_index("expert")
     ids = ids_ref[...]
     shares = rw_ref[...] / jnp.sum(rw_ref[...], axis=0, keepdims=True)
     zero = jnp.zeros((PAD - 8, ids.shape[1]), f32)
@@ -61,7 +55,6 @@
 
     for r, send_ref in enumerate(sends):
         to = lax.rem(place + r, half)
-        send_ref[:part, :] = state_ref[pl.ds(pl.multiple_of(to * part, part), part), :]
         rows = []
         for side in (group, 1 - group):
             first = 2 * (side * half + to)
@@ -69,6 +62,15 @@
             high = both.astype(bf16).astype(f32)
             rows += [high, both - high]
         send_ref[part:, :] = jnp.concatenate(rows + [zero], axis=0).astype(bf16)
+    for c in range(CHUNKS):
+        copies[2 * c].wait()
+        copies[2 * c + 1].wait()
+        for h in range(c * chunk // HEAD_DIM, (c + 1) * chunk // HEAD_DIM):
+            cols = slice(h * HEAD_DIM, (h + 1) * HEAD_DIM)
+            state_ref[cols, :] = dot(k_ref[:, cols], v_ref[:, cols], ((0,), (0,))).astype(bf16)
+    for r, send_ref in enumerate(sends):
+        to = lax.rem(place + r, half)
+        send_ref[:part, :] = state_ref[pl.ds(pl.multiple_of(to * part, part), part), :]
 
 
 def total_kernel(half, after_ref, *refs):
@@ -79,28 +81,39 @@
     for r in range(1, half):
         total = total + gots[r][:part, :].astype(f32)
     send_ref[:part, :] = total.astype(bf16)
+    terms = [got_ref[part:, :].astype(f32)[4:8] for got_ref in gots]
+    send_ref[part:, :] = jnp.concatenate(terms, axis=0).astype(bf16)
+
+
+def prefix_kernel(half, after_ref, far_ref, *refs):
+    del after_ref
+    gots, backs = refs[:half], refs[half:]
+    part = backs[0].shape[0]
+    group, place = lax.div(lax.axis_index("seq"), half), lax.rem(lax.axis_index("seq"), half)
+    for row in range(0, part, STRIP):
+        strip = slice(row, row + STRIP)
+        states = [got_ref[strip, :].astype(f32) for got_ref in gots]
+        before = jnp.where(group == 1, far_ref[strip, :].astype(f32), 0.0)
+        total = before
+        for r in range(half):
+            total = total + jnp.where(r <= place, states[r], 0.0)
+        for r in reversed(range(half)):
+            total = jnp.where(r == place, before, total)
+            backs[r][strip, :] = total.astype(bf16)
+            total = total + states[r]
+
+
+def shares_kernel(half, far_ref, *refs):
+    gots, shares_ref = refs[:half], refs[half]
+    part = gots[0].shape[0] - PAD
+    group, place = lax.div(lax.axis_index("seq"), half), lax.rem(lax.axis_index("seq"), half)
+    far = far_ref[part:, :].astype(f32)
     for r in range(half):
-        send_ref[part + r * PAD : part + (r + 1) * PAD, :] = gots[r][part:, :]
-
-
-def prefix_kernel(half, at_ref, after_ref, far_ref, *refs):
-    del after_ref
-    gots, backs, shares_ref = refs[:half], refs[half:-1], refs[-1]
-    part = backs[0].shape[0]
-    group, place = lax.div(at_ref[0], half), lax.rem(at_ref[0], half)
-    before = jnp.where(group == 1, far_ref[:part, :].astype(f32), 0.0)
-    total = before
-    for r in range(half):
-        total = total + jnp.where(r <= place, gots[r][:part, :].astype(f32), 0.0)
-    for r in reversed(range(half)):
-        total = jnp.where(r == place, before, total)
-        backs[r][...] = total.astype(bf16)
-        total = total + gots[r][:part, :].astype(f32)
         source = lax.rem(place + half - r, half)
         terms = gots[r][part:, :].astype(f32)
-        shares_ref[group * half + source] = terms[0:8] + terms[2:10]
-        terms = far_ref[part + r * PAD : part + (r + 1) * PAD, :].astype(f32)
-        shares_ref[(1 - group) * half + source] = terms[4:12] + terms[6:14]
+        shares_ref[group * half + source, 0:2, :] = terms[0:2] + terms[2:4]
+        terms = far[4 * r : 4 * r + 4]
+        shares_ref[(1 - group) * half + source, 0:2, :] = terms[0:2] + terms[2:4]
 
 
 def local_kernel(q_ref, k_ref, v_ref, within_ref):
@@ -117,33 +130,32 @@
         within_ref[:, cols] = dot(high, v) + dot(low, v)
 
 
-def attention_kernel(half, first, at_ref, after_ref, q_ref, within_ref, hg_ref, fg_ref, *refs):
+def attention_kernel(half, first, after_ref, q_ref, within_ref, hg_ref, fg_ref, *refs):
     del after_ref
-    carried, (att_ref, normed_ref, p_ref) = refs[:half], refs[half:]
+    carried, (att_ref, normed_ref) = refs[:half], refs[half:]
     rows, width = att_ref.shape
     take = slice(first, first + rows)
     part = width // half
+    feature_sq = jnp.zeros((rows, HEAD_DIM), f32)
     for r in range(half):
-        s = lax.rem(lax.rem(at_ref[0], half) + r, half)
-        p_ref[pl.ds(pl.multiple_of(s * part, part), part), :] = carried[r][...]
-    feature_sq = jnp.zeros((rows, HEAD_DIM), f32)
-    for h in range(width // HEAD_DIM):
-        cols = slice(h * HEAD_DIM, (h + 1) * HEAD_DIM)
-        raw = within_ref[take, cols] + dot(q_ref[take, cols], p_ref[cols, :])
-        mean_square = jnp.mean(raw * raw, axis=-1, keepdims=True)
-        att = (raw * lax.rsqrt(mean_square + epsilon) * hg_ref[:, cols]).astype(bf16)
-        att_ref[:, cols] = att
-        att = att.astype(f32)
-        feature_sq = feature_sq + att * att
+        part_of = lax.rem(lax.rem(lax.axis_index("seq"), half) + r, half)
+        for h in range(0, part, HEAD_DIM):
+            cols = pl.ds(pl.multiple_of(part_of * part + h, HEAD_DIM), HEAD_DIM)
+            raw = within_ref[take, cols] + dot(q_ref[take, cols], carried[r][h : h + HEAD_DIM, :])
+            mean_square = jnp.mean(raw * raw, axis=-1, keepdims=True)
+            att = (raw * lax.rsqrt(mean_square + epsilon) * hg_ref[:, cols]).astype(bf16)
+            att_ref[:, cols] = att
+            att = att.astype(f32)
+            feature_sq = feature_sq + att * att
     scale = lax.rsqrt(jnp.sum(feature_sq, axis=-1, keepdims=True) / width + epsilon)
     for h in range(width // HEAD_DIM):
         cols = slice(h * HEAD_DIM, (h + 1) * HEAD_DIM)
         normed_ref[:, cols] = (att_ref[:, cols].astype(f32) * scale * fg_ref[:, cols]).astype(bf16)
 
 
-def expert_kernel(hop, at_ref, w_ref, g0, u0, d0, g1, u1, d1, *refs):
+def expert_kernel(hop, w_ref, g0, u0, d0, g1, u1, d1, *refs):
     n_seq = w_ref.shape[0]
-    seq, core = at_ref[0], at_ref[1]
+    seq, core = lax.axis_index("seq"), lax.axis_index("expert")
     last = n_seq - 1
     place = jnp.where(seq % 2 == 0, seq // 2, last - seq // 2)
     place = lax.rem(place + jnp.where(core == 0, n_seq - hop, hop), n_seq)
@@ -163,13 +175,13 @@
         out_ref[...] = total[i * rows : (i + 1) * rows].astype(bf16)
 
 
-def run_experts(hop, at, pieces, shares, weights):
+def run_experts(hop, pieces, shares, weights):
     rows, width = pieces[0].shape
     hidden = weights[0].shape[1]
     count = len(pieces)
     return pl.pallas_call(
         functools.partial(expert_kernel, hop),
-        in_specs=[SMEM] + [VMEM] * (7 + count),
+        in_specs=[VMEM] * (7 + count),
         out_specs=[VMEM] * count,
         out_shape=[jax.ShapeDtypeStruct((rows, width), bf16)] * count,
         compiler_params=pltpu.CompilerParams(vmem_limit_bytes=24 << 20),
@@ -179,7 +191,7 @@
             transcendentals=2 * count * rows * hidden,
         ),
         name="experts",
-    )(at, shares, *weights, *pieces)
+    )(shares, *weights, *pieces)
 
 
 def in_hbm(*arrays):
@@ -233,7 +245,6 @@
     q, k, v = queries[0], key_rows[0], value_rows[0]
     own = (w_gate[0], w_up[0], w_down[0])
     half = n_seq // 2
-    at = jnp.stack([lax.axis_index("seq"), lax.axis_index("expert")])
 
     ring = ring_of(n_seq)
     hops = []
@@ -254,7 +265,7 @@
     part = width // half
     sends = pl.pallas_call(
         functools.partial(state_kernel, half),
-        in_specs=[SMEM] + [HBM] * 4,
+        in_specs=[HBM] * 4,
         out_specs=[VMEM] * half,
         scratch_shapes=[
             pltpu.VMEM((width, HEAD_DIM), bf16),
@@ -267,7 +278,7 @@
         compiler_params=SMALL,
         out_shape=[jax.ShapeDtypeStruct((part + PAD, HEAD_DIM), bf16)] * half,
         name="states",
-    )(at, *in_hbm(expert_ids[0].T, router_weight[0].T, k, v))
+    )(*in_hbm(expert_ids[0].T, router_weight[0].T, k, v))
     q, k, v, head_gain, ffn_gain = load(
         sends[0], q, k, v, head_gain.reshape(1, width), ffn_gain.reshape(1, width)
     )
@@ -290,28 +301,34 @@
         in_specs=[ANY] + [VMEM] * half,
         out_specs=VMEM,
         compiler_params=SMALL,
-        out_shape=jax.ShapeDtypeStruct((part + PAD * half, HEAD_DIM), bf16),
+        out_shape=jax.ShapeDtypeStruct((part + 4 * half, HEAD_DIM), bf16),
         name="total",
     )(own[0], *gots)
     far = lax.ppermute(near, "seq", [(s, (s + half) % n_seq) for s in range(n_seq)])
-    *backs, shares = pl.pallas_call(
+    backs = pl.pallas_call(
         functools.partial(prefix_kernel, half),
-        in_specs=[SMEM, ANY] + [VMEM] * (half + 1),
-        out_specs=[VMEM] * (half + 1),
-        compiler_params=SMALL,
-        out_shape=[jax.ShapeDtypeStruct((part, HEAD_DIM), bf16)] * half
-        + [jax.ShapeDtypeStruct((n_seq, 8, rows), f32)],
+        in_specs=[ANY] + [VMEM] * (half + 1),
+        out_specs=[VMEM] * half,
+        compiler_params=SMALL,
+        out_shape=[jax.ShapeDtypeStruct((part, HEAD_DIM), bf16)] * half,
         name="prefix",
-    )(at, within, far, *gots)
+    )(within, far, *gots)
+    shares = pl.pallas_call(
+        functools.partial(shares_kernel, half),
+        in_specs=[VMEM] * (half + 1),
+        out_specs=VMEM,
+        compiler_params=SMALL,
+        out_shape=jax.ShapeDtypeStruct((n_seq, 8, rows), f32),
+        name="shares",
+    )(far, *gots)
     carried = along(backs, -1)
     piece = rows // PIECES
     attention, normed = [], []
     for i in range(PIECES):
         att_piece, normed_piece = pl.pallas_call(
             functools.partial(attention_kernel, half, i * piece),
-            in_specs=[SMEM, ANY] + [VMEM] * (half + 4),
+            in_specs=[ANY] + [VMEM] * (half + 4),
             out_specs=[VMEM] * 2,
-            scratch_shapes=[pltpu.VMEM((width, HEAD_DIM), bf16)],
             compiler_params=SMALL,
             cost_estimate=pl.CostEstimate(
                 flops=2 * piece * width * HEAD_DIM,
@@ -320,7 +337,7 @@
             ),
             out_shape=[jax.ShapeDtypeStruct((piece, width), bf16)] * 2,
             name="attend",
-        )(at, normed[-1] if normed else within, q, within, head_gain, ffn_gain, *carried)
+        )(normed[-1] if normed else within, q, within, head_gain, ffn_gain, *carried)
         attention.append(att_piece)
         normed.append(normed_piece)
     weights = [*own, *other]
@@ -328,7 +345,7 @@
     held, partial, first = normed, None, None
     for step in range(n_seq):
         following = [hop(x) for x in held] if step < n_seq - 1 else held
-        result = run_experts(step, at, held, shares, weights)
+        result = run_experts(step, held, shares, weights)
         if step == 0:
             first = result
         elif step == 1:

time: 147 us -> 140 us (0.952)
  Pallas kernels: 31.6 us -> 24.7 us
    pallas_call x10 -> x11, Pallas kernels: 24.1 us -> 18.4 us  [the longest x8 16.2 us: run_experts(): pl.pallas_call(functools.partial(expert_kernel, hop), in_specs=[VMEM] * (...]
  transfers between devices with their start and end apart: 38 -> 38, of which waited for: 28 -> 28; matrix products, arithmetic and copies ran while one was open for 1% -> 1% of each run, Pallas kernels for 20% -> 16%
where the time goes in v2:
time: 140 us; the launch traced here: 139 us
  starting transfers between devices  60.7 us (43%)
  waiting for transfers between devices  50.5 us (36%)
  Pallas kernels  24.7 us (18%)
  other arithmetic  2.66 us (2%)
    ppermute x28, starting transfers between devices, hop(): return lax.ppermute(value, ('seq', 'expert'), hops)  46.4 us
    ppermute x28, waiting for transfers between devices, hop(): return lax.ppermute(value, ('seq', 'expert'), hops)  39.3 us
    pallas_call x8, Pallas kernels, run_experts(): pl.pallas_call(functools.partial(expert_kernel, hop), in_specs=[VMEM] * (...  16.2 us
    ppermute x6, starting transfers between devices, along(): moved.append(lax.ppermute(blocks[r], 'seq', pairs))  10.8 us
    ppermute x6, waiting for transfers between devices, along(): moved.append(lax.ppermute(blocks[r], 'seq', pairs))  7.36 us
    pallas_call x2, Pallas kernels, load(): pl.pallas_call(functools.partial(load_kernel, count), in_specs=[HBM] * (c...  4.29 us
    ppermute x1, waiting for transfers between devices, per_device(): lax.ppermute(near, 'seq', [(s, (s + half) % n_seq) for s in range(n_seq)])  3.82 us
  transfers between devices with their start and end apart: 38, of which 28 were waited for; matrix products, arithmetic and copies ran while one was open for 1% of the time, Pallas kernels for 16%

profile of v2, /device:TPU:0, one launch (start us, length us, event | category | flops | bytes accessed | tf_op | source)
XLA Modules:
  0.0 139.5 jit_solution(3857376655685970306)
XLA Ops:
  0.6 2.0 %states.1 = (bf16[528,128]{1,0:T(8,128)(2,1)S(1)}, bf16[528,128]{1,0:T(8,128)(2,1)S(1)}, bf16[528,128]{1,0:T(8,128)(2,1)S(1)}, bf16[528,128]{1,0:T(8,128)(2,1)S(1)}) custom-call(s32[8,128]{1,0:T(8,128)} %bitcast.28, f32[8,128]{1,0:T(8,128)} %bitcast.29, bf16[128,2048]{1,0:T(8,128)(2,1)} %bitcast.18, bf16[128,2048]{1,0:T(8,128)(2,1)} %bitcast.20), custom_call_target="tpu_custom_call" | custom-call | tf_op jit(solution)/shard_map/states/pallas_call | solution.py:266
  2.6 3.0 %collective-permute-start = (bf16[528,128]{1,0:T(8,128)(2,1)S(1)}, bf16[528,128]{1,0:T(8,128)(2,1)S(1)}, u32[]{:S(2)}, u32[]{:S(2)}) collective-permute-start(bf16[528,128]{1,0:T(8,128)(2,1)S(1)} %get-tuple-element.45), channel_id=1, source_target_pairs={{0,2},{2,4},{4,6},{6,0},{8,10},{10,12},{12,14},{14,8},{1,3},{3,5},... | collective-permute-start | bytes 405512 | tf_op jit(solution)/shard_map/ppermute | solution.py:262
  8.7 2.9 %load.3 = (bf16[2048,512]{1,0:T(8,128)(2,1)S(1)}, bf16[2048,512]{1,0:T(8,128)(2,1)S(1)}, bf16[512,2048]{1,0:T(8,128)(2,1)S(1)}) custom-call(bf16[528,128]{1,0:T(8,128)(2,1)S(1)} %get-tuple-element.38.after_ref.refs_0_, bf16[2048,512]{1,0:T(8,128)(2,1)} %bitcast.22, bf16[2048,512]{1,0:T(8,128)(2,1)} %bitcast.23, bf16[512,2048]{1,0:T(8,128)(2,1)} %bitcast.24), custom_call_target="tpu_custom_call" | custom-call | bytes 6291456 | tf_op jit(solution)/shard_map/load/pallas_call | solution.py:215
  13.3 2.8 %collective-permute-start.3 = (bf16[528,128]{1,0:T(8,128)(2,1)S(1)}, bf16[528,128]{1,0:T(8,128)(2,1)S(1)}, u32[]{:S(2)}, u32[]{:S(2)}) collective-permute-start(bf16[528,128]{1,0:T(8,128)(2,1)S(1)} %total.1), channel_id=1, source_target_pairs={{0,8},{2,10},{4,12},{6,14},{8,0},{10,2},{12,4},{14,6},{1,9},{3,11}... | collective-permute-start | bytes 405512 | tf_op jit(solution)/shard_map/ppermute | solution.py:307
  18.3 3.8 %collective-permute-done.3.far_ref = bf16[528,128]{1,0:T(8,128)(2,1)S(1)} collective-permute-done((bf16[528,128]{1,0:T(8,128)(2,1)S(1)}, bf16[528,128]{1,0:T(8,128)(2,1)S(1)}, u32[]{:S(2)}, u32[]{:S(2)}) %collective-permute-start.3) | collective-permute-done | bytes 135200 | tf_op jit(solution)/shard_map/ppermute | solution.py:307
  25.0 2.4 %collective-permute-done.4.refs_1_ = bf16[512,128]{1,0:T(8,128)(2,1)S(1)} collective-permute-done((bf16[512,128]{1,0:T(8,128)(2,1)S(1)}, bf16[512,128]{1,0:T(8,128)(2,1)S(1)}, u32[]{:S(2)}, u32[]{:S(2)}) %collective-permute-start.4) | collective-permute-done | bytes 131104 | tf_op jit(solution)/shard_map/ppermute | solution.py:262
  27.4 2.2 %collective-permute-start.6 = (bf16[512,128]{1,0:T(8,128)(2,1)S(1)}, bf16[512,128]{1,0:T(8,128)(2,1)S(1)}, u32[]{:S(2)}, u32[]{:S(2)}) collective-permute-start(bf16[512,128]{1,0:T(8,128)(2,1)S(1)} %get-tuple-element.51), channel_id=1, source_target_pairs={{0,2},{2,4},{4,6},{6,0},{8,10},{10,12},{12,14},{14,8},{1,3},{3,5},... | collective-permute-start | bytes 393224 | tf_op jit(solution)/shard_map/ppermute | solution.py:262
  29.6 4.0 %collective-permute-done.6.refs_3_ = bf16[512,128]{1,0:T(8,128)(2,1)S(1)} collective-permute-done((bf16[512,128]{1,0:T(8,128)(2,1)S(1)}, bf16[512,128]{1,0:T(8,128)(2,1)S(1)}, u32[]{:S(2)}, u32[]{:S(2)}) %collective-permute-start.6) | collective-permute-done | bytes 131104 | tf_op jit(solution)/shard_map/ppermute | solution.py:262
  35.4 3.2 %collective-permute-start.10 = (bf16[64,2048]{1,0:T(8,128)(2,1)S(1)}, bf16[64,2048]{1,0:T(8,128)(2,1)S(1)}, u32[]{:S(2)}, u32[]{:S(2)}) collective-permute-start(bf16[64,2048]{1,0:T(8,128)(2,1)S(1)} %get-tuple-element.53.after_ref.refs_0_), channel_id=1, source_target_pairs={{0,4},{1,3},{4,8},{5,1},{8,12},{9,5},{12,14},{13,9},{14,10},{15,13... | collective-permute-start | bytes 786440 | tf_op jit(solution)/shard_map/ppermute | solution.py:256
  38.6 2.4 %collective-permute-done.11.refs_1_ = bf16[64,2048]{1,0:T(8,128)(2,1)S(1)} collective-permute-done((bf16[64,2048]{1,0:T(8,128)(2,1)S(1)}, bf16[64,2048]{1,0:T(8,128)(2,1)S(1)}, u32[]{:S(2)}, u32[]{:S(2)}) %collective-permute-start.11) | collective-permute-done | bytes 262176 | tf_op jit(solution)/shard_map/ppermute | solution.py:256
  45.3 2.1 %collective-permute-done.14.refs_1_ = bf16[64,2048]{1,0:T(8,128)(2,1)S(1)} collective-permute-done((bf16[64,2048]{1,0:T(8,128)(2,1)S(1)}, bf16[64,2048]{1,0:T(8,128)(2,1)S(1)}, u32[]{:S(2)}, u32[]{:S(2)}) %collective-permute-start.14) | collective-permute-done | bytes 262176 | tf_op jit(solution)/shard_map/ppermute | solution.py:256
  51.7 2.1 %collective-permute-done.17.refs_1_ = bf16[64,2048]{1,0:T(8,128)(2,1)S(1)} collective-permute-done((bf16[64,2048]{1,0:T(8,128)(2,1)S(1)}, bf16[64,2048]{1,0:T(8,128)(2,1)S(1)}, u32[]{:S(2)}, u32[]{:S(2)}) %collective-permute-start.17) | collective-permute-done | bytes 262176 | tf_op jit(solution)/shard_map/ppermute | solution.py:256
  58.1 2.1 %collective-permute-done.20.refs_1_ = bf16[64,2048]{1,0:T(8,128)(2,1)S(1)} collective-permute-done((bf16[64,2048]{1,0:T(8,128)(2,1)S(1)}, bf16[64,2048]{1,0:T(8,128)(2,1)S(1)}, u32[]{:S(2)}, u32[]{:S(2)}) %collective-permute-start.20) | collective-permute-done | bytes 262176 | tf_op jit(solution)/shard_map/ppermute | solution.py:256
  64.4 2.1 %collective-permute-done.23.refs_1_ = bf16[64,2048]{1,0:T(8,128)(2,1)S(1)} collective-permute-done((bf16[64,2048]{1,0:T(8,128)(2,1)S(1)}, bf16[64,2048]{1,0:T(8,128)(2,1)S(1)}, u32[]{:S(2)}, u32[]{:S(2)}) %collective-permute-start.23) | collective-permute-done | bytes 262176 | tf_op jit(solution)/shard_map/ppermute | solution.py:256
  77.2 2.0 %experts.8 = (bf16[64,2048]{1,0:T(8,128)(2,1)S(1)}, bf16[64,2048]{1,0:T(8,128)(2,1)S(1)}) custom-call(f32[8,8,128]{2,1,0:T(8,128)S(1)} %shares.1.w_ref, bf16[2048,512]{1,0:T(8,128)(2,1)S(1)} %get-tuple-element.44.after_ref.g0, bf16[2048,512]{1,0:T(8,128)(2,1)S(1)} %get-tuple-element.55.u0, bf16[512,2048]{1,0:T(8,128)(2,1)S(1)} %get-tuple-element.56.d0, ...), custom_call_target="tpu_custom_call" | custom-call | flops 1610612736 | bytes 1048576 | tf_op jit(solution)/shard_map/experts/pallas_call | solution.py:182
  79.2 2.5 %collective-permute-start.12 = (bf16[64,2048]{1,0:T(8,128)(2,1)S(1)}, bf16[64,2048]{1,0:T(8,128)(2,1)S(1)}, u32[]{:S(2)}, u32[]{:S(2)}) collective-permute-start(bf16[64,2048]{1,0:T(8,128)(2,1)S(1)} %get-tuple-element.58), channel_id=1, source_target_pairs={{0,4},{1,3},{4,8},{5,1},{8,12},{9,5},{12,14},{13,9},{14,10},{15,13... | collective-permute-start | bytes 786440 | tf_op jit(solution)/shard_map/ppermute | solution.py:256
  82.5 2.0 %experts.9 = (bf16[64,2048]{1,0:T(8,128)(2,1)S(1)}, bf16[64,2048]{1,0:T(8,128)(2,1)S(1)}) custom-call(f32[8,8,128]{2,1,0:T(8,128)S(1)} %shares.1.w_ref, bf16[2048,512]{1,0:T(8,128)(2,1)S(1)} %get-tuple-element.44.after_ref.g0, bf16[2048,512]{1,0:T(8,128)(2,1)S(1)} %get-tuple-element.55.u0, bf16[512,2048]{1,0:T(8,128)(2,1)S(1)} %get-tuple-element.56.d0, ...), custom_call_target="tpu_custom_call" | custom-call | flops 1610612736 | bytes 1048576 | tf_op jit(solution)/shard_map/experts/pallas_call | solution.py:182
  84.5 2.0 %experts.10 = (bf16[64,2048]{1,0:T(8,128)(2,1)S(1)}, bf16[64,2048]{1,0:T(8,128)(2,1)S(1)}) custom-call(f32[8,8,128]{2,1,0:T(8,128)S(1)} %shares.1.w_ref, bf16[2048,512]{1,0:T(8,128)(2,1)S(1)} %get-tuple-element.44.after_ref.g0, bf16[2048,512]{1,0:T(8,128)(2,1)S(1)} %get-tuple-element.55.u0, bf16[512,2048]{1,0:T(8,128)(2,1)S(1)} %get-tuple-element.56.d0, ...), custom_call_target="tpu_custom_call" | custom-call | flops 1610612736 | bytes 1048576 | tf_op jit(solution)/shard_map/experts/pallas_call | solution.py:182
  86.5 2.0 %experts.11 = (bf16[64,2048]{1,0:T(8,128)(2,1)S(1)}, bf16[64,2048]{1,0:T(8,128)(2,1)S(1)}) custom-call(f32[8,8,128]{2,1,0:T(8,128)S(1)} %shares.1.w_ref, bf16[2048,512]{1,0:T(8,128)(2,1)S(1)} %get-tuple-element.44.after_ref.g0, bf16[2048,512]{1,0:T(8,128)(2,1)S(1)} %get-tuple-element.55.u0, bf16[512,2048]{1,0:T(8,128)(2,1)S(1)} %get-tuple-element.56.d0, ...), custom_call_target="tpu_custom_call" | custom-call | flops 1610612736 | bytes 1048576 | tf_op jit(solution)/shard_map/experts/pallas_call | solution.py:182
  88.5 2.0 %experts.12 = (bf16[64,2048]{1,0:T(8,128)(2,1)S(1)}, bf16[64,2048]{1,0:T(8,128)(2,1)S(1)}) custom-call(f32[8,8,128]{2,1,0:T(8,128)S(1)} %shares.1.w_ref, bf16[2048,512]{1,0:T(8,128)(2,1)S(1)} %get-tuple-element.44.after_ref.g0, bf16[2048,512]{1,0:T(8,128)(2,1)S(1)} %get-tuple-element.55.u0, bf16[512,2048]{1,0:T(8,128)(2,1)S(1)} %get-tuple-element.56.d0, ...), custom_call_target="tpu_custom_call" | custom-call | flops 1610612736 | bytes 1048576 | tf_op jit(solution)/shard_map/experts/pallas_call | solution.py:182
  90.5 2.0 %experts.13 = (bf16[64,2048]{1,0:T(8,128)(2,1)S(1)}, bf16[64,2048]{1,0:T(8,128)(2,1)S(1)}) custom-call(f32[8,8,128]{2,1,0:T(8,128)S(1)} %shares.1.w_ref, bf16[2048,512]{1,0:T(8,128)(2,1)S(1)} %get-tuple-element.44.after_ref.g0, bf16[2048,512]{1,0:T(8,128)(2,1)S(1)} %get-tuple-element.55.u0, bf16[512,2048]{1,0:T(8,128)(2,1)S(1)} %get-tuple-element.56.d0, ...), custom_call_target="tpu_custom_call" | custom-call | flops 1610612736 | bytes 1048576 | tf_op jit(solution)/shard_map/experts/pallas_call | solution.py:182
  92.4 2.0 %experts.15 = (bf16[64,2048]{1,0:T(8,128)(2,1)S(1)}, bf16[64,2048]{1,0:T(8,128)(2,1)S(1)}) custom-call(f32[8,8,128]{2,1,0:T(8,128)S(1)} %shares.1.w_ref, bf16[2048,512]{1,0:T(8,128)(2,1)S(1)} %get-tuple-element.44.after_ref.g0, bf16[2048,512]{1,0:T(8,128)(2,1)S(1)} %get-tuple-element.55.u0, bf16[512,2048]{1,0:T(8,128)(2,1)S(1)} %get-tuple-element.56.d0, ...), custom_call_target="tpu_custom_call" | custom-call | flops 1610612736 | bytes 1048576 | tf_op jit(solution)/shard_map/experts/pallas_call | solution.py:182
  94.5 2.2 %experts.14 = (bf16[64,2048]{1,0:T(8,128)(2,1)S(1)}, bf16[64,2048]{1,0:T(8,128)(2,1)S(1)}) custom-call(f32[8,8,128]{2,1,0:T(8,128)S(1)} %shares.1.w_ref, bf16[2048,512]{1,0:T(8,128)(2,1)S(1)} %get-tuple-element.44.after_ref.g0, bf16[2048,512]{1,0:T(8,128)(2,1)S(1)} %get-tuple-element.55.u0, bf16[512,2048]{1,0:T(8,128)(2,1)S(1)} %get-tuple-element.56.d0, ...), custom_call_target="tpu_custom_call" | custom-call | flops 1610612736 | bytes 1048576 | tf_op jit(solution)/shard_map/experts/pallas_call | solution.py:182
  96.8 1.9 %collective-permute-start.15 = (bf16[64,2048]{1,0:T(8,128)(2,1)S(1)}, bf16[64,2048]{1,0:T(8,128)(2,1)S(1)}, u32[]{:S(2)}, u32[]{:S(2)}) collective-permute-start(bf16[64,2048]{1,0:T(8,128)(2,1)S(1)} %add_convert_fusion.13), channel_id=1, source_target_pairs={{0,4},{1,3},{4,8},{5,1},{8,12},{9,5},{12,14},{13,9},{14,10},{15,13... | collective-permute-start | bytes 786440 | tf_op jit(solution)/shard_map/ppermute | solution.py:256
  99.1 4.1 %collective-permute-done.15 = bf16[64,2048]{1,0:T(8,128)(2,1)S(1)} collective-permute-done((bf16[64,2048]{1,0:T(8,128)(2,1)S(1)}, bf16[64,2048]{1,0:T(8,128)(2,1)S(1)}, u32[]{:S(2)}, u32[]{:S(2)}) %collective-permute-start.15) | collective-permute-done | bytes 262176 | tf_op jit(solution)/shard_map/ppermute | solution.py:256
  103.3 1.9 %collective-permute-start.18 = (bf16[64,2048]{1,0:T(8,128)(2,1)S(1)}, bf16[64,2048]{1,0:T(8,128)(2,1)S(1)}, u32[]{:S(2)}, u32[]{:S(2)}) collective-permute-start(bf16[64,2048]{1,0:T(8,128)(2,1)S(1)} %add_convert_fusion.12), channel_id=1, source_target_pairs={{0,4},{1,3},{4,8},{5,1},{8,12},{9,5},{12,14},{13,9},{14,10},{15,13... | collective-permute-start | bytes 786440 | tf_op jit(solution)/shard_map/ppermute | solution.py:256
  106.1 1.9 %collective-permute-start.33 = (bf16[64,2048]{1,0:T(8,128)(2,1)S(1)}, bf16[64,2048]{1,0:T(8,128)(2,1)S(1)}, u32[]{:S(2)}, u32[]{:S(2)}) collective-permute-start(bf16[64,2048]{1,0:T(8,128)(2,1)S(1)} %add_convert_fusion.5), channel_id=1, source_target_pairs={{0,4},{1,3},{4,8},{5,1},{8,12},{9,5},{12,14},{13,9},{14,10},{15,13... | collective-permute-start | bytes 786440 | tf_op jit(solution)/shard_map/ppermute | solution.py:256
  109.8 1.9 %collective-permute-start.21 = (bf16[64,2048]{1,0:T(8,128)(2,1)S(1)}, bf16[64,2048]{1,0:T(8,128)(2,1)S(1)}, u32[]{:S(2)}, u32[]{:S(2)}) collective-permute-start(bf16[64,2048]{1,0:T(8,128)(2,1)S(1)} %add_convert_fusion.11), channel_id=1, source_target_pairs={{0,4},{1,3},{4,8},{5,1},{8,12},{9,5},{12,14},{13,9},{14,10},{15,13... | collective-permute-start | bytes 786440 | tf_op jit(solution)/shard_map/ppermute | solution.py:256
  116.3 1.9 %collective-permute-start.24 = (bf16[64,2048]{1,0:T(8,128)(2,1)S(1)}, bf16[64,2048]{1,0:T(8,128)(2,1)S(1)}, u32[]{:S(2)}, u32[]{:S(2)}) collective-permute-start(bf16[64,2048]{1,0:T(8,128)(2,1)S(1)} %add_convert_fusion.10), channel_id=1, source_target_pairs={{0,4},{1,3},{4,8},{5,1},{8,12},{9,5},{12,14},{13,9},{14,10},{15,13... | collective-permute-start | bytes 786440 | tf_op jit(solution)/shard_map/ppermute | solution.py:256
  119.1 1.9 %collective-permute-start.35 = (bf16[64,2048]{1,0:T(8,128)(2,1)S(1)}, bf16[64,2048]{1,0:T(8,128)(2,1)S(1)}, u32[]{:S(2)}, u32[]{:S(2)}) collective-permute-start(bf16[64,2048]{1,0:T(8,128)(2,1)S(1)} %add_convert_fusion.3), channel_id=1, source_target_pairs={{0,4},{1,3},{4,8},{5,1},{8,12},{9,5},{12,14},{13,9},{14,10},{15,13... | collective-permute-start | bytes 786440 | tf_op jit(solution)/shard_map/ppermute | solution.py:256
  125.6 1.9 %collective-permute-start.36 = (bf16[64,2048]{1,0:T(8,128)(2,1)S(1)}, bf16[64,2048]{1,0:T(8,128)(2,1)S(1)}, u32[]{:S(2)}, u32[]{:S(2)}) collective-permute-start(bf16[64,2048]{1,0:T(8,128)(2,1)S(1)} %add_convert_fusion.2), channel_id=1, source_target_pairs={{0,4},{1,3},{4,8},{5,1},{8,12},{9,5},{12,14},{13,9},{14,10},{15,13... | collective-permute-start | bytes 786440 | tf_op jit(solution)/shard_map/ppermute | solution.py:256
  135.8 2.7 %collective-permute-done.37 = bf16[64,2048]{1,0:T(8,128)(2,1)S(1)} collective-permute-done((bf16[64,2048]{1,0:T(8,128)(2,1)S(1)}, bf16[64,2048]{1,0:T(8,128)(2,1)S(1)}, u32[]{:S(2)}, u32[]{:S(2)}) %collective-permute-start.37) | collective-permute-done | bytes 262176 | tf_op jit(solution)/shard_map/ppermute | solution.py:256
  (77 shorter events, 62.3 us)
Async XLA Ops:
  2.6 9.5 %collective-permute-start = (bf16[528,128]{1,0:T(8,128)(2,1)S(1)}, bf16[528,128]{1,0:T(8,128)(2,1)S(1)}, u32[]{:S(2)}, u32[]{:S(2)}) collective-permute-start(bf16[528,128]{1,0:T(8,128)(2,1)S(1)} %get-tuple-element.45), channel_id=1, source_target_pairs={{0,2},{2,4},{4,6},{6,0},{8,10},{10,12},{12,14},{14,8},{1,3},{3,5},... | collective-permute-start | bytes 405512 | tf_op jit(solution)/shard_map/ppermute | solution.py:262
  5.7 6.5 %collective-permute-start.1 = (bf16[528,128]{1,0:T(8,128)(2,1)S(1)}, bf16[528,128]{1,0:T(8,128)(2,1)S(1)}, u32[]{:S(2)}, u32[]{:S(2)}) collective-permute-start(bf16[528,128]{1,0:T(8,128)(2,1)S(1)} %get-tuple-element.46), channel_id=1, source_target_pairs={{0,4},{2,6},{4,0},{6,2},{8,12},{10,14},{12,8},{14,10},{1,5},{3,7},... | collective-permute-start | bytes 405512 | tf_op jit(solution)/shard_map/ppermute | solution.py:262
  11.6 65.6 %collective-permute-start.7 = (bf16[2048,512]{1,0:T(8,128)(2,1)S(1)}, bf16[2048,512]{1,0:T(8,128)(2,1)S(1)}, u32[]{:S(2)}, u32[]{:S(2)}) collective-permute-start(bf16[2048,512]{1,0:T(8,128)(2,1)S(1)} %get-tuple-element.44.after_ref.g0), channel_id=1, source_target_pairs={{0,1},{1,0},{2,3},{3,2},{4,5},{5,4},{6,7},{7,6},{8,9},{9,8},{10,11... | collective-permute-start | bytes 6291464 | tf_op jit(solution)/shard_map/ppermute | solution.py:297
  11.7 65.5 %collective-permute-start.8 = (bf16[2048,512]{1,0:T(8,128)(2,1)S(1)}, bf16[2048,512]{1,0:T(8,128)(2,1)S(1)}, u32[]{:S(2)}, u32[]{:S(2)}) collective-permute-start(bf16[2048,512]{1,0:T(8,128)(2,1)S(1)} %get-tuple-element.55.u0), channel_id=1, source_target_pairs={{0,1},{1,0},{2,3},{3,2},{4,5},{5,4},{6,7},{7,6},{8,9},{9,8},{10,11... | collective-permute-start | bytes 6291464 | tf_op jit(solution)/shard_map/ppermute | solution.py:297
  12.2 65.0 %collective-permute-start.9 = (bf16[512,2048]{1,0:T(8,128)(2,1)S(1)}, bf16[512,2048]{1,0:T(8,128)(2,1)S(1)}, u32[]{:S(2)}, u32[]{:S(2)}) collective-permute-start(bf16[512,2048]{1,0:T(8,128)(2,1)S(1)} %get-tuple-element.56.d0), channel_id=1, source_target_pairs={{0,1},{1,0},{2,3},{3,2},{4,5},{5,4},{6,7},{7,6},{8,9},{9,8},{10,11... | collective-permute-start | bytes 6291464 | tf_op jit(solution)/shard_map/ppermute | solution.py:297
  13.3 8.9 %collective-permute-start.3 = (bf16[528,128]{1,0:T(8,128)(2,1)S(1)}, bf16[528,128]{1,0:T(8,128)(2,1)S(1)}, u32[]{:S(2)}, u32[]{:S(2)}) collective-permute-start(bf16[528,128]{1,0:T(8,128)(2,1)S(1)} %total.1), channel_id=1, source_target_pairs={{0,8},{2,10},{4,12},{6,14},{8,0},{10,2},{12,4},{14,6},{1,9},{3,11}... | collective-permute-start | bytes 405512 | tf_op jit(solution)/shard_map/ppermute | solution.py:307
  34.6 6.4 %collective-permute-start.11 = (bf16[64,2048]{1,0:T(8,128)(2,1)S(1)}, bf16[64,2048]{1,0:T(8,128)(2,1)S(1)}, u32[]{:S(2)}, u32[]{:S(2)}) collective-permute-start(bf16[64,2048]{1,0:T(8,128)(2,1)S(1)} %get-tuple-element.57.refs_1_), channel_id=1, source_target_pairs={{0,4},{1,3},{4,8},{5,1},{8,12},{9,5},{12,14},{13,9},{14,10},{15,13... | collective-permute-start | bytes 786440 | tf_op jit(solution)/shard_map/ppermute | solution.py:256
  35.4 8.5 %collective-permute-start.10 = (bf16[64,2048]{1,0:T(8,128)(2,1)S(1)}, bf16[64,2048]{1,0:T(8,128)(2,1)S(1)}, u32[]{:S(2)}, u32[]{:S(2)}) collective-permute-start(bf16[64,2048]{1,0:T(8,128)(2,1)S(1)} %get-tuple-element.53.after_ref.refs_0_), channel_id=1, source_target_pairs={{0,4},{1,3},{4,8},{5,1},{8,12},{9,5},{12,14},{13,9},{14,10},{15,13... | collective-permute-start | bytes 786440 | tf_op jit(solution)/shard_map/ppermute | solution.py:256
  41.1 6.4 %collective-permute-start.14 = (bf16[64,2048]{1,0:T(8,128)(2,1)S(1)}, bf16[64,2048]{1,0:T(8,128)(2,1)S(1)}, u32[]{:S(2)}, u32[]{:S(2)}) collective-permute-start(bf16[64,2048]{1,0:T(8,128)(2,1)S(1)} %collective-permute-done.11.refs_1_), channel_id=1, source_target_pairs={{0,4},{1,3},{4,8},{5,1},{8,12},{9,5},{12,14},{13,9},{14,10},{15,13... | collective-permute-start | bytes 786440 | tf_op jit(solution)/shard_map/ppermute | solution.py:256
  43.9 6.4 %collective-permute-start.13 = (bf16[64,2048]{1,0:T(8,128)(2,1)S(1)}, bf16[64,2048]{1,0:T(8,128)(2,1)S(1)}, u32[]{:S(2)}, u32[]{:S(2)}) collective-permute-start(bf16[64,2048]{1,0:T(8,128)(2,1)S(1)} %collective-permute-done.10.refs_0_), channel_id=1, source_target_pairs={{0,4},{1,3},{4,8},{5,1},{8,12},{9,5},{12,14},{13,9},{14,10},{15,13... | collective-permute-start | bytes 786440 | tf_op jit(solution)/shard_map/ppermute | solution.py:256
  47.4 6.4 %collective-permute-start.17 = (bf16[64,2048]{1,0:T(8,128)(2,1)S(1)}, bf16[64,2048]{1,0:T(8,128)(2,1)S(1)}, u32[]{:S(2)}, u32[]{:S(2)}) collective-permute-start(bf16[64,2048]{1,0:T(8,128)(2,1)S(1)} %collective-permute-done.14.refs_1_), channel_id=1, source_target_pairs={{0,4},{1,3},{4,8},{5,1},{8,12},{9,5},{12,14},{13,9},{14,10},{15,13... | collective-permute-start | bytes 786440 | tf_op jit(solution)/shard_map/ppermute | solution.py:256
  50.2 6.4 %collective-permute-start.16 = (bf16[64,2048]{1,0:T(8,128)(2,1)S(1)}, bf16[64,2048]{1,0:T(8,128)(2,1)S(1)}, u32[]{:S(2)}, u32[]{:S(2)}) collective-permute-start(bf16[64,2048]{1,0:T(8,128)(2,1)S(1)} %collective-permute-done.13.refs_0_), channel_id=1, source_target_pairs={{0,4},{1,3},{4,8},{5,1},{8,12},{9,5},{12,14},{13,9},{14,10},{15,13... | collective-permute-start | bytes 786440 | tf_op jit(solution)/shard_map/ppermute | solution.py:256
  53.8 6.4 %collective-permute-start.20 = (bf16[64,2048]{1,0:T(8,128)(2,1)S(1)}, bf16[64,2048]{1,0:T(8,128)(2,1)S(1)}, u32[]{:S(2)}, u32[]{:S(2)}) collective-permute-start(bf16[64,2048]{1,0:T(8,128)(2,1)S(1)} %collective-permute-done.17.refs_1_), channel_id=1, source_target_pairs={{0,4},{1,3},{4,8},{5,1},{8,12},{9,5},{12,14},{13,9},{14,10},{15,13... | collective-permute-start | bytes 786440 | tf_op jit(solution)/shard_map/ppermute | solution.py:256
  56.6 6.4 %collective-permute-start.19 = (bf16[64,2048]{1,0:T(8,128)(2,1)S(1)}, bf16[64,2048]{1,0:T(8,128)(2,1)S(1)}, u32[]{:S(2)}, u32[]{:S(2)}) collective-permute-start(bf16[64,2048]{1,0:T(8,128)(2,1)S(1)} %collective-permute-done.16.refs_0_), channel_id=1, source_target_pairs={{0,4},{1,3},{4,8},{5,1},{8,12},{9,5},{12,14},{13,9},{14,10},{15,13... | collective-permute-start | bytes 786440 | tf_op jit(solution)/shard_map/ppermute | solution.py:256
  60.2 6.4 %collective-permute-start.23 = (bf16[64,2048]{1,0:T(8,128)(2,1)S(1)}, bf16[64,2048]{1,0:T(8,128)(2,1)S(1)}, u32[]{:S(2)}, u32[]{:S(2)}) collective-permute-start(bf16[64,2048]{1,0:T(8,128)(2,1)S(1)} %collective-permute-done.20.refs_1_), channel_id=1, source_target_pairs={{0,4},{1,3},{4,8},{5,1},{8,12},{9,5},{12,14},{13,9},{14,10},{15,13... | collective-permute-start | bytes 786440 | tf_op jit(solution)/shard_map/ppermute | solution.py:256
  63.0 6.4 %collective-permute-start.22 = (bf16[64,2048]{1,0:T(8,128)(2,1)S(1)}, bf16[64,2048]{1,0:T(8,128)(2,1)S(1)}, u32[]{:S(2)}, u32[]{:S(2)}) collective-permute-start(bf16[64,2048]{1,0:T(8,128)(2,1)S(1)} %collective-permute-done.19.refs_0_), channel_id=1, source_target_pairs={{0,4},{1,3},{4,8},{5,1},{8,12},{9,5},{12,14},{13,9},{14,10},{15,13... | collective-permute-start | bytes 786440 | tf_op jit(solution)/shard_map/ppermute | solution.py:256
  72.9 21.6 %collective-permute-start.29 = (bf16[64,2048]{1,0:T(8,128)(2,1)S(1)}, bf16[64,2048]{1,0:T(8,128)(2,1)S(1)}, u32[]{:S(2)}, u32[]{:S(2)}) collective-permute-start(bf16[64,2048]{1,0:T(8,128)(2,1)S(1)} %collective-permute-done.26.refs_1_), channel_id=1, source_target_pairs={{0,4},{1,3},{4,8},{5,1},{8,12},{9,5},{12,14},{13,9},{14,10},{15,13... | collective-permute-start | bytes 786440 | tf_op jit(solution)/shard_map/ppermute | solution.py:256
  75.7 18.8 %collective-permute-start.28 = (bf16[64,2048]{1,0:T(8,128)(2,1)S(1)}, bf16[64,2048]{1,0:T(8,128)(2,1)S(1)}, u32[]{:S(2)}, u32[]{:S(2)}) collective-permute-start(bf16[64,2048]{1,0:T(8,128)(2,1)S(1)} %collective-permute-done.25.refs_0_), channel_id=1, source_target_pairs={{0,4},{1,3},{4,8},{5,1},{8,12},{9,5},{12,14},{13,9},{14,10},{15,13... | collective-permute-start | bytes 786440 | tf_op jit(solution)/shard_map/ppermute | solution.py:256
  79.2 17.5 %collective-permute-start.12 = (bf16[64,2048]{1,0:T(8,128)(2,1)S(1)}, bf16[64,2048]{1,0:T(8,128)(2,1)S(1)}, u32[]{:S(2)}, u32[]{:S(2)}) collective-permute-start(bf16[64,2048]{1,0:T(8,128)(2,1)S(1)} %get-tuple-element.58), channel_id=1, source_target_pairs={{0,4},{1,3},{4,8},{5,1},{8,12},{9,5},{12,14},{13,9},{14,10},{15,13... | collective-permute-start | bytes 786440 | tf_op jit(solution)/shard_map/ppermute | solution.py:256
  81.7 17.0 %collective-permute-start.31 = (bf16[64,2048]{1,0:T(8,128)(2,1)S(1)}, bf16[64,2048]{1,0:T(8,128)(2,1)S(1)}, u32[]{:S(2)}, u32[]{:S(2)}) collective-permute-start(bf16[64,2048]{1,0:T(8,128)(2,1)S(1)} %get-tuple-element.66), channel_id=1, source_target_pairs={{0,4},{1,3},{4,8},{5,1},{8,12},{9,5},{12,14},{13,9},{14,10},{15,13... | collective-permute-start | bytes 786440 | tf_op jit(solution)/shard_map/ppermute | solution.py:256
  96.8 6.4 %collective-permute-start.15 = (bf16[64,2048]{1,0:T(8,128)(2,1)S(1)}, bf16[64,2048]{1,0:T(8,128)(2,1)S(1)}, u32[]{:S(2)}, u32[]{:S(2)}) collective-permute-start(bf16[64,2048]{1,0:T(8,128)(2,1)S(1)} %add_convert_fusion.13), channel_id=1, source_target_pairs={{0,4},{1,3},{4,8},{5,1},{8,12},{9,5},{12,14},{13,9},{14,10},{15,13... | collective-permute-start | bytes 786440 | tf_op jit(solution)/shard_map/ppermute | solution.py:256
  98.8 7.2 %collective-permute-start.32 = (bf16[64,2048]{1,0:T(8,128)(2,1)S(1)}, bf16[64,2048]{1,0:T(8,128)(2,1)S(1)}, u32[]{:S(2)}, u32[]{:S(2)}) collective-permute-start(bf16[64,2048]{1,0:T(8,128)(2,1)S(1)} %add_convert_fusion.6), channel_id=1, source_target_pairs={{0,4},{1,3},{4,8},{5,1},{8,12},{9,5},{12,14},{13,9},{14,10},{15,13... | collective-permute-start | bytes 786440 | tf_op jit(solution)/shard_map/ppermute | solution.py:256
  103.3 6.4 %collective-permute-start.18 = (bf16[64,2048]{1,0:T(8,128)(2,1)S(1)}, bf16[64,2048]{1,0:T(8,128)(2,1)S(1)}, u32[]{:S(2)}, u32[]{:S(2)}) collective-permute-start(bf16[64,2048]{1,0:T(8,128)(2,1)S(1)} %add_convert_fusion.12), channel_id=1, source_target_pairs={{0,4},{1,3},{4,8},{5,1},{8,12},{9,5},{12,14},{13,9},{14,10},{15,13... | collective-permute-start | bytes 786440 | tf_op jit(solution)/shard_map/ppermute | solution.py:256
  106.1 6.4 %collective-permute-start.33 = (bf16[64,2048]{1,0:T(8,128)(2,1)S(1)}, bf16[64,2048]{1,0:T(8,128)(2,1)S(1)}, u32[]{:S(2)}, u32[]{:S(2)}) collective-permute-start(bf16[64,2048]{1,0:T(8,128)(2,1)S(1)} %add_convert_fusion.5), channel_id=1, source_target_pairs={{0,4},{1,3},{4,8},{5,1},{8,12},{9,5},{12,14},{13,9},{14,10},{15,13... | collective-permute-start | bytes 786440 | tf_op jit(solution)/shard_map/ppermute | solution.py:256
  109.8 6.4 %collective-permute-start.21 = (bf16[64,2048]{1,0:T(8,128)(2,1)S(1)}, bf16[64,2048]{1,0:T(8,128)(2,1)S(1)}, u32[]{:S(2)}, u32[]{:S(2)}) collective-permute-start(bf16[64,2048]{1,0:T(8,128)(2,1)S(1)} %add_convert_fusion.11), channel_id=1, source_target_pairs={{0,4},{1,3},{4,8},{5,1},{8,12},{9,5},{12,14},{13,9},{14,10},{15,13... | collective-permute-start | bytes 786440 | tf_op jit(solution)/shard_map/ppermute | solution.py:256
  112.6 6.4 %collective-permute-start.34 = (bf16[64,2048]{1,0:T(8,128)(2,1)S(1)}, bf16[64,2048]{1,0:T(8,128)(2,1)S(1)}, u32[]{:S(2)}, u32[]{:S(2)}) collective-permute-start(bf16[64,2048]{1,0:T(8,128)(2,1)S(1)} %add_convert_fusion.4), channel_id=1, source_target_pairs={{0,4},{1,3},{4,8},{5,1},{8,12},{9,5},{12,14},{13,9},{14,10},{15,13... | collective-permute-start | bytes 786440 | tf_op jit(solution)/shard_map/ppermute | solution.py:256
  116.3 6.4 %collective-permute-start.24 = (bf16[64,2048]{1,0:T(8,128)(2,1)S(1)}, bf16[64,2048]{1,0:T(8,128)(2,1)S(1)}, u32[]{:S(2)}, u32[]{:S(2)}) collective-permute-start(bf16[64,2048]{1,0:T(8,128)(2,1)S(1)} %add_convert_fusion.10), channel_id=1, source_target_pairs={{0,4},{1,3},{4,8},{5,1},{8,12},{9,5},{12,14},{13,9},{14,10},{15,13... | collective-permute-start | bytes 786440 | tf_op jit(solution)/shard_map/ppermute | solution.py:256
  119.1 6.4 %collective-permute-start.35 = (bf16[64,2048]{1,0:T(8,128)(2,1)S(1)}, bf16[64,2048]{1,0:T(8,128)(2,1)S(1)}, u32[]{:S(2)}, u32[]{:S(2)}) collective-permute-start(bf16[64,2048]{1,0:T(8,128)(2,1)S(1)} %add_convert_fusion.3), channel_id=1, source_target_pairs={{0,4},{1,3},{4,8},{5,1},{8,12},{9,5},{12,14},{13,9},{14,10},{15,13... | collective-permute-start | bytes 786440 | tf_op jit(solution)/shard_map/ppermute | solution.py:256
  122.8 6.4 %collective-permute-start.27 = (bf16[64,2048]{1,0:T(8,128)(2,1)S(1)}, bf16[64,2048]{1,0:T(8,128)(2,1)S(1)}, u32[]{:S(2)}, u32[]{:S(2)}) collective-permute-start(bf16[64,2048]{1,0:T(8,128)(2,1)S(1)} %add_convert_fusion.9), channel_id=1, source_target_pairs={{0,4},{1,3},{4,8},{5,1},{8,12},{9,5},{12,14},{13,9},{14,10},{15,13... | collective-permute-start | bytes 786440 | tf_op jit(solution)/shard_map/ppermute | solution.py:256
  125.6 6.4 %collective-permute-start.36 = (bf16[64,2048]{1,0:T(8,128)(2,1)S(1)}, bf16[64,2048]{1,0:T(8,128)(2,1)S(1)}, u32[]{:S(2)}, u32[]{:S(2)}) collective-permute-start(bf16[64,2048]{1,0:T(8,128)(2,1)S(1)} %add_convert_fusion.2), channel_id=1, source_target_pairs={{0,4},{1,3},{4,8},{5,1},{8,12},{9,5},{12,14},{13,9},{14,10},{15,13... | collective-permute-start | bytes 786440 | tf_op jit(solution)/shard_map/ppermute | solution.py:256
  129.3 6.4 %collective-permute-start.30 = (bf16[64,2048]{1,0:T(8,128)(2,1)S(1)}, bf16[64,2048]{1,0:T(8,128)(2,1)S(1)}, u32[]{:S(2)}, u32[]{:S(2)}) collective-permute-start(bf16[64,2048]{1,0:T(8,128)(2,1)S(1)} %add_convert_fusion.8), channel_id=1, source_target_pairs={{0,4},{1,3},{4,8},{5,1},{8,12},{9,5},{12,14},{13,9},{14,10},{15,13... | collective-permute-start | bytes 786440 | tf_op jit(solution)/shard_map/ppermute | solution.py:256
  132.1 6.4 %collective-permute-start.37 = (bf16[64,2048]{1,0:T(8,128)(2,1)S(1)}, bf16[64,2048]{1,0:T(8,128)(2,1)S(1)}, u32[]{:S(2)}, u32[]{:S(2)}) collective-permute-start(bf16[64,2048]{1,0:T(8,128)(2,1)S(1)} %add_convert_fusion.1), channel_id=1, source_target_pairs={{0,4},{1,3},{4,8},{5,1},{8,12},{9,5},{12,14},{13,9},{14,10},{15,13... | collective-permute-start | bytes 786440 | tf_op jit(solution)/shard_map/ppermute | solution.py:256
  (6 other events, 35.8 us)

commit v3 on v2

--- a/solution.py
+++ b/solution.py
@@ -10,7 +10,7 @@
 
 HEAD_DIM = 128
 PAD = 16
-CHUNKS = 4
+CHUNKS = 1
 PIECES = 2
 STRIP = 32
 
@@ -54,7 +54,7 @@
         return jnp.sum(jnp.where(ids == expert, shares, 0.0), axis=0, keepdims=True)
 
     for r, send_ref in enumerate(sends):
-        to = lax.rem(place + r, half)
+        to = lax.bitwise_xor(place, r)
         rows = []
         for side in (group, 1 - group):
             first = 2 * (side * half + to)
@@ -69,7 +69,7 @@
             cols = slice(h * HEAD_DIM, (h + 1) * HEAD_DIM)
             state_ref[cols, :] = dot(k_ref[:, cols], v_ref[:, cols], ((0,), (0,))).astype(bf16)
     for r, send_ref in enumerate(sends):
-        to = lax.rem(place + r, half)
+        to = lax.bitwise_xor(place, r)
         send_ref[:part, :] = state_ref[pl.ds(pl.multiple_of(to * part, part), part), :]
 
 
@@ -90,17 +90,17 @@
     gots, backs = refs[:half], refs[half:]
     part = backs[0].shape[0]
     group, place = lax.div(lax.axis_index("seq"), half), lax.rem(lax.axis_index("seq"), half)
+    sources = [lax.bitwise_xor(place, r) for r in range(half)]
     for row in range(0, part, STRIP):
         strip = slice(row, row + STRIP)
         states = [got_ref[strip, :].astype(f32) for got_ref in gots]
         before = jnp.where(group == 1, far_ref[strip, :].astype(f32), 0.0)
-        total = before
         for r in range(half):
-            total = total + jnp.where(r <= place, states[r], 0.0)
-        for r in reversed(range(half)):
-            total = jnp.where(r == place, before, total)
+            total = before
+            for other in range(half):
+                if other != r:
+                    total = total + jnp.where(sources[other] < sources[r], states[other], 0.0)
             backs[r][strip, :] = total.astype(bf16)
-            total = total + states[r]
 
 
 def shares_kernel(half, far_ref, *refs):
@@ -109,7 +109,7 @@
     group, place = lax.div(lax.axis_index("seq"), half), lax.rem(lax.axis_index("seq"), half)
     far = far_ref[part:, :].astype(f32)
     for r in range(half):
-        source = lax.rem(place + half - r, half)
+        source = lax.bitwise_xor(place, r)
         terms = gots[r][part:, :].astype(f32)
         shares_ref[group * half + source, 0:2, :] = terms[0:2] + terms[2:4]
         terms = far[4 * r : 4 * r + 4]
@@ -138,7 +138,7 @@
     part = width // half
     feature_sq = jnp.zeros((rows, HEAD_DIM), f32)
     for r in range(half):
-        part_of = lax.rem(lax.rem(lax.axis_index("seq"), half) + r, half)
+        part_of = lax.bitwise_xor(lax.rem(lax.axis_index("seq"), half), r)
         for h in range(0, part, HEAD_DIM):
             cols = pl.ds(pl.multiple_of(part_of * part + h, HEAD_DIM), HEAD_DIM)
             raw = within_ref[take, cols] + dot(q_ref[take, cols], carried[r][h : h + HEAD_DIM, :])
@@ -255,10 +255,10 @@
     def hop(value):
         return lax.ppermute(value, ("seq", "expert"), hops)
 
-    def along(blocks, sign):
+    def along(blocks):
         moved = [blocks[0]]
         for r in range(1, half):
-            pairs = [(s, s // half * half + (s + sign * r) % half) for s in range(n_seq)]
+            pairs = [(s, s ^ r) for s in range(n_seq)]
             moved.append(lax.ppermute(blocks[r], "seq", pairs))
         return moved
 
@@ -295,7 +295,7 @@
     )(q, k, v)
     own = load(sends[0], *own)
     other = [lax.ppermute(w, "expert", [(0, 1), (1, 0)]) for w in own]
-    gots = along(sends, 1)
+    gots = along(sends)
     near = pl.pallas_call(
         functools.partial(total_kernel, half),
         in_specs=[ANY] + [VMEM] * half,
@@ -321,7 +321,7 @@
         out_shape=jax.ShapeDtypeStruct((n_seq, 8, rows), f32),
         name="shares",
     )(far, *gots)
-    carried = along(backs, -1)
+    carried = along(backs)
     piece = rows // PIECES
     attention, normed = [], []
     for i in range(PIECES):

time: 140 us -> 139 us (level)
  starting transfers between devices: 60.7 us -> 40.9 us
  waiting for transfers between devices: 50.5 us -> 69.7 us
    ppermute x28, starting transfers between devices: 46.4 us -> 29.4 us  [hop(): return lax.ppermute(value, ('seq', 'expert'), hops)]
    ppermute x28, waiting for transfers between devices: 39.3 us -> 56.1 us  [hop(): return lax.ppermute(value, ('seq', 'expert'), hops)]
    ppermute x6, starting transfers between devices: 10.8 us -> 7.99 us  [along(): moved.append(lax.ppermute(blocks[r], 'seq', pairs))]
    ppermute x6, waiting for transfers between devices: 7.36 us -> 10.2 us  [along(): moved.append(lax.ppermute(blocks[r], 'seq', pairs))]
  transfers between devices with their start and end apart: 38 -> 38, of which waited for: 28 -> 30; matrix products, arithmetic and copies ran while one was open for 1% -> 1% of each run, Pallas kernels for 16% -> 16%
where the time goes in v3:
time: 139 us; the launch traced here: 138 us
  waiting for transfers between devices  69.7 us (50%)
  starting transfers between devices  40.9 us (29%)
  Pallas kernels  24.4 us (18%)
  other arithmetic  2.66 us (2%)
    ppermute x28, waiting for transfers between devices, hop(): return lax.ppermute(value, ('seq', 'expert'), hops)  56.1 us
    ppermute x28, starting transfers between devices, hop(): return lax.ppermute(value, ('seq', 'expert'), hops)  29.4 us
    pallas_call x8, Pallas kernels, run_experts(): pl.pallas_call(functools.partial(expert_kernel, hop), in_specs=[VMEM] * (...  16.2 us
    ppermute x6, waiting for transfers between devices, along(): moved.append(lax.ppermute(blocks[r], 'seq', pairs))  10.2 us
    ppermute x6, starting transfers between devices, along(): moved.append(lax.ppermute(blocks[r], 'seq', pairs))  7.99 us
    pallas_call x2, Pallas kernels, load(): pl.pallas_call(functools.partial(load_kernel, count), in_specs=[HBM] * (c...  4.29 us
    ppermute x1, waiting for transfers between devices, per_device(): lax.ppermute(near, 'seq', [(s, (s + half) % n_seq) for s in range(n_seq)])  3.38 us
    ppermute x1, starting transfers between devices, per_device(): lax.ppermute(near, 'seq', [(s, (s + half) % n_seq) for s in range(n_seq)])  2.8 us
  transfers between devices with their start and end apart: 38, of which 30 were waited for; matrix products, arithmetic and copies ran while one was open for 1% of the time, Pallas kernels for 16%

profile of v3, /device:TPU:0, one launch (start us, length us, event | category | flops | bytes accessed | tf_op | source)
XLA Modules:
  0.0 138.5 jit_solution(2799093556620790199)
XLA Ops:
  2.3 3.1 %collective-permute-start = (bf16[528,128]{1,0:T(8,128)(2,1)S(1)}, bf16[528,128]{1,0:T(8,128)(2,1)S(1)}, u32[]{:S(2)}, u32[]{:S(2)}) collective-permute-start(bf16[528,128]{1,0:T(8,128)(2,1)S(1)} %get-tuple-element.45), channel_id=1, source_target_pairs={{0,2},{2,0},{4,6},{6,4},{8,10},{10,8},{12,14},{14,12},{1,3},{3,1},... | collective-permute-start | bytes 405512 | tf_op jit(solution)/shard_map/ppermute | solution.py:262
  7.0 2.9 %load.3 = (bf16[2048,512]{1,0:T(8,128)(2,1)S(1)}, bf16[2048,512]{1,0:T(8,128)(2,1)S(1)}, bf16[512,2048]{1,0:T(8,128)(2,1)S(1)}) custom-call(bf16[528,128]{1,0:T(8,128)(2,1)S(1)} %get-tuple-element.38.after_ref.refs_0_, bf16[2048,512]{1,0:T(8,128)(2,1)} %bitcast.22, bf16[2048,512]{1,0:T(8,128)(2,1)} %bitcast.23, bf16[512,2048]{1,0:T(8,128)(2,1)} %bitcast.24), custom_call_target="tpu_custom_call" | custom-call | bytes 6291456 | tf_op jit(solution)/shard_map/load/pallas_call | solution.py:215
  13.2 2.8 %collective-permute-start.3 = (bf16[528,128]{1,0:T(8,128)(2,1)S(1)}, bf16[528,128]{1,0:T(8,128)(2,1)S(1)}, u32[]{:S(2)}, u32[]{:S(2)}) collective-permute-start(bf16[528,128]{1,0:T(8,128)(2,1)S(1)} %total.1), channel_id=1, source_target_pairs={{0,8},{2,10},{4,12},{6,14},{8,0},{10,2},{12,4},{14,6},{1,9},{3,11}... | collective-permute-start | bytes 405512 | tf_op jit(solution)/shard_map/ppermute | solution.py:307
  18.3 3.4 %collective-permute-done.3.far_ref = bf16[528,128]{1,0:T(8,128)(2,1)S(1)} collective-permute-done((bf16[528,128]{1,0:T(8,128)(2,1)S(1)}, bf16[528,128]{1,0:T(8,128)(2,1)S(1)}, u32[]{:S(2)}, u32[]{:S(2)}) %collective-permute-start.3) | collective-permute-done | bytes 135200 | tf_op jit(solution)/shard_map/ppermute | solution.py:307
  23.9 3.1 %collective-permute-done.4.refs_1_ = bf16[512,128]{1,0:T(8,128)(2,1)S(1)} collective-permute-done((bf16[512,128]{1,0:T(8,128)(2,1)S(1)}, bf16[512,128]{1,0:T(8,128)(2,1)S(1)}, u32[]{:S(2)}, u32[]{:S(2)}) %collective-permute-start.4) | collective-permute-done | bytes 131104 | tf_op jit(solution)/shard_map/ppermute | solution.py:262
  29.0 3.9 %collective-permute-done.6.refs_3_ = bf16[512,128]{1,0:T(8,128)(2,1)S(1)} collective-permute-done((bf16[512,128]{1,0:T(8,128)(2,1)S(1)}, bf16[512,128]{1,0:T(8,128)(2,1)S(1)}, u32[]{:S(2)}, u32[]{:S(2)}) %collective-permute-start.6) | collective-permute-done | bytes 131104 | tf_op jit(solution)/shard_map/ppermute | solution.py:262
  36.3 4.0 %collective-permute-done.11.refs_1_ = bf16[64,2048]{1,0:T(8,128)(2,1)S(1)} collective-permute-done((bf16[64,2048]{1,0:T(8,128)(2,1)S(1)}, bf16[64,2048]{1,0:T(8,128)(2,1)S(1)}, u32[]{:S(2)}, u32[]{:S(2)}) %collective-permute-start.11) | collective-permute-done | bytes 262176 | tf_op jit(solution)/shard_map/ppermute | solution.py:256
  40.8 2.3 %collective-permute-done.10.refs_0_ = bf16[64,2048]{1,0:T(8,128)(2,1)S(1)} collective-permute-done((bf16[64,2048]{1,0:T(8,128)(2,1)S(1)}, bf16[64,2048]{1,0:T(8,128)(2,1)S(1)}, u32[]{:S(2)}, u32[]{:S(2)}) %collective-permute-start.10) | collective-permute-done | bytes 262176 | tf_op jit(solution)/shard_map/ppermute | solution.py:256
  43.6 3.1 %collective-permute-done.14.refs_1_ = bf16[64,2048]{1,0:T(8,128)(2,1)S(1)} collective-permute-done((bf16[64,2048]{1,0:T(8,128)(2,1)S(1)}, bf16[64,2048]{1,0:T(8,128)(2,1)S(1)}, u32[]{:S(2)}, u32[]{:S(2)}) %collective-permute-start.14) | collective-permute-done | bytes 262176 | tf_op jit(solution)/shard_map/ppermute | solution.py:256
  47.2 2.3 %collective-permute-done.13.refs_0_ = bf16[64,2048]{1,0:T(8,128)(2,1)S(1)} collective-permute-done((bf16[64,2048]{1,0:T(8,128)(2,1)S(1)}, bf16[64,2048]{1,0:T(8,128)(2,1)S(1)}, u32[]{:S(2)}, u32[]{:S(2)}) %collective-permute-start.13) | collective-permute-done | bytes 262176 | tf_op jit(solution)/shard_map/ppermute | solution.py:256
  50.0 3.1 %collective-permute-done.17.refs_1_ = bf16[64,2048]{1,0:T(8,128)(2,1)S(1)} collective-permute-done((bf16[64,2048]{1,0:T(8,128)(2,1)S(1)}, bf16[64,2048]{1,0:T(8,128)(2,1)S(1)}, u32[]{:S(2)}, u32[]{:S(2)}) %collective-permute-start.17) | collective-permute-done | bytes 262176 | tf_op jit(solution)/shard_map/ppermute | solution.py:256
  53.6 2.3 %collective-permute-done.16.refs_0_ = bf16[64,2048]{1,0:T(8,128)(2,1)S(1)} collective-permute-done((bf16[64,2048]{1,0:T(8,128)(2,1)S(1)}, bf16[64,2048]{1,0:T(8,128)(2,1)S(1)}, u32[]{:S(2)}, u32[]{:S(2)}) %collective-permute-start.16) | collective-permute-done | bytes 262176 | tf_op jit(solution)/shard_map/ppermute | solution.py:256
  56.4 3.1 %collective-permute-done.20.refs_1_ = bf16[64,2048]{1,0:T(8,128)(2,1)S(1)} collective-permute-done((bf16[64,2048]{1,0:T(8,128)(2,1)S(1)}, bf16[64,2048]{1,0:T(8,128)(2,1)S(1)}, u32[]{:S(2)}, u32[]{:S(2)}) %collective-permute-start.20) | collective-permute-done | bytes 262176 | tf_op jit(solution)/shard_map/ppermute | solution.py:256
  59.9 2.3 %collective-permute-done.19.refs_0_ = bf16[64,2048]{1,0:T(8,128)(2,1)S(1)} collective-permute-done((bf16[64,2048]{1,0:T(8,128)(2,1)S(1)}, bf16[64,2048]{1,0:T(8,128)(2,1)S(1)}, u32[]{:S(2)}, u32[]{:S(2)}) %collective-permute-start.19) | collective-permute-done | bytes 262176 | tf_op jit(solution)/shard_map/ppermute | solution.py:256
  62.7 3.1 %collective-permute-done.23.refs_1_ = bf16[64,2048]{1,0:T(8,128)(2,1)S(1)} collective-permute-done((bf16[64,2048]{1,0:T(8,128)(2,1)S(1)}, bf16[64,2048]{1,0:T(8,128)(2,1)S(1)}, u32[]{:S(2)}, u32[]{:S(2)}) %collective-permute-start.23) | collective-permute-done | bytes 262176 | tf_op jit(solution)/shard_map/ppermute | solution.py:256
  66.3 2.3 %collective-permute-done.22.refs_0_ = bf16[64,2048]{1,0:T(8,128)(2,1)S(1)} collective-permute-done((bf16[64,2048]{1,0:T(8,128)(2,1)S(1)}, bf16[64,2048]{1,0:T(8,128)(2,1)S(1)}, u32[]{:S(2)}, u32[]{:S(2)}) %collective-permute-start.22) | collective-permute-done | bytes 262176 | tf_op jit(solution)/shard_map/ppermute | solution.py:256
  70.0 2.2 %collective-permute-done.26.refs_1_ = bf16[64,2048]{1,0:T(8,128)(2,1)S(1)} collective-permute-done((bf16[64,2048]{1,0:T(8,128)(2,1)S(1)}, bf16[64,2048]{1,0:T(8,128)(2,1)S(1)}, u32[]{:S(2)}, u32[]{:S(2)}) %collective-permute-start.26) | collective-permute-done | bytes 262176 | tf_op jit(solution)/shard_map/ppermute | solution.py:256
  72.7 2.3 %collective-permute-done.25.refs_0_ = bf16[64,2048]{1,0:T(8,128)(2,1)S(1)} collective-permute-done((bf16[64,2048]{1,0:T(8,128)(2,1)S(1)}, bf16[64,2048]{1,0:T(8,128)(2,1)S(1)}, u32[]{:S(2)}, u32[]{:S(2)}) %collective-permute-start.25) | collective-permute-done | bytes 262176 | tf_op jit(solution)/shard_map/ppermute | solution.py:256
  75.5 2.0 %experts.8 = (bf16[64,2048]{1,0:T(8,128)(2,1)S(1)}, bf16[64,2048]{1,0:T(8,128)(2,1)S(1)}) custom-call(f32[8,8,128]{2,1,0:T(8,128)S(1)} %shares.1.w_ref, bf16[2048,512]{1,0:T(8,128)(2,1)S(1)} %get-tuple-element.44.after_ref.g0, bf16[2048,512]{1,0:T(8,128)(2,1)S(1)} %get-tuple-element.55.u0, bf16[512,2048]{1,0:T(8,128)(2,1)S(1)} %get-tuple-element.56.d0, ...), custom_call_target="tpu_custom_call" | custom-call | flops 1610612736 | bytes 1048576 | tf_op jit(solution)/shard_map/experts/pallas_call | solution.py:182
  79.4 2.0 %collective-permute-start.31 = (bf16[64,2048]{1,0:T(8,128)(2,1)S(1)}, bf16[64,2048]{1,0:T(8,128)(2,1)S(1)}, u32[]{:S(2)}, u32[]{:S(2)}) collective-permute-start(bf16[64,2048]{1,0:T(8,128)(2,1)S(1)} %get-tuple-element.66), channel_id=1, source_target_pairs={{0,4},{1,3},{4,8},{5,1},{8,12},{9,5},{12,14},{13,9},{14,10},{15,13... | collective-permute-start | bytes 786440 | tf_op jit(solution)/shard_map/ppermute | solution.py:256
  81.5 2.0 %experts.9 = (bf16[64,2048]{1,0:T(8,128)(2,1)S(1)}, bf16[64,2048]{1,0:T(8,128)(2,1)S(1)}) custom-call(f32[8,8,128]{2,1,0:T(8,128)S(1)} %shares.1.w_ref, bf16[2048,512]{1,0:T(8,128)(2,1)S(1)} %get-tuple-element.44.after_ref.g0, bf16[2048,512]{1,0:T(8,128)(2,1)S(1)} %get-tuple-element.55.u0, bf16[512,2048]{1,0:T(8,128)(2,1)S(1)} %get-tuple-element.56.d0, ...), custom_call_target="tpu_custom_call" | custom-call | flops 1610612736 | bytes 1048576 | tf_op jit(solution)/shard_map/experts/pallas_call | solution.py:182
  85.5 2.0 %experts.11 = (bf16[64,2048]{1,0:T(8,128)(2,1)S(1)}, bf16[64,2048]{1,0:T(8,128)(2,1)S(1)}) custom-call(f32[8,8,128]{2,1,0:T(8,128)S(1)} %shares.1.w_ref, bf16[2048,512]{1,0:T(8,128)(2,1)S(1)} %get-tuple-element.44.after_ref.g0, bf16[2048,512]{1,0:T(8,128)(2,1)S(1)} %get-tuple-element.55.u0, bf16[512,2048]{1,0:T(8,128)(2,1)S(1)} %get-tuple-element.56.d0, ...), custom_call_target="tpu_custom_call" | custom-call | flops 1610612736 | bytes 1048576 | tf_op jit(solution)/shard_map/experts/pallas_call | solution.py:182
  87.5 2.0 %experts.12 = (bf16[64,2048]{1,0:T(8,128)(2,1)S(1)}, bf16[64,2048]{1,0:T(8,128)(2,1)S(1)}) custom-call(f32[8,8,128]{2,1,0:T(8,128)S(1)} %shares.1.w_ref, bf16[2048,512]{1,0:T(8,128)(2,1)S(1)} %get-tuple-element.44.after_ref.g0, bf16[2048,512]{1,0:T(8,128)(2,1)S(1)} %get-tuple-element.55.u0, bf16[512,2048]{1,0:T(8,128)(2,1)S(1)} %get-tuple-element.56.d0, ...), custom_call_target="tpu_custom_call" | custom-call | flops 1610612736 | bytes 1048576 | tf_op jit(solution)/shard_map/experts/pallas_call | solution.py:182
  91.5 2.0 %experts.15 = (bf16[64,2048]{1,0:T(8,128)(2,1)S(1)}, bf16[64,2048]{1,0:T(8,128)(2,1)S(1)}) custom-call(f32[8,8,128]{2,1,0:T(8,128)S(1)} %shares.1.w_ref, bf16[2048,512]{1,0:T(8,128)(2,1)S(1)} %get-tuple-element.44.after_ref.g0, bf16[2048,512]{1,0:T(8,128)(2,1)S(1)} %get-tuple-element.55.u0, bf16[512,2048]{1,0:T(8,128)(2,1)S(1)} %get-tuple-element.56.d0, ...), custom_call_target="tpu_custom_call" | custom-call | flops 1610612736 | bytes 1048576 | tf_op jit(solution)/shard_map/experts/pallas_call | solution.py:182
  93.5 2.2 %experts.14 = (bf16[64,2048]{1,0:T(8,128)(2,1)S(1)}, bf16[64,2048]{1,0:T(8,128)(2,1)S(1)}) custom-call(f32[8,8,128]{2,1,0:T(8,128)S(1)} %shares.1.w_ref, bf16[2048,512]{1,0:T(8,128)(2,1)S(1)} %get-tuple-element.44.after_ref.g0, bf16[2048,512]{1,0:T(8,128)(2,1)S(1)} %get-tuple-element.55.u0, bf16[512,2048]{1,0:T(8,128)(2,1)S(1)} %get-tuple-element.56.d0, ...), custom_call_target="tpu_custom_call" | custom-call | flops 1610612736 | bytes 1048576 | tf_op jit(solution)/shard_map/experts/pallas_call | solution.py:182
  97.7 4.6 %collective-permute-done.15 = bf16[64,2048]{1,0:T(8,128)(2,1)S(1)} collective-permute-done((bf16[64,2048]{1,0:T(8,128)(2,1)S(1)}, bf16[64,2048]{1,0:T(8,128)(2,1)S(1)}, u32[]{:S(2)}, u32[]{:S(2)}) %collective-permute-start.15) | collective-permute-done | bytes 262176 | tf_op jit(solution)/shard_map/ppermute | solution.py:256
  106.7 2.1 %collective-permute-done.18 = bf16[64,2048]{1,0:T(8,128)(2,1)S(1)} collective-permute-done((bf16[64,2048]{1,0:T(8,128)(2,1)S(1)}, bf16[64,2048]{1,0:T(8,128)(2,1)S(1)}, u32[]{:S(2)}, u32[]{:S(2)}) %collective-permute-start.18) | collective-permute-done | bytes 262176 | tf_op jit(solution)/shard_map/ppermute | solution.py:256
  113.2 2.1 %collective-permute-done.21 = bf16[64,2048]{1,0:T(8,128)(2,1)S(1)} collective-permute-done((bf16[64,2048]{1,0:T(8,128)(2,1)S(1)}, bf16[64,2048]{1,0:T(8,128)(2,1)S(1)}, u32[]{:S(2)}, u32[]{:S(2)}) %collective-permute-start.21) | collective-permute-done | bytes 262176 | tf_op jit(solution)/shard_map/ppermute | solution.py:256
  119.7 2.1 %collective-permute-done.24 = bf16[64,2048]{1,0:T(8,128)(2,1)S(1)} collective-permute-done((bf16[64,2048]{1,0:T(8,128)(2,1)S(1)}, bf16[64,2048]{1,0:T(8,128)(2,1)S(1)}, u32[]{:S(2)}, u32[]{:S(2)}) %collective-permute-start.24) | collective-permute-done | bytes 262176 | tf_op jit(solution)/shard_map/ppermute | solution.py:256
  126.2 2.1 %collective-permute-done.27 = bf16[64,2048]{1,0:T(8,128)(2,1)S(1)} collective-permute-done((bf16[64,2048]{1,0:T(8,128)(2,1)S(1)}, bf16[64,2048]{1,0:T(8,128)(2,1)S(1)}, u32[]{:S(2)}, u32[]{:S(2)}) %collective-permute-start.27) | collective-permute-done | bytes 262176 | tf_op jit(solution)/shard_map/ppermute | solution.py:256
  132.6 2.1 %collective-permute-done.30 = bf16[64,2048]{1,0:T(8,128)(2,1)S(1)} collective-permute-done((bf16[64,2048]{1,0:T(8,128)(2,1)S(1)}, bf16[64,2048]{1,0:T(8,128)(2,1)S(1)}, u32[]{:S(2)}, u32[]{:S(2)}) %collective-permute-start.30) | collective-permute-done | bytes 262176 | tf_op jit(solution)/shard_map/ppermute | solution.py:256
  134.8 2.7 %collective-permute-done.37 = bf16[64,2048]{1,0:T(8,128)(2,1)S(1)} collective-permute-done((bf16[64,2048]{1,0:T(8,128)(2,1)S(1)}, bf16[64,2048]{1,0:T(8,128)(2,1)S(1)}, u32[]{:S(2)}, u32[]{:S(2)}) %collective-permute-start.37) | collective-permute-done | bytes 262176 | tf_op jit(solution)/shard_map/ppermute | solution.py:256
  (77 shorter events, 54.2 us)
Async XLA Ops:
  2.3 8.1 %collective-permute-start = (bf16[528,128]{1,0:T(8,128)(2,1)S(1)}, bf16[528,128]{1,0:T(8,128)(2,1)S(1)}, u32[]{:S(2)}, u32[]{:S(2)}) collective-permute-start(bf16[528,128]{1,0:T(8,128)(2,1)S(1)} %get-tuple-element.45), channel_id=1, source_target_pairs={{0,2},{2,0},{4,6},{6,4},{8,10},{10,8},{12,14},{14,12},{1,3},{3,1},... | collective-permute-start | bytes 405512 | tf_op jit(solution)/shard_map/ppermute | solution.py:262
  5.4 6.5 %collective-permute-start.1 = (bf16[528,128]{1,0:T(8,128)(2,1)S(1)}, bf16[528,128]{1,0:T(8,128)(2,1)S(1)}, u32[]{:S(2)}, u32[]{:S(2)}) collective-permute-start(bf16[528,128]{1,0:T(8,128)(2,1)S(1)} %get-tuple-element.46), channel_id=1, source_target_pairs={{0,4},{2,6},{4,0},{6,2},{8,12},{10,14},{12,8},{14,10},{1,5},{3,7},... | collective-permute-start | bytes 405512 | tf_op jit(solution)/shard_map/ppermute | solution.py:262
  9.9 65.6 %collective-permute-start.7 = (bf16[2048,512]{1,0:T(8,128)(2,1)S(1)}, bf16[2048,512]{1,0:T(8,128)(2,1)S(1)}, u32[]{:S(2)}, u32[]{:S(2)}) collective-permute-start(bf16[2048,512]{1,0:T(8,128)(2,1)S(1)} %get-tuple-element.44.after_ref.g0), channel_id=1, source_target_pairs={{0,1},{1,0},{2,3},{3,2},{4,5},{5,4},{6,7},{7,6},{8,9},{9,8},{10,11... | collective-permute-start | bytes 6291464 | tf_op jit(solution)/shard_map/ppermute | solution.py:297
  9.9 65.6 %collective-permute-start.8 = (bf16[2048,512]{1,0:T(8,128)(2,1)S(1)}, bf16[2048,512]{1,0:T(8,128)(2,1)S(1)}, u32[]{:S(2)}, u32[]{:S(2)}) collective-permute-start(bf16[2048,512]{1,0:T(8,128)(2,1)S(1)} %get-tuple-element.55.u0), channel_id=1, source_target_pairs={{0,1},{1,0},{2,3},{3,2},{4,5},{5,4},{6,7},{7,6},{8,9},{9,8},{10,11... | collective-permute-start | bytes 6291464 | tf_op jit(solution)/shard_map/ppermute | solution.py:297
  10.4 65.1 %collective-permute-start.9 = (bf16[512,2048]{1,0:T(8,128)(2,1)S(1)}, bf16[512,2048]{1,0:T(8,128)(2,1)S(1)}, u32[]{:S(2)}, u32[]{:S(2)}) collective-permute-start(bf16[512,2048]{1,0:T(8,128)(2,1)S(1)} %get-tuple-element.56.d0), channel_id=1, source_target_pairs={{0,1},{1,0},{2,3},{3,2},{4,5},{5,4},{6,7},{7,6},{8,9},{9,8},{10,11... | collective-permute-start | bytes 6291464 | tf_op jit(solution)/shard_map/ppermute | solution.py:297
  13.2 8.5 %collective-permute-start.3 = (bf16[528,128]{1,0:T(8,128)(2,1)S(1)}, bf16[528,128]{1,0:T(8,128)(2,1)S(1)}, u32[]{:S(2)}, u32[]{:S(2)}) collective-permute-start(bf16[528,128]{1,0:T(8,128)(2,1)S(1)} %total.1), channel_id=1, source_target_pairs={{0,8},{2,10},{4,12},{6,14},{8,0},{10,2},{12,4},{14,6},{1,9},{3,11}... | collective-permute-start | bytes 405512 | tf_op jit(solution)/shard_map/ppermute | solution.py:307
  33.9 6.4 %collective-permute-start.11 = (bf16[64,2048]{1,0:T(8,128)(2,1)S(1)}, bf16[64,2048]{1,0:T(8,128)(2,1)S(1)}, u32[]{:S(2)}, u32[]{:S(2)}) collective-permute-start(bf16[64,2048]{1,0:T(8,128)(2,1)S(1)} %get-tuple-element.57.refs_1_), channel_id=1, source_target_pairs={{0,4},{1,3},{4,8},{5,1},{8,12},{9,5},{12,14},{13,9},{14,10},{15,13... | collective-permute-start | bytes 786440 | tf_op jit(solution)/shard_map/ppermute | solution.py:256
  34.4 8.7 %collective-permute-start.10 = (bf16[64,2048]{1,0:T(8,128)(2,1)S(1)}, bf16[64,2048]{1,0:T(8,128)(2,1)S(1)}, u32[]{:S(2)}, u32[]{:S(2)}) collective-permute-start(bf16[64,2048]{1,0:T(8,128)(2,1)S(1)} %get-tuple-element.53.after_ref.refs_0_), channel_id=1, source_target_pairs={{0,4},{1,3},{4,8},{5,1},{8,12},{9,5},{12,14},{13,9},{14,10},{15,13... | collective-permute-start | bytes 786440 | tf_op jit(solution)/shard_map/ppermute | solution.py:256
  40.3 6.4 %collective-permute-start.14 = (bf16[64,2048]{1,0:T(8,128)(2,1)S(1)}, bf16[64,2048]{1,0:T(8,128)(2,1)S(1)}, u32[]{:S(2)}, u32[]{:S(2)}) collective-permute-start(bf16[64,2048]{1,0:T(8,128)(2,1)S(1)} %collective-permute-done.11.refs_1_), channel_id=1, source_target_pairs={{0,4},{1,3},{4,8},{5,1},{8,12},{9,5},{12,14},{13,9},{14,10},{15,13... | collective-permute-start | bytes 786440 | tf_op jit(solution)/shard_map/ppermute | solution.py:256
  43.1 6.4 %collective-permute-start.13 = (bf16[64,2048]{1,0:T(8,128)(2,1)S(1)}, bf16[64,2048]{1,0:T(8,128)(2,1)S(1)}, u32[]{:S(2)}, u32[]{:S(2)}) collective-permute-start(bf16[64,2048]{1,0:T(8,128)(2,1)S(1)} %collective-permute-done.10.refs_0_), channel_id=1, source_target_pairs={{0,4},{1,3},{4,8},{5,1},{8,12},{9,5},{12,14},{13,9},{14,10},{15,13... | collective-permute-start | bytes 786440 | tf_op jit(solution)/shard_map/ppermute | solution.py:256
  46.7 6.4 %collective-permute-start.17 = (bf16[64,2048]{1,0:T(8,128)(2,1)S(1)}, bf16[64,2048]{1,0:T(8,128)(2,1)S(1)}, u32[]{:S(2)}, u32[]{:S(2)}) collective-permute-start(bf16[64,2048]{1,0:T(8,128)(2,1)S(1)} %collective-permute-done.14.refs_1_), channel_id=1, source_target_pairs={{0,4},{1,3},{4,8},{5,1},{8,12},{9,5},{12,14},{13,9},{14,10},{15,13... | collective-permute-start | bytes 786440 | tf_op jit(solution)/shard_map/ppermute | solution.py:256
  49.5 6.4 %collective-permute-start.16 = (bf16[64,2048]{1,0:T(8,128)(2,1)S(1)}, bf16[64,2048]{1,0:T(8,128)(2,1)S(1)}, u32[]{:S(2)}, u32[]{:S(2)}) collective-permute-start(bf16[64,2048]{1,0:T(8,128)(2,1)S(1)} %collective-permute-done.13.refs_0_), channel_id=1, source_target_pairs={{0,4},{1,3},{4,8},{5,1},{8,12},{9,5},{12,14},{13,9},{14,10},{15,13... | collective-permute-start | bytes 786440 | tf_op jit(solution)/shard_map/ppermute | solution.py:256
  53.1 6.4 %collective-permute-start.20 = (bf16[64,2048]{1,0:T(8,128)(2,1)S(1)}, bf16[64,2048]{1,0:T(8,128)(2,1)S(1)}, u32[]{:S(2)}, u32[]{:S(2)}) collective-permute-start(bf16[64,2048]{1,0:T(8,128)(2,1)S(1)} %collective-permute-done.17.refs_1_), channel_id=1, source_target_pairs={{0,4},{1,3},{4,8},{5,1},{8,12},{9,5},{12,14},{13,9},{14,10},{15,13... | collective-permute-start | bytes 786440 | tf_op jit(solution)/shard_map/ppermute | solution.py:256
  55.9 6.4 %collective-permute-start.19 = (bf16[64,2048]{1,0:T(8,128)(2,1)S(1)}, bf16[64,2048]{1,0:T(8,128)(2,1)S(1)}, u32[]{:S(2)}, u32[]{:S(2)}) collective-permute-start(bf16[64,2048]{1,0:T(8,128)(2,1)S(1)} %collective-permute-done.16.refs_0_), channel_id=1, source_target_pairs={{0,4},{1,3},{4,8},{5,1},{8,12},{9,5},{12,14},{13,9},{14,10},{15,13... | collective-permute-start | bytes 786440 | tf_op jit(solution)/shard_map/ppermute | solution.py:256
  62.2 6.4 %collective-permute-start.22 = (bf16[64,2048]{1,0:T(8,128)(2,1)S(1)}, bf16[64,2048]{1,0:T(8,128)(2,1)S(1)}, u32[]{:S(2)}, u32[]{:S(2)}) collective-permute-start(bf16[64,2048]{1,0:T(8,128)(2,1)S(1)} %collective-permute-done.19.refs_0_), channel_id=1, source_target_pairs={{0,4},{1,3},{4,8},{5,1},{8,12},{9,5},{12,14},{13,9},{14,10},{15,13... | collective-permute-start | bytes 786440 | tf_op jit(solution)/shard_map/ppermute | solution.py:256
  65.8 6.4 %collective-permute-start.26 = (bf16[64,2048]{1,0:T(8,128)(2,1)S(1)}, bf16[64,2048]{1,0:T(8,128)(2,1)S(1)}, u32[]{:S(2)}, u32[]{:S(2)}) collective-permute-start(bf16[64,2048]{1,0:T(8,128)(2,1)S(1)} %collective-permute-done.23.refs_1_), channel_id=1, source_target_pairs={{0,4},{1,3},{4,8},{5,1},{8,12},{9,5},{12,14},{13,9},{14,10},{15,13... | collective-permute-start | bytes 786440 | tf_op jit(solution)/shard_map/ppermute | solution.py:256
  72.2 21.3 %collective-permute-start.29 = (bf16[64,2048]{1,0:T(8,128)(2,1)S(1)}, bf16[64,2048]{1,0:T(8,128)(2,1)S(1)}, u32[]{:S(2)}, u32[]{:S(2)}) collective-permute-start(bf16[64,2048]{1,0:T(8,128)(2,1)S(1)} %collective-permute-done.26.refs_1_), channel_id=1, source_target_pairs={{0,4},{1,3},{4,8},{5,1},{8,12},{9,5},{12,14},{13,9},{14,10},{15,13... | collective-permute-start | bytes 786440 | tf_op jit(solution)/shard_map/ppermute | solution.py:256
  75.0 18.5 %collective-permute-start.28 = (bf16[64,2048]{1,0:T(8,128)(2,1)S(1)}, bf16[64,2048]{1,0:T(8,128)(2,1)S(1)}, u32[]{:S(2)}, u32[]{:S(2)}) collective-permute-start(bf16[64,2048]{1,0:T(8,128)(2,1)S(1)} %collective-permute-done.25.refs_0_), channel_id=1, source_target_pairs={{0,4},{1,3},{4,8},{5,1},{8,12},{9,5},{12,14},{13,9},{14,10},{15,13... | collective-permute-start | bytes 786440 | tf_op jit(solution)/shard_map/ppermute | solution.py:256
  77.5 18.3 %collective-permute-start.12 = (bf16[64,2048]{1,0:T(8,128)(2,1)S(1)}, bf16[64,2048]{1,0:T(8,128)(2,1)S(1)}, u32[]{:S(2)}, u32[]{:S(2)}) collective-permute-start(bf16[64,2048]{1,0:T(8,128)(2,1)S(1)} %get-tuple-element.58), channel_id=1, source_target_pairs={{0,4},{1,3},{4,8},{5,1},{8,12},{9,5},{12,14},{13,9},{14,10},{15,13... | collective-permute-start | bytes 786440 | tf_op jit(solution)/shard_map/ppermute | solution.py:256
  79.4 17.9 %collective-permute-start.31 = (bf16[64,2048]{1,0:T(8,128)(2,1)S(1)}, bf16[64,2048]{1,0:T(8,128)(2,1)S(1)}, u32[]{:S(2)}, u32[]{:S(2)}) collective-permute-start(bf16[64,2048]{1,0:T(8,128)(2,1)S(1)} %get-tuple-element.66), channel_id=1, source_target_pairs={{0,4},{1,3},{4,8},{5,1},{8,12},{9,5},{12,14},{13,9},{14,10},{15,13... | collective-permute-start | bytes 786440 | tf_op jit(solution)/shard_map/ppermute | solution.py:256
  95.8 6.4 %collective-permute-start.15 = (bf16[64,2048]{1,0:T(8,128)(2,1)S(1)}, bf16[64,2048]{1,0:T(8,128)(2,1)S(1)}, u32[]{:S(2)}, u32[]{:S(2)}) collective-permute-start(bf16[64,2048]{1,0:T(8,128)(2,1)S(1)} %add_convert_fusion.13), channel_id=1, source_target_pairs={{0,4},{1,3},{4,8},{5,1},{8,12},{9,5},{12,14},{13,9},{14,10},{15,13... | collective-permute-start | bytes 786440 | tf_op jit(solution)/shard_map/ppermute | solution.py:256
  97.4 7.6 %collective-permute-start.32 = (bf16[64,2048]{1,0:T(8,128)(2,1)S(1)}, bf16[64,2048]{1,0:T(8,128)(2,1)S(1)}, u32[]{:S(2)}, u32[]{:S(2)}) collective-permute-start(bf16[64,2048]{1,0:T(8,128)(2,1)S(1)} %add_convert_fusion.6), channel_id=1, source_target_pairs={{0,4},{1,3},{4,8},{5,1},{8,12},{9,5},{12,14},{13,9},{14,10},{15,13... | collective-permute-start | bytes 786440 | tf_op jit(solution)/shard_map/ppermute | solution.py:256
  102.3 6.4 %collective-permute-start.18 = (bf16[64,2048]{1,0:T(8,128)(2,1)S(1)}, bf16[64,2048]{1,0:T(8,128)(2,1)S(1)}, u32[]{:S(2)}, u32[]{:S(2)}) collective-permute-start(bf16[64,2048]{1,0:T(8,128)(2,1)S(1)} %add_convert_fusion.12), channel_id=1, source_target_pairs={{0,4},{1,3},{4,8},{5,1},{8,12},{9,5},{12,14},{13,9},{14,10},{15,13... | collective-permute-start | bytes 786440 | tf_op jit(solution)/shard_map/ppermute | solution.py:256
  105.1 6.4 %collective-permute-start.33 = (bf16[64,2048]{1,0:T(8,128)(2,1)S(1)}, bf16[64,2048]{1,0:T(8,128)(2,1)S(1)}, u32[]{:S(2)}, u32[]{:S(2)}) collective-permute-start(bf16[64,2048]{1,0:T(8,128)(2,1)S(1)} %add_convert_fusion.5), channel_id=1, source_target_pairs={{0,4},{1,3},{4,8},{5,1},{8,12},{9,5},{12,14},{13,9},{14,10},{15,13... | collective-permute-start | bytes 786440 | tf_op jit(solution)/shard_map/ppermute | solution.py:256
  108.8 6.4 %collective-permute-start.21 = (bf16[64,2048]{1,0:T(8,128)(2,1)S(1)}, bf16[64,2048]{1,0:T(8,128)(2,1)S(1)}, u32[]{:S(2)}, u32[]{:S(2)}) collective-permute-start(bf16[64,2048]{1,0:T(8,128)(2,1)S(1)} %add_convert_fusion.11), channel_id=1, source_target_pairs={{0,4},{1,3},{4,8},{5,1},{8,12},{9,5},{12,14},{13,9},{14,10},{15,13... | collective-permute-start | bytes 786440 | tf_op jit(solution)/shard_map/ppermute | solution.py:256
  111.6 6.4 %collective-permute-start.34 = (bf16[64,2048]{1,0:T(8,128)(2,1)S(1)}, bf16[64,2048]{1,0:T(8,128)(2,1)S(1)}, u32[]{:S(2)}, u32[]{:S(2)}) collective-permute-start(bf16[64,2048]{1,0:T(8,128)(2,1)S(1)} %add_convert_fusion.4), channel_id=1, source_target_pairs={{0,4},{1,3},{4,8},{5,1},{8,12},{9,5},{12,14},{13,9},{14,10},{15,13... | collective-permute-start | bytes 786440 | tf_op jit(solution)/shard_map/ppermute | solution.py:256
  115.3 6.4 %collective-permute-start.24 = (bf16[64,2048]{1,0:T(8,128)(2,1)S(1)}, bf16[64,2048]{1,0:T(8,128)(2,1)S(1)}, u32[]{:S(2)}, u32[]{:S(2)}) collective-permute-start(bf16[64,2048]{1,0:T(8,128)(2,1)S(1)} %add_convert_fusion.10), channel_id=1, source_target_pairs={{0,4},{1,3},{4,8},{5,1},{8,12},{9,5},{12,14},{13,9},{14,10},{15,13... | collective-permute-start | bytes 786440 | tf_op jit(solution)/shard_map/ppermute | solution.py:256
  118.1 6.4 %collective-permute-start.35 = (bf16[64,2048]{1,0:T(8,128)(2,1)S(1)}, bf16[64,2048]{1,0:T(8,128)(2,1)S(1)}, u32[]{:S(2)}, u32[]{:S(2)}) collective-permute-start(bf16[64,2048]{1,0:T(8,128)(2,1)S(1)} %add_convert_fusion.3), channel_id=1, source_target_pairs={{0,4},{1,3},{4,8},{5,1},{8,12},{9,5},{12,14},{13,9},{14,10},{15,13... | collective-permute-start | bytes 786440 | tf_op jit(solution)/shard_map/ppermute | solution.py:256
  121.8 6.4 %collective-permute-start.27 = (bf16[64,2048]{1,0:T(8,128)(2,1)S(1)}, bf16[64,2048]{1,0:T(8,128)(2,1)S(1)}, u32[]{:S(2)}, u32[]{:S(2)}) collective-permute-start(bf16[64,2048]{1,0:T(8,128)(2,1)S(1)} %add_convert_fusion.9), channel_id=1, source_target_pairs={{0,4},{1,3},{4,8},{5,1},{8,12},{9,5},{12,14},{13,9},{14,10},{15,13... | collective-permute-start | bytes 786440 | tf_op jit(solution)/shard_map/ppermute | solution.py:256
  124.6 6.4 %collective-permute-start.36 = (bf16[64,2048]{1,0:T(8,128)(2,1)S(1)}, bf16[64,2048]{1,0:T(8,128)(2,1)S(1)}, u32[]{:S(2)}, u32[]{:S(2)}) collective-permute-start(bf16[64,2048]{1,0:T(8,128)(2,1)S(1)} %add_convert_fusion.2), channel_id=1, source_target_pairs={{0,4},{1,3},{4,8},{5,1},{8,12},{9,5},{12,14},{13,9},{14,10},{15,13... | collective-permute-start | bytes 786440 | tf_op jit(solution)/shard_map/ppermute | solution.py:256
  128.3 6.4 %collective-permute-start.30 = (bf16[64,2048]{1,0:T(8,128)(2,1)S(1)}, bf16[64,2048]{1,0:T(8,128)(2,1)S(1)}, u32[]{:S(2)}, u32[]{:S(2)}) collective-permute-start(bf16[64,2048]{1,0:T(8,128)(2,1)S(1)} %add_convert_fusion.8), channel_id=1, source_target_pairs={{0,4},{1,3},{4,8},{5,1},{8,12},{9,5},{12,14},{13,9},{14,10},{15,13... | collective-permute-start | bytes 786440 | tf_op jit(solution)/shard_map/ppermute | solution.py:256
  131.1 6.4 %collective-permute-start.37 = (bf16[64,2048]{1,0:T(8,128)(2,1)S(1)}, bf16[64,2048]{1,0:T(8,128)(2,1)S(1)}, u32[]{:S(2)}, u32[]{:S(2)}) collective-permute-start(bf16[64,2048]{1,0:T(8,128)(2,1)S(1)} %add_convert_fusion.1), channel_id=1, source_target_pairs={{0,4},{1,3},{4,8},{5,1},{8,12},{9,5},{12,14},{13,9},{14,10},{15,13... | collective-permute-start | bytes 786440 | tf_op jit(solution)/shard_map/ppermute | solution.py:256
  (6 other events, 35.5 us)

commit v4 on v3

--- a/solution.py
+++ b/solution.py
@@ -9,7 +9,7 @@
 
 
 HEAD_DIM = 128
-PAD = 16
+PAD = 8
 CHUNKS = 1
 PIECES = 2
 STRIP = 32
@@ -48,7 +48,6 @@
     group, place, core = lax.div(lax.axis_index("seq"), half), lax.rem(lax.axis_index("seq"), half), lax.axis_index("expert")
     ids = ids_ref[...]
     shares = rw_ref[...] / jnp.sum(rw_ref[...], axis=0, keepdims=True)
-    zero = jnp.zeros((PAD - 8, ids.shape[1]), f32)
 
     def share_of(expert):
         return jnp.sum(jnp.where(ids == expert, shares, 0.0), axis=0, keepdims=True)
@@ -61,7 +60,7 @@
             both = jnp.concatenate([share_of(first + core), share_of(first + 1 - core)], axis=0)
             high = both.astype(bf16).astype(f32)
             rows += [high, both - high]
-        send_ref[part:, :] = jnp.concatenate(rows + [zero], axis=0).astype(bf16)
+        send_ref[part:, :] = jnp.concatenate(rows, axis=0).astype(bf16)
     for c in range(CHUNKS):
         copies[2 * c].wait()
         copies[2 * c + 1].wait()
@@ -294,7 +293,9 @@
         name="local",
     )(q, k, v)
     own = load(sends[0], *own)
-    other = [lax.ppermute(w, "expert", [(0, 1), (1, 0)]) for w in own]
+    other = []
+    for w in own:
+        other.append(lax.ppermute(w, "expert", [(0, 1), (1, 0)]))
     gots = along(sends)
     near = pl.pallas_call(
         functools.partial(total_kernel, half),

time: 139 us -> 138 us (level)
  no operation moved by 1% of the time
where the time goes in v4:
time: 138 us
  waiting for transfers between devices  69 us (50%)
  starting transfers between devices  41.1 us (30%)
  Pallas kernels  24.4 us (18%)
  other arithmetic  2.66 us (2%)
    ppermute x28, waiting for transfers between devices, hop(): return lax.ppermute(value, ('seq', 'expert'), hops)  55.7 us
    ppermute x28, starting transfers between devices, hop(): return lax.ppermute(value, ('seq', 'expert'), hops)  29.6 us
    pallas_call x8, Pallas kernels, run_experts(): pl.pallas_call(functools.partial(expert_kernel, hop), in_specs=[VMEM] * (...  16.2 us
    ppermute x6, waiting for transfers between devices, along(): moved.append(lax.ppermute(blocks[r], 'seq', pairs))  9.98 us
    ppermute x6, starting transfers between devices, along(): moved.append(lax.ppermute(blocks[r], 'seq', pairs))  8.07 us
    pallas_call x2, Pallas kernels, load(): pl.pallas_call(functools.partial(load_kernel, count), in_specs=[HBM] * (c...  4.29 us
    ppermute x1, waiting for transfers between devices, per_device(): lax.ppermute(near, 'seq', [(s, (s + half) % n_seq) for s in range(n_seq)])  3.34 us
    ppermute x1, starting transfers between devices, per_device(): lax.ppermute(near, 'seq', [(s, (s + half) % n_seq) for s in range(n_seq)])  2.8 us
  transfers between devices with their start and end apart: 38, of which 30 were waited for; matrix products, arithmetic and copies ran while one was open for 1% of the time, Pallas kernels for 16%

profile of v4, /device:TPU:0, one launch (start us, length us, event | category | flops | bytes accessed | tf_op | source)
XLA Modules:
  0.0 138.1 jit_solution(5828771513664335678)
XLA Ops:
  2.3 3.1 %collective-permute-start = (bf16[520,128]{1,0:T(8,128)(2,1)S(1)}, bf16[520,128]{1,0:T(8,128)(2,1)S(1)}, u32[]{:S(2)}, u32[]{:S(2)}) collective-permute-start(bf16[520,128]{1,0:T(8,128)(2,1)S(1)} %get-tuple-element.45), channel_id=1, source_target_pairs={{0,2},{2,0},{4,6},{6,4},{8,10},{10,8},{12,14},{14,12},{1,3},{3,1},... | collective-permute-start | bytes 399368 | tf_op jit(solution)/shard_map/ppermute | solution.py:261
  7.0 2.9 %load.3 = (bf16[2048,512]{1,0:T(8,128)(2,1)S(1)}, bf16[2048,512]{1,0:T(8,128)(2,1)S(1)}, bf16[512,2048]{1,0:T(8,128)(2,1)S(1)}) custom-call(bf16[520,128]{1,0:T(8,128)(2,1)S(1)} %get-tuple-element.38.after_ref.refs_0_, bf16[2048,512]{1,0:T(8,128)(2,1)} %bitcast.18, bf16[2048,512]{1,0:T(8,128)(2,1)} %bitcast.19, bf16[512,2048]{1,0:T(8,128)(2,1)} %bitcast.20), custom_call_target="tpu_custom_call" | custom-call | bytes 6291456 | tf_op jit(solution)/shard_map/load/pallas_call | solution.py:214
  13.1 2.8 %collective-permute-start.3 = (bf16[528,128]{1,0:T(8,128)(2,1)S(1)}, bf16[528,128]{1,0:T(8,128)(2,1)S(1)}, u32[]{:S(2)}, u32[]{:S(2)}) collective-permute-start(bf16[528,128]{1,0:T(8,128)(2,1)S(1)} %total.1), channel_id=1, source_target_pairs={{0,8},{2,10},{4,12},{6,14},{8,0},{10,2},{12,4},{14,6},{1,9},{3,11}... | collective-permute-start | bytes 405512 | tf_op jit(solution)/shard_map/ppermute | solution.py:308
  18.2 3.3 %collective-permute-done.3.far_ref = bf16[528,128]{1,0:T(8,128)(2,1)S(1)} collective-permute-done((bf16[528,128]{1,0:T(8,128)(2,1)S(1)}, bf16[528,128]{1,0:T(8,128)(2,1)S(1)}, u32[]{:S(2)}, u32[]{:S(2)}) %collective-permute-start.3) | collective-permute-done | bytes 135200 | tf_op jit(solution)/shard_map/ppermute | solution.py:308
  23.8 3.0 %collective-permute-done.4.refs_1_ = bf16[512,128]{1,0:T(8,128)(2,1)S(1)} collective-permute-done((bf16[512,128]{1,0:T(8,128)(2,1)S(1)}, bf16[512,128]{1,0:T(8,128)(2,1)S(1)}, u32[]{:S(2)}, u32[]{:S(2)}) %collective-permute-start.4) | collective-permute-done | bytes 131104 | tf_op jit(solution)/shard_map/ppermute | solution.py:261
  29.0 3.7 %collective-permute-done.6.refs_3_ = bf16[512,128]{1,0:T(8,128)(2,1)S(1)} collective-permute-done((bf16[512,128]{1,0:T(8,128)(2,1)S(1)}, bf16[512,128]{1,0:T(8,128)(2,1)S(1)}, u32[]{:S(2)}, u32[]{:S(2)}) %collective-permute-start.6) | collective-permute-done | bytes 131104 | tf_op jit(solution)/shard_map/ppermute | solution.py:261
  34.0 2.2 %collective-permute-start.10 = (bf16[64,2048]{1,0:T(8,128)(2,1)S(1)}, bf16[64,2048]{1,0:T(8,128)(2,1)S(1)}, u32[]{:S(2)}, u32[]{:S(2)}) collective-permute-start(bf16[64,2048]{1,0:T(8,128)(2,1)S(1)} %get-tuple-element.53.after_ref.refs_0_), channel_id=1, source_target_pairs={{0,4},{1,3},{4,8},{5,1},{8,12},{9,5},{12,14},{13,9},{14,10},{15,13... | collective-permute-start | bytes 786440 | tf_op jit(solution)/shard_map/ppermute | solution.py:255
  36.2 4.0 %collective-permute-done.11.refs_1_ = bf16[64,2048]{1,0:T(8,128)(2,1)S(1)} collective-permute-done((bf16[64,2048]{1,0:T(8,128)(2,1)S(1)}, bf16[64,2048]{1,0:T(8,128)(2,1)S(1)}, u32[]{:S(2)}, u32[]{:S(2)}) %collective-permute-start.11) | collective-permute-done | bytes 262176 | tf_op jit(solution)/shard_map/ppermute | solution.py:255
  40.4 2.6 %collective-permute-done.10.refs_0_ = bf16[64,2048]{1,0:T(8,128)(2,1)S(1)} collective-permute-done((bf16[64,2048]{1,0:T(8,128)(2,1)S(1)}, bf16[64,2048]{1,0:T(8,128)(2,1)S(1)}, u32[]{:S(2)}, u32[]{:S(2)}) %collective-permute-start.10) | collective-permute-done | bytes 262176 | tf_op jit(solution)/shard_map/ppermute | solution.py:255
  43.2 3.3 %collective-permute-done.14.refs_1_ = bf16[64,2048]{1,0:T(8,128)(2,1)S(1)} collective-permute-done((bf16[64,2048]{1,0:T(8,128)(2,1)S(1)}, bf16[64,2048]{1,0:T(8,128)(2,1)S(1)}, u32[]{:S(2)}, u32[]{:S(2)}) %collective-permute-start.14) | collective-permute-done | bytes 262176 | tf_op jit(solution)/shard_map/ppermute | solution.py:255
  46.8 2.6 %collective-permute-done.13.refs_0_ = bf16[64,2048]{1,0:T(8,128)(2,1)S(1)} collective-permute-done((bf16[64,2048]{1,0:T(8,128)(2,1)S(1)}, bf16[64,2048]{1,0:T(8,128)(2,1)S(1)}, u32[]{:S(2)}, u32[]{:S(2)}) %collective-permute-start.13) | collective-permute-done | bytes 262176 | tf_op jit(solution)/shard_map/ppermute | solution.py:255
  49.6 3.3 %collective-permute-done.17.refs_1_ = bf16[64,2048]{1,0:T(8,128)(2,1)S(1)} collective-permute-done((bf16[64,2048]{1,0:T(8,128)(2,1)S(1)}, bf16[64,2048]{1,0:T(8,128)(2,1)S(1)}, u32[]{:S(2)}, u32[]{:S(2)}) %collective-permute-start.17) | collective-permute-done | bytes 262176 | tf_op jit(solution)/shard_map/ppermute | solution.py:255
  53.2 2.6 %collective-permute-done.16.refs_0_ = bf16[64,2048]{1,0:T(8,128)(2,1)S(1)} collective-permute-done((bf16[64,2048]{1,0:T(8,128)(2,1)S(1)}, bf16[64,2048]{1,0:T(8,128)(2,1)S(1)}, u32[]{:S(2)}, u32[]{:S(2)}) %collective-permute-start.16) | collective-permute-done | bytes 262176 | tf_op jit(solution)/shard_map/ppermute | solution.py:255
  56.0 3.3 %collective-permute-done.20.refs_1_ = bf16[64,2048]{1,0:T(8,128)(2,1)S(1)} collective-permute-done((bf16[64,2048]{1,0:T(8,128)(2,1)S(1)}, bf16[64,2048]{1,0:T(8,128)(2,1)S(1)}, u32[]{:S(2)}, u32[]{:S(2)}) %collective-permute-start.20) | collective-permute-done | bytes 262176 | tf_op jit(solution)/shard_map/ppermute | solution.py:255
  59.5 2.6 %collective-permute-done.19.refs_0_ = bf16[64,2048]{1,0:T(8,128)(2,1)S(1)} collective-permute-done((bf16[64,2048]{1,0:T(8,128)(2,1)S(1)}, bf16[64,2048]{1,0:T(8,128)(2,1)S(1)}, u32[]{:S(2)}, u32[]{:S(2)}) %collective-permute-start.19) | collective-permute-done | bytes 262176 | tf_op jit(solution)/shard_map/ppermute | solution.py:255
  62.3 3.3 %collective-permute-done.23.refs_1_ = bf16[64,2048]{1,0:T(8,128)(2,1)S(1)} collective-permute-done((bf16[64,2048]{1,0:T(8,128)(2,1)S(1)}, bf16[64,2048]{1,0:T(8,128)(2,1)S(1)}, u32[]{:S(2)}, u32[]{:S(2)}) %collective-permute-start.23) | collective-permute-done | bytes 262176 | tf_op jit(solution)/shard_map/ppermute | solution.py:255
  65.9 2.6 %collective-permute-done.22.refs_0_ = bf16[64,2048]{1,0:T(8,128)(2,1)S(1)} collective-permute-done((bf16[64,2048]{1,0:T(8,128)(2,1)S(1)}, bf16[64,2048]{1,0:T(8,128)(2,1)S(1)}, u32[]{:S(2)}, u32[]{:S(2)}) %collective-permute-start.22) | collective-permute-done | bytes 262176 | tf_op jit(solution)/shard_map/ppermute | solution.py:255
  69.6 2.5 %collective-permute-done.26.refs_1_ = bf16[64,2048]{1,0:T(8,128)(2,1)S(1)} collective-permute-done((bf16[64,2048]{1,0:T(8,128)(2,1)S(1)}, bf16[64,2048]{1,0:T(8,128)(2,1)S(1)}, u32[]{:S(2)}, u32[]{:S(2)}) %collective-permute-start.26) | collective-permute-done | bytes 262176 | tf_op jit(solution)/shard_map/ppermute | solution.py:255
  72.3 2.6 %collective-permute-done.25.refs_0_ = bf16[64,2048]{1,0:T(8,128)(2,1)S(1)} collective-permute-done((bf16[64,2048]{1,0:T(8,128)(2,1)S(1)}, bf16[64,2048]{1,0:T(8,128)(2,1)S(1)}, u32[]{:S(2)}, u32[]{:S(2)}) %collective-permute-start.25) | collective-permute-done | bytes 262176 | tf_op jit(solution)/shard_map/ppermute | solution.py:255
  75.1 2.0 %experts.8 = (bf16[64,2048]{1,0:T(8,128)(2,1)S(1)}, bf16[64,2048]{1,0:T(8,128)(2,1)S(1)}) custom-call(f32[8,8,128]{2,1,0:T(8,128)S(1)} %shares.1.w_ref, bf16[2048,512]{1,0:T(8,128)(2,1)S(1)} %get-tuple-element.44.after_ref.g0, bf16[2048,512]{1,0:T(8,128)(2,1)S(1)} %get-tuple-element.55.u0, bf16[512,2048]{1,0:T(8,128)(2,1)S(1)} %get-tuple-element.56.d0, ...), custom_call_target="tpu_custom_call" | custom-call | flops 1610612736 | bytes 1048576 | tf_op jit(solution)/shard_map/experts/pallas_call | solution.py:181
  77.1 2.2 %collective-permute-start.12 = (bf16[64,2048]{1,0:T(8,128)(2,1)S(1)}, bf16[64,2048]{1,0:T(8,128)(2,1)S(1)}, u32[]{:S(2)}, u32[]{:S(2)}) collective-permute-start(bf16[64,2048]{1,0:T(8,128)(2,1)S(1)} %get-tuple-element.58), channel_id=1, source_target_pairs={{0,4},{1,3},{4,8},{5,1},{8,12},{9,5},{12,14},{13,9},{14,10},{15,13... | collective-permute-start | bytes 786440 | tf_op jit(solution)/shard_map/ppermute | solution.py:255
  81.1 2.0 %experts.9 = (bf16[64,2048]{1,0:T(8,128)(2,1)S(1)}, bf16[64,2048]{1,0:T(8,128)(2,1)S(1)}) custom-call(f32[8,8,128]{2,1,0:T(8,128)S(1)} %shares.1.w_ref, bf16[2048,512]{1,0:T(8,128)(2,1)S(1)} %get-tuple-element.44.after_ref.g0, bf16[2048,512]{1,0:T(8,128)(2,1)S(1)} %get-tuple-element.55.u0, bf16[512,2048]{1,0:T(8,128)(2,1)S(1)} %get-tuple-element.56.d0, ...), custom_call_target="tpu_custom_call" | custom-call | flops 1610612736 | bytes 1048576 | tf_op jit(solution)/shard_map/experts/pallas_call | solution.py:181
  83.1 2.0 %experts.10 = (bf16[64,2048]{1,0:T(8,128)(2,1)S(1)}, bf16[64,2048]{1,0:T(8,128)(2,1)S(1)}) custom-call(f32[8,8,128]{2,1,0:T(8,128)S(1)} %shares.1.w_ref, bf16[2048,512]{1,0:T(8,128)(2,1)S(1)} %get-tuple-element.44.after_ref.g0, bf16[2048,512]{1,0:T(8,128)(2,1)S(1)} %get-tuple-element.55.u0, bf16[512,2048]{1,0:T(8,128)(2,1)S(1)} %get-tuple-element.56.d0, ...), custom_call_target="tpu_custom_call" | custom-call | flops 1610612736 | bytes 1048576 | tf_op jit(solution)/shard_map/experts/pallas_call | solution.py:181
  85.1 2.0 %experts.11 = (bf16[64,2048]{1,0:T(8,128)(2,1)S(1)}, bf16[64,2048]{1,0:T(8,128)(2,1)S(1)}) custom-call(f32[8,8,128]{2,1,0:T(8,128)S(1)} %shares.1.w_ref, bf16[2048,512]{1,0:T(8,128)(2,1)S(1)} %get-tuple-element.44.after_ref.g0, bf16[2048,512]{1,0:T(8,128)(2,1)S(1)} %get-tuple-element.55.u0, bf16[512,2048]{1,0:T(8,128)(2,1)S(1)} %get-tuple-element.56.d0, ...), custom_call_target="tpu_custom_call" | custom-call | flops 1610612736 | bytes 1048576 | tf_op jit(solution)/shard_map/experts/pallas_call | solution.py:181
  87.1 2.0 %experts.12 = (bf16[64,2048]{1,0:T(8,128)(2,1)S(1)}, bf16[64,2048]{1,0:T(8,128)(2,1)S(1)}) custom-call(f32[8,8,128]{2,1,0:T(8,128)S(1)} %shares.1.w_ref, bf16[2048,512]{1,0:T(8,128)(2,1)S(1)} %get-tuple-element.44.after_ref.g0, bf16[2048,512]{1,0:T(8,128)(2,1)S(1)} %get-tuple-element.55.u0, bf16[512,2048]{1,0:T(8,128)(2,1)S(1)} %get-tuple-element.56.d0, ...), custom_call_target="tpu_custom_call" | custom-call | flops 1610612736 | bytes 1048576 | tf_op jit(solution)/shard_map/experts/pallas_call | solution.py:181
  89.1 2.0 %experts.13 = (bf16[64,2048]{1,0:T(8,128)(2,1)S(1)}, bf16[64,2048]{1,0:T(8,128)(2,1)S(1)}) custom-call(f32[8,8,128]{2,1,0:T(8,128)S(1)} %shares.1.w_ref, bf16[2048,512]{1,0:T(8,128)(2,1)S(1)} %get-tuple-element.44.after_ref.g0, bf16[2048,512]{1,0:T(8,128)(2,1)S(1)} %get-tuple-element.55.u0, bf16[512,2048]{1,0:T(8,128)(2,1)S(1)} %get-tuple-element.56.d0, ...), custom_call_target="tpu_custom_call" | custom-call | flops 1610612736 | bytes 1048576 | tf_op jit(solution)/shard_map/experts/pallas_call | solution.py:181
  91.1 2.0 %experts.15 = (bf16[64,2048]{1,0:T(8,128)(2,1)S(1)}, bf16[64,2048]{1,0:T(8,128)(2,1)S(1)}) custom-call(f32[8,8,128]{2,1,0:T(8,128)S(1)} %shares.1.w_ref, bf16[2048,512]{1,0:T(8,128)(2,1)S(1)} %get-tuple-element.44.after_ref.g0, bf16[2048,512]{1,0:T(8,128)(2,1)S(1)} %get-tuple-element.55.u0, bf16[512,2048]{1,0:T(8,128)(2,1)S(1)} %get-tuple-element.56.d0, ...), custom_call_target="tpu_custom_call" | custom-call | flops 1610612736 | bytes 1048576 | tf_op jit(solution)/shard_map/experts/pallas_call | solution.py:181
  93.1 2.2 %experts.14 = (bf16[64,2048]{1,0:T(8,128)(2,1)S(1)}, bf16[64,2048]{1,0:T(8,128)(2,1)S(1)}) custom-call(f32[8,8,128]{2,1,0:T(8,128)S(1)} %shares.1.w_ref, bf16[2048,512]{1,0:T(8,128)(2,1)S(1)} %get-tuple-element.44.after_ref.g0, bf16[2048,512]{1,0:T(8,128)(2,1)S(1)} %get-tuple-element.55.u0, bf16[512,2048]{1,0:T(8,128)(2,1)S(1)} %get-tuple-element.56.d0, ...), custom_call_target="tpu_custom_call" | custom-call | flops 1610612736 | bytes 1048576 | tf_op jit(solution)/shard_map/experts/pallas_call | solution.py:181
  95.5 1.8 %collective-permute-start.15 = (bf16[64,2048]{1,0:T(8,128)(2,1)S(1)}, bf16[64,2048]{1,0:T(8,128)(2,1)S(1)}, u32[]{:S(2)}, u32[]{:S(2)}) collective-permute-start(bf16[64,2048]{1,0:T(8,128)(2,1)S(1)} %add_convert_fusion.13), channel_id=1, source_target_pairs={{0,4},{1,3},{4,8},{5,1},{8,12},{9,5},{12,14},{13,9},{14,10},{15,13... | collective-permute-start | bytes 786440 | tf_op jit(solution)/shard_map/ppermute | solution.py:255
  97.6 4.3 %collective-permute-done.15 = bf16[64,2048]{1,0:T(8,128)(2,1)S(1)} collective-permute-done((bf16[64,2048]{1,0:T(8,128)(2,1)S(1)}, bf16[64,2048]{1,0:T(8,128)(2,1)S(1)}, u32[]{:S(2)}, u32[]{:S(2)}) %collective-permute-start.15) | collective-permute-done | bytes 262176 | tf_op jit(solution)/shard_map/ppermute | solution.py:255
  102.0 1.8 %collective-permute-start.18 = (bf16[64,2048]{1,0:T(8,128)(2,1)S(1)}, bf16[64,2048]{1,0:T(8,128)(2,1)S(1)}, u32[]{:S(2)}, u32[]{:S(2)}) collective-permute-start(bf16[64,2048]{1,0:T(8,128)(2,1)S(1)} %add_convert_fusion.12), channel_id=1, source_target_pairs={{0,4},{1,3},{4,8},{5,1},{8,12},{9,5},{12,14},{13,9},{14,10},{15,13... | collective-permute-start | bytes 786440 | tf_op jit(solution)/shard_map/ppermute | solution.py:255
  134.5 2.7 %collective-permute-done.37 = bf16[64,2048]{1,0:T(8,128)(2,1)S(1)} collective-permute-done((bf16[64,2048]{1,0:T(8,128)(2,1)S(1)}, bf16[64,2048]{1,0:T(8,128)(2,1)S(1)}, u32[]{:S(2)}, u32[]{:S(2)}) %collective-permute-start.37) | collective-permute-done | bytes 262176 | tf_op jit(solution)/shard_map/ppermute | solution.py:255
  (77 shorter events, 52.0 us)
Async XLA Ops:
  2.3 8.1 %collective-permute-start = (bf16[520,128]{1,0:T(8,128)(2,1)S(1)}, bf16[520,128]{1,0:T(8,128)(2,1)S(1)}, u32[]{:S(2)}, u32[]{:S(2)}) collective-permute-start(bf16[520,128]{1,0:T(8,128)(2,1)S(1)} %get-tuple-element.45), channel_id=1, source_target_pairs={{0,2},{2,0},{4,6},{6,4},{8,10},{10,8},{12,14},{14,12},{1,3},{3,1},... | collective-permute-start | bytes 399368 | tf_op jit(solution)/shard_map/ppermute | solution.py:261
  5.4 6.4 %collective-permute-start.1 = (bf16[520,128]{1,0:T(8,128)(2,1)S(1)}, bf16[520,128]{1,0:T(8,128)(2,1)S(1)}, u32[]{:S(2)}, u32[]{:S(2)}) collective-permute-start(bf16[520,128]{1,0:T(8,128)(2,1)S(1)} %get-tuple-element.46), channel_id=1, source_target_pairs={{0,4},{2,6},{4,0},{6,2},{8,12},{10,14},{12,8},{14,10},{1,5},{3,7},... | collective-permute-start | bytes 399368 | tf_op jit(solution)/shard_map/ppermute | solution.py:261
  9.9 65.2 %collective-permute-start.7 = (bf16[2048,512]{1,0:T(8,128)(2,1)S(1)}, bf16[2048,512]{1,0:T(8,128)(2,1)S(1)}, u32[]{:S(2)}, u32[]{:S(2)}) collective-permute-start(bf16[2048,512]{1,0:T(8,128)(2,1)S(1)} %get-tuple-element.44.after_ref.g0), channel_id=1, source_target_pairs={{0,1},{1,0},{2,3},{3,2},{4,5},{5,4},{6,7},{7,6},{8,9},{9,8},{10,11... | collective-permute-start | bytes 6291464 | tf_op jit(solution)/shard_map/ppermute | solution.py:298
  9.9 65.2 %collective-permute-start.8 = (bf16[2048,512]{1,0:T(8,128)(2,1)S(1)}, bf16[2048,512]{1,0:T(8,128)(2,1)S(1)}, u32[]{:S(2)}, u32[]{:S(2)}) collective-permute-start(bf16[2048,512]{1,0:T(8,128)(2,1)S(1)} %get-tuple-element.55.u0), channel_id=1, source_target_pairs={{0,1},{1,0},{2,3},{3,2},{4,5},{5,4},{6,7},{7,6},{8,9},{9,8},{10,11... | collective-permute-start | bytes 6291464 | tf_op jit(solution)/shard_map/ppermute | solution.py:298
  10.4 64.7 %collective-permute-start.9 = (bf16[512,2048]{1,0:T(8,128)(2,1)S(1)}, bf16[512,2048]{1,0:T(8,128)(2,1)S(1)}, u32[]{:S(2)}, u32[]{:S(2)}) collective-permute-start(bf16[512,2048]{1,0:T(8,128)(2,1)S(1)} %get-tuple-element.56.d0), channel_id=1, source_target_pairs={{0,1},{1,0},{2,3},{3,2},{4,5},{5,4},{6,7},{7,6},{8,9},{9,8},{10,11... | collective-permute-start | bytes 6291464 | tf_op jit(solution)/shard_map/ppermute | solution.py:298
  13.1 8.4 %collective-permute-start.3 = (bf16[528,128]{1,0:T(8,128)(2,1)S(1)}, bf16[528,128]{1,0:T(8,128)(2,1)S(1)}, u32[]{:S(2)}, u32[]{:S(2)}) collective-permute-start(bf16[528,128]{1,0:T(8,128)(2,1)S(1)} %total.1), channel_id=1, source_target_pairs={{0,8},{2,10},{4,12},{6,14},{8,0},{10,2},{12,4},{14,6},{1,9},{3,11}... | collective-permute-start | bytes 405512 | tf_op jit(solution)/shard_map/ppermute | solution.py:308
  33.8 6.4 %collective-permute-start.11 = (bf16[64,2048]{1,0:T(8,128)(2,1)S(1)}, bf16[64,2048]{1,0:T(8,128)(2,1)S(1)}, u32[]{:S(2)}, u32[]{:S(2)}) collective-permute-start(bf16[64,2048]{1,0:T(8,128)(2,1)S(1)} %get-tuple-element.57.refs_1_), channel_id=1, source_target_pairs={{0,4},{1,3},{4,8},{5,1},{8,12},{9,5},{12,14},{13,9},{14,10},{15,13... | collective-permute-start | bytes 786440 | tf_op jit(solution)/shard_map/ppermute | solution.py:255
  34.0 8.9 %collective-permute-start.10 = (bf16[64,2048]{1,0:T(8,128)(2,1)S(1)}, bf16[64,2048]{1,0:T(8,128)(2,1)S(1)}, u32[]{:S(2)}, u32[]{:S(2)}) collective-permute-start(bf16[64,2048]{1,0:T(8,128)(2,1)S(1)} %get-tuple-element.53.after_ref.refs_0_), channel_id=1, source_target_pairs={{0,4},{1,3},{4,8},{5,1},{8,12},{9,5},{12,14},{13,9},{14,10},{15,13... | collective-permute-start | bytes 786440 | tf_op jit(solution)/shard_map/ppermute | solution.py:255
  40.2 6.4 %collective-permute-start.14 = (bf16[64,2048]{1,0:T(8,128)(2,1)S(1)}, bf16[64,2048]{1,0:T(8,128)(2,1)S(1)}, u32[]{:S(2)}, u32[]{:S(2)}) collective-permute-start(bf16[64,2048]{1,0:T(8,128)(2,1)S(1)} %collective-permute-done.11.refs_1_), channel_id=1, source_target_pairs={{0,4},{1,3},{4,8},{5,1},{8,12},{9,5},{12,14},{13,9},{14,10},{15,13... | collective-permute-start | bytes 786440 | tf_op jit(solution)/shard_map/ppermute | solution.py:255
  43.0 6.4 %collective-permute-start.13 = (bf16[64,2048]{1,0:T(8,128)(2,1)S(1)}, bf16[64,2048]{1,0:T(8,128)(2,1)S(1)}, u32[]{:S(2)}, u32[]{:S(2)}) collective-permute-start(bf16[64,2048]{1,0:T(8,128)(2,1)S(1)} %collective-permute-done.10.refs_0_), channel_id=1, source_target_pairs={{0,4},{1,3},{4,8},{5,1},{8,12},{9,5},{12,14},{13,9},{14,10},{15,13... | collective-permute-start | bytes 786440 | tf_op jit(solution)/shard_map/ppermute | solution.py:255
  46.6 6.4 %collective-permute-start.17 = (bf16[64,2048]{1,0:T(8,128)(2,1)S(1)}, bf16[64,2048]{1,0:T(8,128)(2,1)S(1)}, u32[]{:S(2)}, u32[]{:S(2)}) collective-permute-start(bf16[64,2048]{1,0:T(8,128)(2,1)S(1)} %collective-permute-done.14.refs_1_), channel_id=1, source_target_pairs={{0,4},{1,3},{4,8},{5,1},{8,12},{9,5},{12,14},{13,9},{14,10},{15,13... | collective-permute-start | bytes 786440 | tf_op jit(solution)/shard_map/ppermute | solution.py:255
  49.4 6.4 %collective-permute-start.16 = (bf16[64,2048]{1,0:T(8,128)(2,1)S(1)}, bf16[64,2048]{1,0:T(8,128)(2,1)S(1)}, u32[]{:S(2)}, u32[]{:S(2)}) collective-permute-start(bf16[64,2048]{1,0:T(8,128)(2,1)S(1)} %collective-permute-done.13.refs_0_), channel_id=1, source_target_pairs={{0,4},{1,3},{4,8},{5,1},{8,12},{9,5},{12,14},{13,9},{14,10},{15,13... | collective-permute-start | bytes 786440 | tf_op jit(solution)/shard_map/ppermute | solution.py:255
  52.9 6.4 %collective-permute-start.20 = (bf16[64,2048]{1,0:T(8,128)(2,1)S(1)}, bf16[64,2048]{1,0:T(8,128)(2,1)S(1)}, u32[]{:S(2)}, u32[]{:S(2)}) collective-permute-start(bf16[64,2048]{1,0:T(8,128)(2,1)S(1)} %collective-permute-done.17.refs_1_), channel_id=1, source_target_pairs={{0,4},{1,3},{4,8},{5,1},{8,12},{9,5},{12,14},{13,9},{14,10},{15,13... | collective-permute-start | bytes 786440 | tf_op jit(solution)/shard_map/ppermute | solution.py:255
  55.7 6.4 %collective-permute-start.19 = (bf16[64,2048]{1,0:T(8,128)(2,1)S(1)}, bf16[64,2048]{1,0:T(8,128)(2,1)S(1)}, u32[]{:S(2)}, u32[]{:S(2)}) collective-permute-start(bf16[64,2048]{1,0:T(8,128)(2,1)S(1)} %collective-permute-done.16.refs_0_), channel_id=1, source_target_pairs={{0,4},{1,3},{4,8},{5,1},{8,12},{9,5},{12,14},{13,9},{14,10},{15,13... | collective-permute-start | bytes 786440 | tf_op jit(solution)/shard_map/ppermute | solution.py:255
  59.3 6.4 %collective-permute-start.23 = (bf16[64,2048]{1,0:T(8,128)(2,1)S(1)}, bf16[64,2048]{1,0:T(8,128)(2,1)S(1)}, u32[]{:S(2)}, u32[]{:S(2)}) collective-permute-start(bf16[64,2048]{1,0:T(8,128)(2,1)S(1)} %collective-permute-done.20.refs_1_), channel_id=1, source_target_pairs={{0,4},{1,3},{4,8},{5,1},{8,12},{9,5},{12,14},{13,9},{14,10},{15,13... | collective-permute-start | bytes 786440 | tf_op jit(solution)/shard_map/ppermute | solution.py:255
  65.7 6.4 %collective-permute-start.26 = (bf16[64,2048]{1,0:T(8,128)(2,1)S(1)}, bf16[64,2048]{1,0:T(8,128)(2,1)S(1)}, u32[]{:S(2)}, u32[]{:S(2)}) collective-permute-start(bf16[64,2048]{1,0:T(8,128)(2,1)S(1)} %collective-permute-done.23.refs_1_), channel_id=1, source_target_pairs={{0,4},{1,3},{4,8},{5,1},{8,12},{9,5},{12,14},{13,9},{14,10},{15,13... | collective-permute-start | bytes 786440 | tf_op jit(solution)/shard_map/ppermute | solution.py:255
  72.0 21.1 %collective-permute-start.29 = (bf16[64,2048]{1,0:T(8,128)(2,1)S(1)}, bf16[64,2048]{1,0:T(8,128)(2,1)S(1)}, u32[]{:S(2)}, u32[]{:S(2)}) collective-permute-start(bf16[64,2048]{1,0:T(8,128)(2,1)S(1)} %collective-permute-done.26.refs_1_), channel_id=1, source_target_pairs={{0,4},{1,3},{4,8},{5,1},{8,12},{9,5},{12,14},{13,9},{14,10},{15,13... | collective-permute-start | bytes 786440 | tf_op jit(solution)/shard_map/ppermute | solution.py:255
  74.9 18.3 %collective-permute-start.28 = (bf16[64,2048]{1,0:T(8,128)(2,1)S(1)}, bf16[64,2048]{1,0:T(8,128)(2,1)S(1)}, u32[]{:S(2)}, u32[]{:S(2)}) collective-permute-start(bf16[64,2048]{1,0:T(8,128)(2,1)S(1)} %collective-permute-done.25.refs_0_), channel_id=1, source_target_pairs={{0,4},{1,3},{4,8},{5,1},{8,12},{9,5},{12,14},{13,9},{14,10},{15,13... | collective-permute-start | bytes 786440 | tf_op jit(solution)/shard_map/ppermute | solution.py:255
  77.1 18.3 %collective-permute-start.12 = (bf16[64,2048]{1,0:T(8,128)(2,1)S(1)}, bf16[64,2048]{1,0:T(8,128)(2,1)S(1)}, u32[]{:S(2)}, u32[]{:S(2)}) collective-permute-start(bf16[64,2048]{1,0:T(8,128)(2,1)S(1)} %get-tuple-element.58), channel_id=1, source_target_pairs={{0,4},{1,3},{4,8},{5,1},{8,12},{9,5},{12,14},{13,9},{14,10},{15,13... | collective-permute-start | bytes 786440 | tf_op jit(solution)/shard_map/ppermute | solution.py:255
  79.3 18.0 %collective-permute-start.31 = (bf16[64,2048]{1,0:T(8,128)(2,1)S(1)}, bf16[64,2048]{1,0:T(8,128)(2,1)S(1)}, u32[]{:S(2)}, u32[]{:S(2)}) collective-permute-start(bf16[64,2048]{1,0:T(8,128)(2,1)S(1)} %get-tuple-element.66), channel_id=1, source_target_pairs={{0,4},{1,3},{4,8},{5,1},{8,12},{9,5},{12,14},{13,9},{14,10},{15,13... | collective-permute-start | bytes 786440 | tf_op jit(solution)/shard_map/ppermute | solution.py:255
  95.5 6.4 %collective-permute-start.15 = (bf16[64,2048]{1,0:T(8,128)(2,1)S(1)}, bf16[64,2048]{1,0:T(8,128)(2,1)S(1)}, u32[]{:S(2)}, u32[]{:S(2)}) collective-permute-start(bf16[64,2048]{1,0:T(8,128)(2,1)S(1)} %add_convert_fusion.13), channel_id=1, source_target_pairs={{0,4},{1,3},{4,8},{5,1},{8,12},{9,5},{12,14},{13,9},{14,10},{15,13... | collective-permute-start | bytes 786440 | tf_op jit(solution)/shard_map/ppermute | solution.py:255
  97.4 7.3 %collective-permute-start.32 = (bf16[64,2048]{1,0:T(8,128)(2,1)S(1)}, bf16[64,2048]{1,0:T(8,128)(2,1)S(1)}, u32[]{:S(2)}, u32[]{:S(2)}) collective-permute-start(bf16[64,2048]{1,0:T(8,128)(2,1)S(1)} %add_convert_fusion.6), channel_id=1, source_target_pairs={{0,4},{1,3},{4,8},{5,1},{8,12},{9,5},{12,14},{13,9},{14,10},{15,13... | collective-permute-start | bytes 786440 | tf_op jit(solution)/shard_map/ppermute | solution.py:255
  102.0 6.4 %collective-permute-start.18 = (bf16[64,2048]{1,0:T(8,128)(2,1)S(1)}, bf16[64,2048]{1,0:T(8,128)(2,1)S(1)}, u32[]{:S(2)}, u32[]{:S(2)}) collective-permute-start(bf16[64,2048]{1,0:T(8,128)(2,1)S(1)} %add_convert_fusion.12), channel_id=1, source_target_pairs={{0,4},{1,3},{4,8},{5,1},{8,12},{9,5},{12,14},{13,9},{14,10},{15,13... | collective-permute-start | bytes 786440 | tf_op jit(solution)/shard_map/ppermute | solution.py:255
  104.8 6.4 %collective-permute-start.33 = (bf16[64,2048]{1,0:T(8,128)(2,1)S(1)}, bf16[64,2048]{1,0:T(8,128)(2,1)S(1)}, u32[]{:S(2)}, u32[]{:S(2)}) collective-permute-start(bf16[64,2048]{1,0:T(8,128)(2,1)S(1)} %add_convert_fusion.5), channel_id=1, source_target_pairs={{0,4},{1,3},{4,8},{5,1},{8,12},{9,5},{12,14},{13,9},{14,10},{15,13... | collective-permute-start | bytes 786440 | tf_op jit(solution)/shard_map/ppermute | solution.py:255
  108.4 6.4 %collective-permute-start.21 = (bf16[64,2048]{1,0:T(8,128)(2,1)S(1)}, bf16[64,2048]{1,0:T(8,128)(2,1)S(1)}, u32[]{:S(2)}, u32[]{:S(2)}) collective-permute-start(bf16[64,2048]{1,0:T(8,128)(2,1)S(1)} %add_convert_fusion.11), channel_id=1, source_target_pairs={{0,4},{1,3},{4,8},{5,1},{8,12},{9,5},{12,14},{13,9},{14,10},{15,13... | collective-permute-start | bytes 786440 | tf_op jit(solution)/shard_map/ppermute | solution.py:255
  111.3 6.4 %collective-permute-start.34 = (bf16[64,2048]{1,0:T(8,128)(2,1)S(1)}, bf16[64,2048]{1,0:T(8,128)(2,1)S(1)}, u32[]{:S(2)}, u32[]{:S(2)}) collective-permute-start(bf16[64,2048]{1,0:T(8,128)(2,1)S(1)} %add_convert_fusion.4), channel_id=1, source_target_pairs={{0,4},{1,3},{4,8},{5,1},{8,12},{9,5},{12,14},{13,9},{14,10},{15,13... | collective-permute-start | bytes 786440 | tf_op jit(solution)/shard_map/ppermute | solution.py:255
  114.9 6.4 %collective-permute-start.24 = (bf16[64,2048]{1,0:T(8,128)(2,1)S(1)}, bf16[64,2048]{1,0:T(8,128)(2,1)S(1)}, u32[]{:S(2)}, u32[]{:S(2)}) collective-permute-start(bf16[64,2048]{1,0:T(8,128)(2,1)S(1)} %add_convert_fusion.10), channel_id=1, source_target_pairs={{0,4},{1,3},{4,8},{5,1},{8,12},{9,5},{12,14},{13,9},{14,10},{15,13... | collective-permute-start | bytes 786440 | tf_op jit(solution)/shard_map/ppermute | solution.py:255
  117.8 6.4 %collective-permute-start.35 = (bf16[64,2048]{1,0:T(8,128)(2,1)S(1)}, bf16[64,2048]{1,0:T(8,128)(2,1)S(1)}, u32[]{:S(2)}, u32[]{:S(2)}) collective-permute-start(bf16[64,2048]{1,0:T(8,128)(2,1)S(1)} %add_convert_fusion.3), channel_id=1, source_target_pairs={{0,4},{1,3},{4,8},{5,1},{8,12},{9,5},{12,14},{13,9},{14,10},{15,13... | collective-permute-start | bytes 786440 | tf_op jit(solution)/shard_map/ppermute | solution.py:255
  121.4 6.4 %collective-permute-start.27 = (bf16[64,2048]{1,0:T(8,128)(2,1)S(1)}, bf16[64,2048]{1,0:T(8,128)(2,1)S(1)}, u32[]{:S(2)}, u32[]{:S(2)}) collective-permute-start(bf16[64,2048]{1,0:T(8,128)(2,1)S(1)} %add_convert_fusion.9), channel_id=1, source_target_pairs={{0,4},{1,3},{4,8},{5,1},{8,12},{9,5},{12,14},{13,9},{14,10},{15,13... | collective-permute-start | bytes 786440 | tf_op jit(solution)/shard_map/ppermute | solution.py:255
  124.2 6.4 %collective-permute-start.36 = (bf16[64,2048]{1,0:T(8,128)(2,1)S(1)}, bf16[64,2048]{1,0:T(8,128)(2,1)S(1)}, u32[]{:S(2)}, u32[]{:S(2)}) collective-permute-start(bf16[64,2048]{1,0:T(8,128)(2,1)S(1)} %add_convert_fusion.2), channel_id=1, source_target_pairs={{0,4},{1,3},{4,8},{5,1},{8,12},{9,5},{12,14},{13,9},{14,10},{15,13... | collective-permute-start | bytes 786440 | tf_op jit(solution)/shard_map/ppermute | solution.py:255
  127.9 6.4 %collective-permute-start.30 = (bf16[64,2048]{1,0:T(8,128)(2,1)S(1)}, bf16[64,2048]{1,0:T(8,128)(2,1)S(1)}, u32[]{:S(2)}, u32[]{:S(2)}) collective-permute-start(bf16[64,2048]{1,0:T(8,128)(2,1)S(1)} %add_convert_fusion.8), channel_id=1, source_target_pairs={{0,4},{1,3},{4,8},{5,1},{8,12},{9,5},{12,14},{13,9},{14,10},{15,13... | collective-permute-start | bytes 786440 | tf_op jit(solution)/shard_map/ppermute | solution.py:255
  130.7 6.4 %collective-permute-start.37 = (bf16[64,2048]{1,0:T(8,128)(2,1)S(1)}, bf16[64,2048]{1,0:T(8,128)(2,1)S(1)}, u32[]{:S(2)}, u32[]{:S(2)}) collective-permute-start(bf16[64,2048]{1,0:T(8,128)(2,1)S(1)} %add_convert_fusion.1), channel_id=1, source_target_pairs={{0,4},{1,3},{4,8},{5,1},{8,12},{9,5},{12,14},{13,9},{14,10},{15,13... | collective-permute-start | bytes 786440 | tf_op jit(solution)/shard_map/ppermute | solution.py:255
  (6 other events, 35.5 us)
